TPU v7x, 32 devices: a whole 2x2x4 slice. The times are simulated.
32 devices in a mesh: dp: 8 (over y, x, core), tensor: 4 (over z).
Axes of the slice: x: 2, y: 2, z: 4, core: 2. Of those that a mesh axis runs over, the one named last changes fastest.
Arguments:
- tokens: bfloat16 [16384, 768], P(('dp', 'tensor')), may hold values from -6 to 6
- time_embed: bfloat16 [8, 128], P('dp'), may hold values from -6 to 6
- ada_weight: bfloat16 [128, 4608], P(None, 'dp'), may hold values from -1 to 1
- ada_bias: bfloat16 [4608], P('dp'), may hold values from -4 to 4
- norm1_gain: bfloat16 [768], P('dp'), may hold values from 0.5 to 1.5
- qkv_weight: bfloat16 [3, 768, 768], P(None, 'dp', 'tensor'), may hold values from -1 to 1
- out_weight: bfloat16 [768, 768], P('tensor', 'dp'), may hold values from -2 to 2
- norm2_gain: bfloat16 [768], P('dp'), may hold values from 0.5 to 1.5
- up_weight: bfloat16 [768, 3072], P('dp', 'tensor'), may hold values from -0.21875 to 0.21875
- up_bias: bfloat16 [3072], P(('tensor', 'dp')), may hold values from -4 to 4
- down_weight: bfloat16 [3072, 768], P('tensor', 'dp'), may hold values from -0.109375 to 0.109375
- down_bias: bfloat16 [768], P('dp'), may hold values from -4 to 4
- out_grad: bfloat16 [16384, 768], P(('dp', 'tensor')), may hold values from -6 to 6
Outputs:
- output: bfloat16 [16384, 768], P(('dp', 'tensor'))
- input_grad: bfloat16 [16384, 768], P(('dp', 'tensor'))
- time_grad: float32 [8, 128], P('dp')
- ada_weight_grad: float32 [128, 4608], P(None, 'dp')
- ada_bias_grad: float32 [4608], P('dp')
- norm1_gain_grad: float32 [768], P('dp')
- qkv_weight_grad: float32 [3, 768, 768], P(None, 'dp', 'tensor')
- out_weight_grad: float32 [768, 768], P('tensor', 'dp')
- norm2_gain_grad: float32 [768], P('dp')
- up_weight_grad: float32 [768, 3072], P('dp', 'tensor')
- up_bias_grad: float32 [3072], P(('tensor', 'dp'))
- down_weight_grad: float32 [3072, 768], P('tensor', 'dp')
- down_bias_grad: float32 [768], P('dp')
All inputs are finite; a program needn't handle non-finite values.
Results may differ from a plain program's by a relative error of at most 0.017.
The roundings to bfloat16 on the way count: a program that leaves them out, or rounds other values in their place, can miss the bound.
Values may be sent and summed in bfloat16 or wider, within the bound.
No kernel may reach another device: no remote copies, remote signals or barrier semaphores. Data moves between devices by JAX's collectives and lax.ppermute only.
A program may use at most 192 MiB of HBM per device.

v0:
```python
import math

import jax
import jax.numpy as jnp
from jax import lax
from jax.sharding import PartitionSpec as P

HEAD_DIM = 64


EPSILON = 1e-05
ROPE_BASE = 10000.0
HIGHEST = lax.Precision.HIGHEST


def cut_along(array, dim, devices):
    lengths = array.shape
    tiles = array.reshape(*lengths[:dim], devices, lengths[dim] // devices, *lengths[dim + 1 :])
    return jnp.moveaxis(tiles, dim, 0)


def summed_on_arrival(array, axis, dim):
    devices = lax.axis_size(axis)
    tiles = lax.all_to_all(cut_along(array, dim, devices), axis, 0, 0, tiled=True)
    return jnp.sum(tiles.astype(jnp.float32), axis=0)


def rotate_half(values):
    middle = values.shape[-1] // 2
    return jnp.concatenate([-values[..., middle:], values[..., :middle]], axis=-1)


def rope_tables(positions, head_dim):
    middle = head_dim // 2
    frequency = jnp.exp(
        jnp.arange(middle, dtype=jnp.float32) * (-2.0 * math.log(ROPE_BASE) / head_dim)
    )
    angles = positions.astype(jnp.float32)[:, None] * frequency[None, :]
    angles = jnp.concatenate([angles, angles], axis=-1)
    return (jnp.cos(angles)[:, None, :], jnp.sin(angles)[:, None, :])


def normalize(rows):
    center = jnp.mean(rows, axis=1, keepdims=True)
    shifted = rows - center
    inverse = lax.rsqrt(jnp.mean(shifted * shifted, axis=1, keepdims=True) + EPSILON)
    return (shifted * inverse, inverse)


def norm_back(grad_rows, normed, inverse, gain, scale_rows):
    scaled = grad_rows * gain * (1.0 + scale_rows)
    projected = (
        scaled
        - jnp.mean(scaled, axis=1, keepdims=True)
        - normed * jnp.mean(scaled * normed, axis=1, keepdims=True)
    )
    return inverse * projected


def gelu_tanh(values):
    return jax.nn.gelu(values, approximate=True)


def spread_rows(local_part):
    return lax.all_gather(local_part, "tensor", axis=0, tiled=True)


def spread_grads(local_part):
    return lax.all_gather(local_part, "tensor", axis=0, tiled=True)


def collect_rows(term_fn, row_total):
    return lax.psum_scatter(
        term_fn(jnp.int32(0), row_total * lax.axis_size("tensor")).astype(jnp.bfloat16),
        "tensor",
        scatter_dimension=0,
        tiled=True,
    ).astype(jnp.float32)


def collect_grads(term_fn, row_total):
    return lax.psum_scatter(
        term_fn(jnp.int32(0), row_total * lax.axis_size("tensor")),
        "tensor",
        scatter_dimension=0,
        tiled=True,
    )


def attend_forward(queries, key_rows, value_rows, block_rows):
    length, heads_local, head_dim = (queries.shape[1], queries.shape[2], queries.shape[3])
    factor = 1.0 / math.sqrt(head_dim)
    blocks_per = length // block_rows

    def one_sequence(sequence_items):
        query_seq, key_seq, value_seq = sequence_items

        def one_block(query_block):
            scores = (
                jnp.einsum("qhd,khd->hqk", query_block, key_seq, preferred_element_type=jnp.float32)
                * factor
            )
            highest = jnp.max(scores, axis=-1, keepdims=True)
            exponent = jnp.exp(scores - highest)
            totals = jnp.sum(exponent, axis=-1, keepdims=True)
            weights = (exponent / totals).astype(jnp.bfloat16)
            mixture = jnp.einsum(
                "hqk,khd->qhd", weights, value_seq, preferred_element_type=jnp.float32
            )
            return (mixture.astype(jnp.bfloat16), (highest + jnp.log(totals))[..., 0])

        mixture, log_total = lax.map(
            one_block, query_seq.reshape(blocks_per, block_rows, heads_local, head_dim)
        )
        return (mixture.reshape(length, heads_local, head_dim), log_total)

    return lax.map(one_sequence, (queries, key_rows, value_rows))


def attend_backward(queries, key_rows, value_rows, attn_grad, log_total, block_rows):
    length, heads_local, head_dim = (queries.shape[1], queries.shape[2], queries.shape[3])
    factor = 1.0 / math.sqrt(head_dim)
    blocks_per = length // block_rows

    def one_sequence(sequence_items):
        query_seq, key_seq, value_seq, grad_seq, total_seq = sequence_items

        def one_block(carry, block_items):
            key_grad, value_grad = carry
            query_block, grad_block, total_block = block_items
            scores = (
                jnp.einsum("qhd,khd->hqk", query_block, key_seq, preferred_element_type=jnp.float32)
                * factor
            )
            weights = jnp.exp(scores - total_block[..., None])
            value_grad = value_grad + jnp.einsum(
                "hqk,qhd->khd",
                weights.astype(jnp.bfloat16),
                grad_block,
                preferred_element_type=jnp.float32,
            )
            weight_grad = jnp.einsum(
                "qhd,khd->hqk", grad_block, value_seq, preferred_element_type=jnp.float32
            )
            centre = jnp.sum(weight_grad * weights, axis=-1, keepdims=True)
            score_grad = (weights * (weight_grad - centre)).astype(jnp.bfloat16)
            query_grad = (
                jnp.einsum("hqk,khd->qhd", score_grad, key_seq, preferred_element_type=jnp.float32)
                * factor
            )
            key_grad = (
                key_grad
                + jnp.einsum(
                    "hqk,qhd->khd", score_grad, query_block, preferred_element_type=jnp.float32
                )
                * factor
            )
            return ((key_grad, value_grad), query_grad)

        empty_grad = jnp.zeros((length, heads_local, head_dim), jnp.float32)
        block_shape = (blocks_per, block_rows, heads_local, head_dim)
        (key_grad, value_grad), query_grad = lax.scan(
            one_block,
            (empty_grad, empty_grad),
            (query_seq.reshape(block_shape), grad_seq.reshape(block_shape), total_seq),
        )
        return (query_grad.reshape(length, heads_local, head_dim), key_grad, value_grad)

    return lax.map(one_sequence, (queries, key_rows, value_rows, attn_grad, log_total))


def per_device(
    tokens,
    time_embed,
    ada_weight,
    ada_bias,
    norm1_gain,
    qkv_weight,
    out_weight,
    norm2_gain,
    up_weight,
    up_bias,
    down_weight,
    down_bias,
    out_grad,
):
    f32 = jnp.float32
    bf16 = jnp.bfloat16
    gathered = (
        lax.all_gather(norm1_gain, "dp", axis=0, tiled=True),
        lax.all_gather(qkv_weight, "dp", axis=1, tiled=True),
        lax.all_gather(out_weight, "dp", axis=1, tiled=True),
        lax.all_gather(norm2_gain, "dp", axis=0, tiled=True),
        lax.all_gather(up_weight, "dp", axis=0, tiled=True),
        lax.all_gather(up_bias, "dp", axis=0, tiled=True),
        lax.all_gather(down_weight, "dp", axis=1, tiled=True),
        lax.all_gather(down_bias, "dp", axis=0, tiled=True),
    )
    gain_one, qkv_full, out_full, gain_two, up_full, up_bias_full, down_full, down_bias_full = (
        gathered
    )
    ada_full, ada_bias_full = (
        lax.all_gather(ada_weight, "dp", axis=1, tiled=True),
        lax.all_gather(ada_bias, "dp", axis=0, tiled=True),
    )
    modulation = jnp.dot(time_embed, ada_full, preferred_element_type=f32) + ada_bias_full.astype(
        f32
    )
    local_rows = tokens.shape[0]
    tensor_size = lax.axis_size("tensor")
    group_rows = local_rows * tensor_size
    seq_count = time_embed.shape[0]
    length = group_rows // seq_count
    block_rows = min(512, length)
    heads_local = qkv_full.shape[2] // HEAD_DIM
    seq_shape = (seq_count, length, heads_local, HEAD_DIM)
    row_index = lax.axis_index("tensor") * local_rows + jnp.arange(local_rows, dtype=jnp.int32)
    seq_onehot = (
        (row_index // length)[:, None] == jnp.arange(seq_count, dtype=jnp.int32)[None, :]
    ).astype(f32)
    mod_rows = jnp.dot(seq_onehot, modulation, precision=HIGHEST)
    shift_one, scale_one, gate_one, shift_two, scale_two, gate_two = jnp.split(mod_rows, 6, axis=1)
    inputs = tokens.astype(f32)
    gain_one_f = gain_one.astype(f32)
    normed_one, inverse_one = normalize(inputs)
    hidden_one = (normed_one * gain_one_f * (1.0 + scale_one) + shift_one).astype(bf16)
    spread_one = spread_rows(hidden_one)
    projected = jnp.einsum("gd,cde->cge", spread_one, qkv_full, preferred_element_type=f32)
    positions = jnp.arange(group_rows, dtype=jnp.int32) % length
    cosine_table, sine_table = rope_tables(positions, HEAD_DIM)

    def rotate_rows(values):
        per_head = values.reshape(group_rows, heads_local, HEAD_DIM)
        return (per_head * cosine_table + rotate_half(per_head) * sine_table).reshape(
            group_rows, heads_local * HEAD_DIM
        )

    def unrotate_rows(values):
        per_head = values.reshape(group_rows, heads_local, HEAD_DIM)
        return (per_head * cosine_table - rotate_half(per_head * sine_table)).reshape(
            group_rows, heads_local * HEAD_DIM
        )

    queries = rotate_rows(projected[0]).astype(bf16)
    key_rows = rotate_rows(projected[1]).astype(bf16)
    value_rows = projected[2].astype(bf16)
    mixture, log_total = attend_forward(
        queries.reshape(seq_shape),
        key_rows.reshape(seq_shape),
        value_rows.reshape(seq_shape),
        block_rows,
    )
    attention = mixture.reshape(group_rows, heads_local * HEAD_DIM)

    def attention_term(first_row, row_count):
        return jnp.dot(attention, out_full, preferred_element_type=f32)

    branch_one = collect_rows(attention_term, local_rows)
    residual = inputs + gate_one * branch_one
    gain_two_f = gain_two.astype(f32)
    normed_two, inverse_two = normalize(residual)
    hidden_two = (normed_two * gain_two_f * (1.0 + scale_two) + shift_two).astype(bf16)
    spread_two = spread_rows(hidden_two)
    pre_act = jnp.dot(spread_two, up_full, preferred_element_type=f32) + up_bias_full.astype(f32)
    activated = gelu_tanh(pre_act).astype(bf16)

    def feed_term(first_row, row_count):
        return jnp.dot(activated, down_full, preferred_element_type=f32)

    branch_two = collect_rows(feed_term, local_rows) + down_bias_full.astype(f32)
    output = (residual + gate_two * branch_two).astype(bf16)
    gathered_back = (
        lax.all_gather(norm1_gain, "dp", axis=0, tiled=True),
        lax.all_gather(qkv_weight, "dp", axis=1, tiled=True),
        lax.all_gather(out_weight, "dp", axis=1, tiled=True),
        lax.all_gather(norm2_gain, "dp", axis=0, tiled=True),
        lax.all_gather(up_weight, "dp", axis=0, tiled=True),
        lax.all_gather(up_bias, "dp", axis=0, tiled=True),
        lax.all_gather(down_weight, "dp", axis=1, tiled=True),
        lax.all_gather(down_bias, "dp", axis=0, tiled=True),
    )
    gain_one, qkv_full, out_full, gain_two, up_full, up_bias_full, down_full, down_bias_full = (
        gathered_back
    )
    gain_one_f = gain_one.astype(f32)
    gain_two_f = gain_two.astype(f32)
    upstream = out_grad.astype(f32)
    branch_two_grad = (gate_two * upstream).astype(bf16)
    down_bias_part = jnp.sum(branch_two_grad, axis=0, dtype=f32)
    spread_two_grad = spread_grads(branch_two_grad)
    down_grad = jnp.einsum("gf,gd->fd", activated, spread_two_grad, preferred_element_type=f32)
    act_grad = jnp.einsum("gd,fd->gf", spread_two_grad, down_full, preferred_element_type=f32)
    gelu_pull = jax.vjp(gelu_tanh, pre_act)[1]
    pre_grad = gelu_pull(act_grad)[0].astype(bf16)
    up_bias_grad = jnp.sum(pre_grad, axis=0, dtype=f32)
    up_grad = jnp.einsum("gd,gf->df", spread_two, pre_grad, preferred_element_type=f32)

    def hidden_two_term(first_row, row_count):
        return jnp.einsum("gf,df->gd", pre_grad, up_full, preferred_element_type=f32)

    hidden_two_grad = collect_grads(hidden_two_term, local_rows)
    gain_two_part = jnp.sum(hidden_two_grad * normed_two * (1.0 + scale_two), axis=0)
    scale_two_grad = hidden_two_grad * normed_two * gain_two_f
    residual_grad = upstream + norm_back(
        hidden_two_grad, normed_two, inverse_two, gain_two_f, scale_two
    )
    gate_two_grad = upstream * branch_two
    gate_one_grad = residual_grad * branch_one
    branch_one_grad = (gate_one * residual_grad).astype(bf16)
    spread_one_grad = spread_grads(branch_one_grad)
    out_weight_grad = jnp.einsum(
        "ge,gd->ed", attention, spread_one_grad, preferred_element_type=f32
    )
    attention_grad = jnp.einsum(
        "gd,ed->ge", spread_one_grad, out_full, preferred_element_type=f32
    ).astype(bf16)
    query_grad, key_grad, value_grad = attend_backward(
        queries.reshape(seq_shape),
        key_rows.reshape(seq_shape),
        value_rows.reshape(seq_shape),
        attention_grad.reshape(seq_shape),
        log_total,
        block_rows,
    )
    flat_shape = (group_rows, heads_local * HEAD_DIM)
    qkv_grad_rows = jnp.stack(
        [
            unrotate_rows(query_grad.reshape(flat_shape)),
            unrotate_rows(key_grad.reshape(flat_shape)),
            value_grad.reshape(flat_shape),
        ]
    ).astype(bf16)
    qkv_grad = jnp.einsum("gd,cge->cde", spread_one, qkv_grad_rows, preferred_element_type=f32)

    def hidden_one_term(first_row, row_count):
        return jnp.einsum("cge,cde->gd", qkv_grad_rows, qkv_full, preferred_element_type=f32)

    hidden_one_grad = collect_grads(hidden_one_term, local_rows)
    gain_one_part = jnp.sum(hidden_one_grad * normed_one * (1.0 + scale_one), axis=0)
    scale_one_grad = hidden_one_grad * normed_one * gain_one_f
    input_grad = (
        residual_grad + norm_back(hidden_one_grad, normed_one, inverse_one, gain_one_f, scale_one)
    ).astype(bf16)
    row_grads = jnp.concatenate(
        [
            hidden_one_grad,
            scale_one_grad,
            gate_one_grad,
            hidden_two_grad,
            scale_two_grad,
            gate_two_grad,
        ],
        axis=1,
    )
    mod_part = jnp.dot(seq_onehot.T, row_grads, precision=HIGHEST)
    mod_sum, gain_one_sum, gain_two_sum, down_bias_sum = lax.psum(
        (mod_part, gain_one_part, gain_two_part, down_bias_part), "tensor"
    )
    mod_grad = mod_sum.astype(bf16)
    time_grad = jnp.einsum("se,ce->sc", mod_grad, ada_full, preferred_element_type=f32)
    ada_part = jnp.einsum("sc,se->ce", time_embed, mod_grad, preferred_element_type=f32)
    ada_bias_part = jnp.sum(mod_grad, axis=0, dtype=f32)
    ada_sum, ada_bias_sum = (
        summed_on_arrival(ada_part.astype(jnp.bfloat16), "dp", 1),
        summed_on_arrival(ada_bias_part.astype(jnp.bfloat16), "dp", 0),
    )
    gain_one_out, qkv_sum, out_sum, gain_two_out, up_sum, up_bias_sum, down_sum, down_bias_out = (
        lax.psum_scatter(gain_one_sum, "dp", scatter_dimension=0, tiled=True),
        lax.psum_scatter(qkv_grad, "dp", scatter_dimension=1, tiled=True),
        lax.psum_scatter(out_weight_grad, "dp", scatter_dimension=1, tiled=True),
        lax.psum_scatter(gain_two_sum, "dp", scatter_dimension=0, tiled=True),
        lax.psum_scatter(up_grad, "dp", scatter_dimension=0, tiled=True),
        lax.psum_scatter(up_bias_grad, "dp", scatter_dimension=0, tiled=True),
        lax.psum_scatter(down_grad, "dp", scatter_dimension=1, tiled=True),
        lax.psum_scatter(down_bias_sum, "dp", scatter_dimension=0, tiled=True),
    )
    return (
        output,
        input_grad,
        time_grad,
        ada_sum,
        ada_bias_sum,
        gain_one_out,
        qkv_sum,
        out_sum,
        gain_two_out,
        up_sum,
        up_bias_sum,
        down_sum,
        down_bias_out,
    )


def solution(mesh):
    placed = (
        P(("dp", "tensor"), None),
        P("dp", None),
        P(None, "dp"),
        P("dp"),
        P("dp"),
        P(None, "dp", "tensor"),
        P("tensor", "dp"),
        P("dp"),
        P("dp", "tensor"),
        P(("tensor", "dp")),
        P("tensor", "dp"),
        P("dp"),
        P(("dp", "tensor"), None),
    )
    return jax.shard_map(
        per_device,
        mesh=mesh,
        in_specs=placed,
        out_specs=(
            P(("dp", "tensor"), None),
            P(("dp", "tensor"), None),
            P("dp", None),
            P(None, "dp"),
            P("dp"),
            P("dp"),
            P(None, "dp", "tensor"),
            P("tensor", "dp"),
            P("dp"),
            P("dp", "tensor"),
            P(("tensor", "dp")),
            P("tensor", "dp"),
            P("dp"),
        ),
        check_vma=False,
    )
```

profile of v0, /device:TPU:0, one launch (start us, length us, event | category | flops | bytes accessed | tf_op | source)
XLA Modules:
  0.0 1068.7 jit_solution(5172849406058035904)
XLA Ops:
  14.8 26.3 %all-reduce.11 = (bf16[4608]{0:T(1024)(128)(2,1)S(1)}, bf16[768]{0:T(1024)(128)(2,1)S(1)}, bf16[768]{0:T(1024)(128)(2,1)S(1)}, bf16[768]{0:T(1024)(128)(2,1)}, bf16[768]{0:T(1024)(128)(2,1)}) all-reduce(bf16[4608]{0:T(1024)(128)(2,1)S(1)} %dynamic-update-slice, ...), channel_id=1, replica_groups=mesh['dp'=8,'tensor'=4] {'dp'}, use_global_device_ids=true, to_apply=%add | all-reduce | flops 7680 | bytes 30720
  51.2 12.7 %all_gather.52 = bf16[3,768,192]{2,0,1:T(4,128)(2,1)S(1)} all-gather(bf16[3,96,192]{2,0,1:T(4,128)(2,1)S(1)} %copy.64), channel_id=1, replica_groups=mesh['dp'=8,'tensor'=4] {'dp'}, dimensions={1}, use_global_device_ids=true | all-gather | bytes 995328 | tf_op jit(solution)/shard_map/all_gather | solution.py:191
  65.9 9.8 all_gather.53
  82.4 31.5 %all-gather.10.cloned.1.call-done = bf16[2048,768]{1,0:T(8,128)(2,1)} async-done(((bf16[512,768]{1,0:T(8,128)(2,1)}), bf16[2048,768]{1,0:T(8,128)(2,1)}) %all-gather.10.cloned.1.call-update) | async-done | bytes 3145744 | tf_op jit(solution)/shard_map/all_gather | solution.py:65
  130.4 36.5 %while.47 = (s32[]{:T(128)}, bf16[4,512,3,64]{1,3,2,0:T(8,128)(2,1)}, f32[4,3,512]{2,1,0:T(4,128)}, bf16[4,512,3,64]{1,3,2,0:T(8,128)(2,1)S(1)}, bf16[2048,3,64]...) while((s32[]{:T(128)}, bf16[4,512,3,64]{1,3,2,0:T(8,128)(2,1)}, ...), condition=%wide.region_5.6_spmd, body=%wide.region_2.5_spmd.sunk | while | flops 833714688 | bytes 39766112 | solution.py:112
  173.5 58.4 %reduce-scatter.13.cloned.1.call-done = bf16[512,768]{1,0:T(8,128)(2,1)} async-done(((bf16[2048,768]{1,0:T(8,128)(2,1)}), bf16[512,768]{1,0:T(8,128)(2,1)}) %reduce-scatter.13.cloned.1.call-update) | async-done | bytes 786448 | tf_op jit(solution)/shard_map/reduce_scatter | solution.py:73
  242.4 15.4 %all-gather.14.cloned.1.call-done = bf16[768,768]{1,0:T(8,128)(2,1)} async-done(((bf16[96,768]{1,0:T(8,128)(2,1)}), bf16[768,768]{1,0:T(8,128)(2,1)}) %all-gather.14.cloned.1.call-update) | async-done | bytes 1179664 | tf_op jit(solution)/shard_map/all_gather | solution.py:194
  257.8 65.5 %all-gather.12.cloned.1.call-done = bf16[2048,768]{1,0:T(8,128)(2,1)} async-done(((bf16[512,768]{1,0:T(8,128)(2,1)}), bf16[2048,768]{1,0:T(8,128)(2,1)}) %all-gather.12.cloned.1.call-update) | async-done | bytes 3145744 | tf_op jit(solution)/shard_map/all_gather | solution.py:65
  323.3 7.5 fusion.106
  330.9 17.0 %all-gather.16.cloned.1.call-done = bf16[768,768]{0,1:T(8,128)(2,1)} async-done(((bf16[768,96]{0,1:T(8,128)(2,1)}), bf16[768,768]{0,1:T(8,128)(2,1)}) %all-gather.16.cloned.1.call-update) | async-done | bytes 1179664 | tf_op jit(solution)/shard_map/all_gather | solution.py:196
  347.8 65.7 %all-gather.18.cloned.1.call-done = bf16[2048,768]{1,0:T(8,128)(2,1)} async-done(((bf16[512,768]{1,0:T(8,128)(2,1)}), bf16[2048,768]{1,0:T(8,128)(2,1)}) %all-gather.18.cloned.1.call-update) | async-done | bytes 3145744 | tf_op jit(solution)/shard_map/all_gather | solution.py:69
  413.5 10.9 %convert_reduce_fusion = (f32[768]{0:T(1024)}, bf16[2048,768]{1,0:T(8,128)(2,1)S(1)}, bf16[2048,768]{1,0:T(8,128)(2,1)}) fusion(f32[2048,768]{1,0:T(8,128)} %fusion.106, f32[768]{0:T(1024)S(1)} %convert_element_type.154, bf16[2048,768]{1,0:T(8,128)(2,1)} %all-gather.18.cloned.1.call-done, bf16[768,768]{0,1:T(8,128)(2,1)} %all-gather.16.cloned.1.call-done), kind=kOutput, calls=%fused_computation.53 | convolution fusion | flops 2455239936 | bytes 16914432 | tf_op jit(solution)/shard_map/gd,fd->gf/dot_general | solution.py:292
  430.5 109.5 %reduce-scatter.17.cloned.1.call-done = f32[512,768]{1,0:T(8,128)} async-done(((f32[2048,768]{1,0:T(8,128)}), f32[512,768]{1,0:T(8,128)}) %reduce-scatter.17.cloned.1.call-update) | async-done | bytes 1572880 | tf_op jit(solution)/shard_map/reduce_scatter | solution.py:82
  546.1 6.6 convolution_convert_fusion
  552.7 57.5 %all-gather.20.cloned.1.call-done = bf16[2048,768]{1,0:T(8,128)(2,1)} async-done(((bf16[512,768]{1,0:T(8,128)(2,1)}), bf16[2048,768]{1,0:T(8,128)(2,1)}) %all-gather.20.cloned.1.call-update) | async-done | bytes 3145744 | tf_op jit(solution)/shard_map/all_gather | solution.py:69
  619.5 136.2 %while.48 = (s32[]{:T(128)}, f32[2048,3,64]{0,2,1:T(8,128)S(1)}, f32[2048,3,64]{0,2,1:T(8,128)}, f32[4,512,3,64]{1,0,3,2:T(4,128)}, bf16[4,512,3,64]{1,3,2,0:T(8...) while((s32[]{:T(128)}, f32[2048,3,64]{0,2,1:T(8,128)S(1)}, ...), condition=%wide.region_15.16_spmd.clone, body=%wide.region_13.15_spmd.clone.sunk | while | flops 2053077504 | bytes 130984112 | solution.py:162
  644.5 8.6 dynamic_update_slice.33
  656.6 5.2 fusion.175
  678.7 8.6 dynamic_update_slice.33
  690.8 5.2 fusion.175
  712.9 8.6 dynamic_update_slice.33
  747.1 8.6 dynamic_update_slice.33
  777.2 6.1 fusion.71
  789.1 7.0 fusion.109
  797.5 6.9 fusion.110
  804.5 77.0 %reduce-scatter.19.cloned.1.call-done = f32[512,768]{1,0:T(8,128)} async-done(((f32[2048,768]{1,0:T(8,128)}), f32[512,768]{1,0:T(8,128)}) %reduce-scatter.19.cloned.1.call-update) | async-done | bytes 1572880 | tf_op jit(solution)/shard_map/reduce_scatter | solution.py:82
  886.7 24.1 %all-reduce.9 = (f32[768]{0:T(1024)S(1)}, f32[768]{0:T(1024)S(1)}, f32[768]{0:T(1024)S(1)}, f32[768]{0:T(1024)S(1)}) all-reduce(f32[768]{0:T(1024)S(1)} %get-tuple-element.310, f32[768]{0:T(1024)S(1)} %get-tuple-element.309, f32[768]{0:T(1024)S(1)} %copy-done.49, f32[768]{0:T(1024)S(1)} %copy-done.48), channel_id=6, replica_groups=mesh['dp'=8,'tensor'=4] {'dp'}, use_global_device_ids=true, to_apply=%region_24.25.clone | all-reduce | flops 3072 | bytes 24576
  921.9 20.7 %all-reduce.10 = (bf16[1,4608]{1,0:T(2,128)(2,1)S(1)}, f32[96]{0:T(128)}, f32[96]{0:T(128)}, f32[96]{0:T(128)}) all-reduce(f32[1,4608]{1,0:T(1,128)S(1)} %fusion.108, f32[96]{0:T(128)S(1)} %dynamic-slice.7, f32[96]{0:T(128)S(1)} %dynamic-slice.9, f32[96]{0:T(128)S(1)} %dynamic-slice.13), channel_id=1, replica_groups=mesh['dp'=8,'tensor'=4] {'tensor'}, use_global_device_ids=true, to_apply=%region_19.20 | all-reduce | flops 4896 | bytes 29952 | tf_op jit(solution)/shard_map/psum | solution.py:356
  958.1 8.3 reduce-scatter.25.cloned.1.call-done
  970.4 5.4 all-to-all-done
  976.7 38.8 %reduce-scatter.21.cloned.1.call-done = f32[96,768]{1,0:T(8,128)} async-done(((f32[768,768]{1,0:T(8,128)}), f32[96,768]{1,0:T(8,128)}) %reduce-scatter.21.cloned.1.call-update) | async-done | bytes 294928 | tf_op jit(solution)/shard_map/reduce_scatter | solution.py:372
  1015.5 46.3 %reduce-scatter.23.cloned.1.call-done = f32[768,96]{0,1:T(8,128)} async-done(((f32[768,768]{0,1:T(8,128)}), f32[768,96]{0,1:T(8,128)}) %reduce-scatter.23.cloned.1.call-update) | async-done | bytes 294928 | tf_op jit(solution)/shard_map/reduce_scatter | solution.py:374
  (307 shorter events, 271.2 us)
Async XLA Ops:
  7.2 35.7 %all-gather.8.cloned.1.call-start = ((), (), s32[]{:S(2)}) async-start(), calls=%async_computation.10 | async-start | bytes 1327104 | tf_op jit(solution)/shard_map/all_gather | solution.py:203
  7.9 105.9 %all-gather.10.cloned.1.call-start = ((), (), s32[]{:S(2)}) async-start(), calls=%async_computation.11 | async-start | bytes 3932160 | tf_op jit(solution)/shard_map/all_gather | solution.py:65
  50.8 181.1 %reduce-scatter.13.cloned.1.call-start = ((), (), s32[]{:S(2)}) async-start(), calls=%async_computation.12 | async-start | bytes 3932160 | tf_op jit(solution)/shard_map/reduce_scatter | solution.py:73
  82.3 47.7 %copy-start.10 = (f32[2048,64]{0,1:T(8,128)}, f32[2048,64]{0,1:T(8,128)S(1)}, u32[]{:S(2)}) copy-start(f32[2048,64]{0,1:T(8,128)S(1)} %get-tuple-element.392) | copy-start | bytes 1572868
  82.4 47.7 %copy-start.22 = (f32[2048,64]{0,1:T(8,128)}, f32[2048,64]{0,1:T(8,128)S(1)}, u32[]{:S(2)}) copy-start(f32[2048,64]{0,1:T(8,128)S(1)} %get-tuple-element.393) | copy-start | bytes 1572868
  172.9 84.9 %all-gather.14.cloned.1.call-start = ((), (), s32[]{:S(2)}) async-start(), calls=%async_computation.14 | async-start | bytes 1327104 | tf_op jit(solution)/shard_map/all_gather | solution.py:194
  173.4 149.9 %all-gather.12.cloned.1.call-start = ((), (), s32[]{:S(2)}) async-start(), calls=%async_computation.13 | async-start | bytes 3932160 | tf_op jit(solution)/shard_map/all_gather | solution.py:65
  173.5 366.5 %copy-start.43 = (f32[768]{0:T(1024)}, f32[768]{0:T(1024)S(1)}, u32[]{:S(2)}) copy-start(f32[768]{0:T(1024)S(1)} %convert_element_type.152) | copy-start | bytes 9220
  234.1 308.4 %copy-start.1 = (f32[512,768]{1,0:T(8,128)}, f32[512,768]{1,0:T(8,128)S(1)}, u32[]{:S(2)}) copy-start(f32[512,768]{1,0:T(8,128)S(1)} %get-tuple-element.367) | copy-start | bytes 4718596
  234.1 308.4 %copy-start.35 = (f32[512]{0:T(512)}, f32[512]{0:T(512)S(1)}, u32[]{:S(2)}) copy-start(f32[512]{0:T(512)S(1)} %broadcast_multiply_fusion.9) | copy-start | bytes 6148
  235.8 306.8 %copy-start.37 = (f32[512]{0:T(512)}, f32[512]{0:T(512)S(1)}, u32[]{:S(2)}) copy-start(f32[512]{0:T(512)S(1)} %add_rsqrt_fusion) | copy-start | bytes 6148
  240.4 107.4 %all-gather.16.cloned.1.call-start = ((), (), s32[]{:S(2)}) async-start(), calls=%async_computation.15 | async-start | bytes 1327104 | tf_op jit(solution)/shard_map/all_gather | solution.py:196
  240.9 172.5 %all-gather.18.cloned.1.call-start = ((), (), s32[]{:S(2)}) async-start(), calls=%async_computation.17 | async-start | bytes 3932160 | tf_op jit(solution)/shard_map/all_gather | solution.py:69
  241.7 298.3 %reduce-scatter.17.cloned.1.call-start = ((), (), s32[]{:S(2)}) async-start(), calls=%async_computation.18 | async-start | bytes 7864320 | tf_op jit(solution)/shard_map/reduce_scatter | solution.py:82
  430.5 179.7 %all-gather.20.cloned.1.call-start = ((), (), s32[]{:S(2)}) async-start(), calls=%async_computation.19 | async-start | bytes 3932160 | tf_op jit(solution)/shard_map/all_gather | solution.py:69
  546.0 258.4 %reduce-scatter.15.cloned.1.call-start = ((), (), s32[]{:S(2)}) async-start(), calls=%async_computation.16 | async-start | bytes 3932160 | tf_op jit(solution)/shard_map/reduce_scatter | solution.py:73
  552.7 328.7 %reduce-scatter.19.cloned.1.call-start = ((), (), s32[]{:S(2)}) async-start(), calls=%async_computation.20 | async-start | bytes 7864320 | tf_op jit(solution)/shard_map/reduce_scatter | solution.py:82
  771.9 184.6 %reduce-scatter.27.cloned.1.call-start = ((), (), s32[]{:S(2)}) async-start(), calls=%async_computation.24 | async-start | bytes 884736
  777.1 189.3 %reduce-scatter.25.cloned.1.call-start = ((), (), s32[]{:S(2)}) async-start(), calls=%async_computation.23 | async-start | bytes 2211840
  789.0 226.4 %reduce-scatter.21.cloned.1.call-start = ((), (), s32[]{:S(2)}) async-start(), calls=%async_computation.21 | async-start | bytes 2654208 | tf_op jit(solution)/shard_map/reduce_scatter | solution.py:372
  796.1 265.7 %reduce-scatter.23.cloned.1.call-start = ((), (), s32[]{:S(2)}) async-start(), calls=%async_computation.22 | async-start | bytes 2654208 | tf_op jit(solution)/shard_map/reduce_scatter | solution.py:374
  797.4 84.0 %copy-start.38 = (f32[512]{0:T(512)S(1)}, f32[512]{0:T(512)}, u32[]{:S(2)}) copy-start(f32[512]{0:T(512)} %copy-done.37) | copy-start | bytes 6148
  797.5 84.0 %copy-start.40 = (f32[512]{0:T(512)S(1)}, f32[512]{0:T(512)}, u32[]{:S(2)}) copy-start(f32[512]{0:T(512)} %copy-done.39) | copy-start | bytes 6148
  797.5 84.0 %copy-start.42 = (f32[768]{0:T(1024)S(1)}, f32[768]{0:T(1024)}, u32[]{:S(2)}) copy-start(f32[768]{0:T(1024)} %copy-done.41) | copy-start | bytes 9220
  797.5 84.0 %copy-start.46 = (f32[512]{0:T(512)S(1)}, f32[512]{0:T(512)}, u32[]{:S(2)}) copy-start(f32[512]{0:T(512)} %copy-done.45) | copy-start | bytes 6148
  804.4 77.1 %copy-start.2 = (f32[512,768]{1,0:T(8,128)S(1)}, f32[512,768]{1,0:T(8,128)}, u32[]{:S(2)}) copy-start(f32[512,768]{1,0:T(8,128)} %copy-done.1) | copy-start | bytes 4718596
  804.4 77.1 %copy-start.5 = (bf16[512,768]{1,0:T(8,128)(2,1)S(1)}, bf16[512,768]{1,0:T(8,128)(2,1)}, u32[]{:S(2)}) copy-start(bf16[512,768]{1,0:T(8,128)(2,1)} %param.17) | copy-start | bytes 2359300
  804.4 77.1 %copy-start.36 = (f32[512]{0:T(512)S(1)}, f32[512]{0:T(512)}, u32[]{:S(2)}) copy-start(f32[512]{0:T(512)} %copy-done.35) | copy-start | bytes 6148
  804.4 82.3 %copy-start.48 = (f32[768]{0:T(1024)S(1)}, f32[768]{0:T(1024)}, u32[]{:S(2)}) copy-start(f32[768]{0:T(1024)} %get-tuple-element.358) | copy-start | bytes 9220
  804.4 82.3 %copy-start.49 = (f32[768]{0:T(1024)S(1)}, f32[768]{0:T(1024)}, u32[]{:S(2)}) copy-start(f32[768]{0:T(1024)} %get-tuple-element.360) | copy-start | bytes 9220
  944.7 8.0 all-to-all-start.1
  952.7 23.1 %all-to-all-start = ((bf16[8,128,576]{1,2,0:T(8,128)(2,1)}), bf16[8,128,576]{1,2,0:T(8,128)(2,1)S(1)}, u32[]{:S(2)}, u32[]{:S(2)}) async-start(bf16[8,128,576]{1,2,0:T(8,128)(2,1)} %bitcast.24), calls=%async_computation.4 | async-start | bytes 2359296 | tf_op jit(solution)/shard_map/all_to_all | solution.py:24
  (43 other events, 224.2 us)
Sparse Core Ops, SparseCore 0:
  9.9 26.8 all-gather.7
  51.0 62.8 all-gather.9
  173.0 58.8 reduce-scatter.12
  233.7 24.0 all-gather.13
  259.8 63.4 all-gather.11
  325.1 22.6 all-gather.15
  349.9 63.4 all-gather.17
  430.6 109.3 reduce-scatter.16
  546.1 64.0 all-gather.19
  612.3 58.8 reduce-scatter.14
  772.0 109.3 reduce-scatter.18
  884.4 35.5 reduce-scatter.26
  923.4 42.9 reduce-scatter.24
  970.6 44.8 reduce-scatter.20
  1019.3 42.4 reduce-scatter.22
where the time goes:
time: 1080 us; the launch traced here: 1070 us
  waiting for transfers between devices  601 us (56%)
  matrix products  176 us (16%)
  local copies, waits for them, and re-layouts  97.6 us (9%)
  blocking collectives  93.6 us (9%)
  other arithmetic  75.5 us (7%)
  between operations  17.2 us (2%)
    reduce_scatter x2, waiting for transfers between devices, collect_grads(): lax.psum_scatter(term_fn(jnp.int32(0), row_total * lax.axis_size('tensor'...  186 us
    all_gather x2, waiting for transfers between devices, spread_grads(): return lax.all_gather(local_part, 'tensor', axis=0, tiled=True)  123 us
    all_gather x2, waiting for transfers between devices, spread_rows(): return lax.all_gather(local_part, 'tensor', axis=0, tiled=True)  97 us
    reduce_scatter x2, waiting for transfers between devices, collect_rows(): lax.psum_scatter(term_fn(jnp.int32(0), row_total * lax.axis_size('tensor'...  58.4 us
    unnamed x2, blocking collectives  50.4 us
    reduce_scatter x1, waiting for transfers between devices, per_device(): lax.psum_scatter(down_grad, 'dp', scatter_dimension=1, tiled=True)  46.3 us
    reduce_scatter x1, waiting for transfers between devices, per_device(): lax.psum_scatter(up_grad, 'dp', scatter_dimension=0, tiled=True)  38.8 us
    unnamed x136, local copies, waits for them, and re-layouts  38 us
  transfers between devices with their start and end apart: 17, of which 14 were waited for; matrix products, arithmetic and copies ran while one was open for 23% of the time, Pallas kernels for 0%

commit v1 on v0

v1 whole, which is shorter than its diff:
```python
import functools
import math

import jax
import jax.numpy as jnp
from jax import lax
from jax.experimental import pallas as pl
from jax.experimental.pallas import tpu as pltpu
from jax.sharding import PartitionSpec as P

HEAD_DIM = 64
EPSILON = 1e-05
ROPE_BASE = 10000.0
GROUP = 4
PLANE_OF = (0, 3, 1, 2)
SEQ_OF = (0, 2, 3, 1)
AXES = ("dp", "tensor")
f32 = jnp.float32
bf16 = jnp.bfloat16


def permute(array, dp_size, target):
    pairs = []
    for d in range(dp_size):
        for z in range(GROUP):
            to_d, to_z = target(d, z)
            pairs.append((d * GROUP + z, to_d * GROUP + to_z))
    return lax.ppermute(array, AXES, pairs)


def swap_dp(array, dp_size, mask):
    return permute(array, dp_size, lambda d, z: (d ^ mask, z))


def swap_z(array, dp_size, mask):
    return permute(array, dp_size, lambda d, z: (d, z ^ mask))


def to_group(array, dp_size):
    return permute(array, dp_size, lambda d, z: (d // GROUP * GROUP + z, PLANE_OF[d % GROUP]))


def from_group(array, dp_size):
    return permute(array, dp_size, lambda d, z: (d // GROUP * GROUP + SEQ_OF[z], d % GROUP))


def reorder(array, index):
    count = array.shape[0]
    for k in range(count.bit_length() - 1):
        pairs = array.reshape(count >> (k + 1), 2, 1 << k, *array.shape[1:])
        pairs = jnp.concatenate([pairs[:, 1:], pairs[:, :1]], axis=1).reshape(array.shape)
        array = jnp.where((index >> k) % 2 == 1, pairs, array)
    return array


def seq_of(plane):
    return jnp.where(plane == 0, 0, jnp.where(plane == 3, 1, plane + 1))


def gather_dp(array, dp_size, me):
    if dp_size != 8:
        return lax.all_gather(array, "dp", axis=0, tiled=False)
    blocks = [array] + [swap_dp(array, dp_size, k) for k in range(1, 8)]
    return reorder(jnp.stack(blocks), me)


def place_kernel(where_ref, own, x, y, d0, d1, c_own, c_x, c_y, c_d0, c_d1, out, sems):
    rows = own.shape[1]
    me, slot = where_ref[0], where_ref[1]
    copies = []
    for ref, rel, first in (
        (own, 0, 0),
        (x, 2, 0),
        (y, 4, 0),
        (d0, 6, 0),
        (d1, 6, 2),
        (c_own, 1, 0),
        (c_x, 3, 0),
        (c_y, 5, 0),
        (c_d0, 7, 0),
        (c_d1, 7, 2),
    ):
        start = pl.multiple_of((me ^ rel) * rows, rows)
        for t in range(ref.shape[0]):
            copy = pltpu.make_async_copy(
                ref.at[t], out.at[(first + t) ^ slot, pl.ds(start, rows)], sems.at[len(copies)]
            )
            copy.start()
            copies.append(copy)
    for copy in copies:
        copy.wait()


def gather_weights(shard, dp_size, me, slot):
    rows, columns = shard.shape
    if dp_size != 8:
        full = lax.all_gather(shard, "dp", axis=0, tiled=True)
        full = jnp.stack([full] + [swap_z(full, dp_size, t) for t in range(1, GROUP)])
        return reorder(full, slot)
    own = jnp.stack([shard] + [swap_z(shard, dp_size, t) for t in range(1, GROUP)])
    x = swap_dp(own, dp_size, 2)
    y = swap_dp(own, dp_size, 4)
    d0 = swap_dp(x[:2], dp_size, 4)
    d1 = swap_dp(y[2:], dp_size, 2)
    near = (own, x, y, d0, d1)
    far = tuple(swap_dp(piece, dp_size, 1) for piece in near)
    return pl.pallas_call(
        place_kernel,
        out_shape=jax.ShapeDtypeStruct((GROUP, dp_size * rows, columns), shard.dtype),
        in_specs=[pl.BlockSpec(memory_space=pltpu.SMEM)] + [pl.BlockSpec(memory_space=pl.ANY)] * 10,
        out_specs=pl.BlockSpec(memory_space=pltpu.VMEM),
        scratch_shapes=[pltpu.SemaphoreType.DMA((32,))],
        compiler_params=pltpu.CompilerParams(vmem_limit_bytes=24 << 20),
        name="place",
    )(jnp.stack([me, slot]).astype(jnp.int32), *near, *far)


def spread_kernel(where_ref, grad, out, sems):
    rows = out.shape[2]
    me, slot = where_ref[0], where_ref[1]
    copies = []
    for k, rel in enumerate((0, 2, 4, 6, 1, 3, 5, 7)):
        start = pl.multiple_of((me ^ rel) * rows, rows)
        for t in range(GROUP):
            copy = pltpu.make_async_copy(
                grad.at[t ^ slot, pl.ds(start, rows)], out.at[k, t], sems.at[len(copies)]
            )
            copy.start()
            copies.append(copy)
    for copy in copies:
        copy.wait()


def plus(a, b):
    return (a.astype(f32) + b.astype(f32)).astype(bf16)


def reduce_weights(grad, dp_size, me, slot):
    columns = grad.shape[2]
    rows = grad.shape[1] // dp_size
    if dp_size != 8:
        grad = reorder(grad, slot)
        grad = lax.psum_scatter(grad, "dp", scatter_dimension=1, tiled=True)
        total = grad[0].astype(f32)
        for t in range(1, GROUP):
            total = total + swap_z(grad[t], dp_size, t).astype(f32)
        return total
    parts = pl.pallas_call(
        spread_kernel,
        out_shape=jax.ShapeDtypeStruct((8, GROUP, rows, columns), grad.dtype),
        in_specs=[
            pl.BlockSpec(memory_space=pltpu.SMEM),
            pl.BlockSpec(memory_space=pltpu.VMEM),
        ],
        out_specs=pl.BlockSpec(memory_space=pl.ANY),
        scratch_shapes=[pltpu.SemaphoreType.DMA((32,))],
        compiler_params=pltpu.CompilerParams(vmem_limit_bytes=24 << 20),
        name="spread",
    )(jnp.stack([me, slot]).astype(jnp.int32), grad)
    far = swap_dp(parts[4:], dp_size, 1)
    diagonal = plus(parts[3], far[3])
    from_x = swap_dp(diagonal[:2], dp_size, 2)
    from_y = swap_dp(diagonal[2:], dp_size, 4)
    x = parts[1].astype(f32) + far[1].astype(f32)
    y = parts[2].astype(f32) + far[2].astype(f32)
    x = jnp.concatenate([x[:2], x[2:] + from_y.astype(f32)]).astype(bf16)
    y = jnp.concatenate([y[:2] + from_x.astype(f32), y[2:]]).astype(bf16)
    from_x = swap_dp(x, dp_size, 2)
    from_y = swap_dp(y, dp_size, 4)
    own = (
        parts[0].astype(f32) + far[0].astype(f32) + from_x.astype(f32) + from_y.astype(f32)
    )
    total = own[0]
    for t in range(1, GROUP):
        total = total + swap_z(own[t].astype(bf16), dp_size, t).astype(f32)
    return total


def attend_kernel(a0, a1, a2, a3, o0, o1, o2, o3, lse, key_t, value_t, key):
    pieces = (a0, a1, a2, a3)
    block = a0.shape[1]
    for i, piece in enumerate(pieces):
        columns = slice(i * block, (i + 1) * block)
        key_t[:, columns] = piece[HEAD_DIM : 2 * HEAD_DIM]
        value_t[:, columns] = piece[2 * HEAD_DIM :]
    key[...] = key_t[...].T
    for i, (piece, out) in enumerate(zip(pieces, (o0, o1, o2, o3))):
        query = piece[:HEAD_DIM] * bf16(HEAD_DIM**-0.5)
        scores = jnp.dot(key[...], query, preferred_element_type=f32)
        highest = jnp.max(scores, axis=0, keepdims=True)
        exponent = jnp.exp(scores - highest)
        totals = jnp.sum(exponent, axis=0, keepdims=True)
        mixture = jnp.dot(value_t[...], exponent.astype(bf16), preferred_element_type=f32)
        out[...] = (mixture / totals).astype(bf16)
        lse[i : i + 1, :] = highest + jnp.log(totals)


def attend(pieces):
    block = pieces[0].shape[1]
    length = GROUP * block
    vmem = pl.BlockSpec(memory_space=pltpu.VMEM)
    *outs, lse = pl.pallas_call(
        attend_kernel,
        out_shape=[jax.ShapeDtypeStruct((HEAD_DIM, block), bf16)] * GROUP
        + [jax.ShapeDtypeStruct((GROUP, block), f32)],
        in_specs=[vmem] * GROUP,
        out_specs=[vmem] * (GROUP + 1),
        scratch_shapes=[
            pltpu.VMEM((HEAD_DIM, length), bf16),
            pltpu.VMEM((HEAD_DIM, length), bf16),
            pltpu.VMEM((length, HEAD_DIM), bf16),
        ],
        compiler_params=pltpu.CompilerParams(vmem_limit_bytes=40 << 20),
        cost_estimate=pl.CostEstimate(
            flops=16 * length * length * HEAD_DIM,
            bytes_accessed=2 * 4 * length * HEAD_DIM,
            transcendentals=length * length,
        ),
        name="attend",
    )(*pieces)
    return outs, lse


def attend_back_kernel(*refs):
    pieces, grads = refs[0:4], refs[4:8]
    lse, cosine, sine = refs[8:11]
    outs = refs[11:15]
    key_t, key, value_t, query_grad, key_grad, value_grad = refs[15:]
    block = pieces[0].shape[1]
    rows = min(256, block)
    for i, piece in enumerate(pieces):
        columns = slice(i * block, (i + 1) * block)
        key_t[:, columns] = piece[HEAD_DIM : 2 * HEAD_DIM]
        value_t[:, columns] = piece[2 * HEAD_DIM :]
        key[columns, :] = piece[HEAD_DIM : 2 * HEAD_DIM].T
    for i, (piece, grad) in enumerate(zip(pieces, grads)):
        log_total = lse[i : i + 1, :].T
        for c in range(block // rows):
            at = slice(c * rows, (c + 1) * rows)
            query_t = piece[:HEAD_DIM, at] * bf16(HEAD_DIM**-0.5)
            grad_t = grad[:, at]
            scores = jnp.dot(query_t.T, key_t[...], preferred_element_type=f32)
            weights = jnp.exp(scores - log_total[at])
            pull = jnp.dot(grad_t.T, value_t[...], preferred_element_type=f32)
            centre = jnp.sum(weights * pull, axis=1, keepdims=True)
            score_grad = (weights * (pull - centre)).astype(bf16)
            value_term = jnp.dot(grad_t, weights.astype(bf16), preferred_element_type=f32)
            key_term = jnp.dot(query_t, score_grad, preferred_element_type=f32)
            if i == 0 and c == 0:
                value_grad[...] = value_term
                key_grad[...] = key_term
            else:
                value_grad[...] += value_term
                key_grad[...] += key_term
            query_grad[:, i * block + c * rows : i * block + (c + 1) * rows] = (
                jnp.dot(score_grad, key[...], preferred_element_type=f32) * HEAD_DIM**-0.5
            ).T
    half = HEAD_DIM // 2
    for i, out in enumerate(outs):
        columns = slice(i * block, (i + 1) * block)
        cos, sin = cosine[:, columns], sine[:, columns]
        for first, source in ((0, query_grad), (HEAD_DIM, key_grad)):
            upper, lower = source[:half, columns], source[half:, columns]
            out[first : first + half] = (upper * cos + lower * sin).astype(bf16)
            out[first + half : first + HEAD_DIM] = (lower * cos - upper * sin).astype(bf16)
        out[2 * HEAD_DIM :] = value_grad[:, columns].astype(bf16)


def attend_back(pieces, grads, lse, cosine, sine):
    block = pieces[0].shape[1]
    length = GROUP * block
    vmem = pl.BlockSpec(memory_space=pltpu.VMEM)
    return pl.pallas_call(
        attend_back_kernel,
        out_shape=[jax.ShapeDtypeStruct((3 * HEAD_DIM, block), bf16)] * GROUP,
        in_specs=[vmem] * 11,
        out_specs=[vmem] * GROUP,
        scratch_shapes=[
            pltpu.VMEM((HEAD_DIM, length), bf16),
            pltpu.VMEM((length, HEAD_DIM), bf16),
            pltpu.VMEM((HEAD_DIM, length), bf16),
            pltpu.VMEM((HEAD_DIM, length), f32),
            pltpu.VMEM((HEAD_DIM, length), f32),
            pltpu.VMEM((HEAD_DIM, length), f32),
        ],
        compiler_params=pltpu.CompilerParams(vmem_limit_bytes=48 << 20),
        cost_estimate=pl.CostEstimate(
            flops=40 * length * length * HEAD_DIM,
            bytes_accessed=2 * 8 * length * HEAD_DIM,
            transcendentals=length * length,
        ),
        name="attend_back",
    )(*pieces, *grads, lse, cosine, sine)


def normalize(rows):
    center = jnp.mean(rows, axis=1, keepdims=True)
    shifted = rows - center
    inverse = lax.rsqrt(jnp.mean(shifted * shifted, axis=1, keepdims=True) + EPSILON)
    return shifted * inverse, inverse


def norm_back(scaled, normed, inverse):
    return inverse * (
        scaled
        - jnp.mean(scaled, axis=1, keepdims=True)
        - normed * jnp.mean(scaled * normed, axis=1, keepdims=True)
    )


def gelu_tanh(values):
    return jax.nn.gelu(values, approximate=True)


def einsum(spec, a, b):
    return jnp.einsum(spec, a, b, preferred_element_type=f32)


def per_device(
    dp_size,
    tokens,
    time_embed,
    ada_weight,
    ada_bias,
    norm1_gain,
    qkv_weight,
    out_weight,
    norm2_gain,
    up_weight,
    up_bias,
    down_weight,
    down_bias,
    out_grad,
):
    me = lax.axis_index("dp")
    z = lax.axis_index("tensor")
    position = me % GROUP
    rows, width = tokens.shape
    heads = qkv_weight.shape[2] // HEAD_DIM
    wide = heads * HEAD_DIM
    hidden = up_weight.shape[1]
    cond = time_embed.shape[1]

    first_shard = jnp.concatenate([*qkv_weight, out_weight.T], axis=1)
    second_shard = jnp.concatenate([up_weight, down_weight.T], axis=1)
    first_full = gather_weights(first_shard, dp_size, me, position)
    second_full = gather_weights(second_shard, dp_size, me, jnp.int32(0))
    qkv_full, out_full = first_full[:, :, : 3 * wide], first_full[:, :, 3 * wide :]
    up_full, down_full = second_full[:, :, :hidden], second_full[:, :, hidden:]

    moved = to_group(tokens, dp_size)
    upstream = to_group(out_grad, dp_size).astype(f32)

    per = norm1_gain.shape[0]
    lanes = max(per, cond, up_bias.shape[0])

    def fit(row):
        return jnp.pad(row, (0, lanes - row.shape[0]))

    small = jnp.stack(
        [fit(time_embed[0]), fit(norm1_gain), fit(norm2_gain), fit(down_bias), fit(up_bias)]
    )
    small = gather_dp(small, dp_size, me)
    embeds = small[:, 0, :cond]
    gain_one = small[:, 1, :per].reshape(1, width).astype(f32)
    gain_two = small[:, 2, :per].reshape(1, width).astype(f32)
    bias_down = small[:, 3, :per].reshape(1, width).astype(f32)
    bias_up = small[:, 4, : up_bias.shape[0]].reshape(1, hidden)
    bias_up = jnp.stack([bias_up] + [swap_z(bias_up, dp_size, t) for t in range(1, GROUP)])
    bias_up = bias_up.astype(f32)
    slices = einsum("sc,ce->se", embeds, ada_weight) + ada_bias.astype(f32)
    sequence = me // GROUP * GROUP + seq_of(z)
    modulation = gather_dp(slices, dp_size, me)
    modulation = lax.dynamic_index_in_dim(modulation, sequence, 1).reshape(6, 1, width)
    shift_one, scale_one, gate_one, shift_two, scale_two, gate_two = modulation
    ada_full = gather_dp(ada_weight, dp_size, me)

    half = HEAD_DIM // 2
    frequency = jnp.exp(
        jnp.arange(half, dtype=f32) * (-2.0 * math.log(ROPE_BASE) / HEAD_DIM)
    )
    quarter = position ^ jnp.arange(GROUP, dtype=jnp.int32)
    places = (quarter[:, None] * rows + jnp.arange(rows, dtype=jnp.int32)[None, :]).reshape(-1)
    angles = frequency[:, None] * places.astype(f32)[None, :]
    cosine, sine = jnp.cos(angles), jnp.sin(angles)

    inputs = moved.astype(f32)
    normed_one, inverse_one = normalize(inputs)
    factor_one = gain_one * (1.0 + scale_one)
    hidden_one = (normed_one * gain_one * (1.0 + scale_one) + shift_one).astype(bf16)
    projected = einsum("ld,tdc->tcl", hidden_one, qkv_full)
    projected = projected.reshape(GROUP, 3, heads, 2, half, rows)
    cos_own, sin_own = cosine[:, :rows], sine[:, :rows]
    upper, lower = projected[:, :2, :, 0], projected[:, :2, :, 1]
    rotated = jnp.stack(
        [upper * cos_own - lower * sin_own, lower * cos_own + upper * sin_own], axis=3
    )
    packed = jnp.concatenate([rotated, projected[:, 2:]], axis=1).astype(bf16)
    packed = packed.transpose(0, 2, 1, 3, 4, 5).reshape(GROUP, heads, 3 * HEAD_DIM, rows)

    def exchange(blocks):
        return [blocks[0]] + [swap_dp(blocks[r], dp_size, r) for r in range(1, GROUP)]

    saved, mixtures = [], []
    for h in range(heads):
        pieces = exchange([packed[r, h] for r in range(GROUP)])
        outs, lse = attend(pieces)
        saved.append((pieces, lse))
        mixtures.append(exchange(outs))
    attention = jnp.stack(
        [jnp.concatenate([mixtures[h][r] for h in range(heads)]) for r in range(GROUP)]
    )
    branch_one = einsum("rfl,rdf->ld", attention, out_full)

    residual = inputs + gate_one * branch_one
    normed_two, inverse_two = normalize(residual)
    hidden_two = (normed_two * gain_two * (1.0 + scale_two) + shift_two).astype(bf16)
    pre = einsum("ld,tdf->tlf", hidden_two, up_full) + bias_up
    activated = gelu_tanh(pre).astype(bf16)
    branch_two = einsum("tlf,tdf->ld", activated, down_full) + bias_down
    output = (residual + gate_two * branch_two).astype(bf16)
    output = from_group(output, dp_size)

    branch_two_grad = (gate_two * upstream).astype(bf16)
    act_grad = einsum("ld,tdf->tlf", branch_two_grad, down_full)
    pre_grad = jax.vjp(gelu_tanh, pre)[1](act_grad)[0].astype(bf16)
    hidden_two_grad = einsum("tlf,tdf->ld", pre_grad, up_full)
    factor_two = gain_two * (1.0 + scale_two)
    residual_grad = upstream + norm_back(hidden_two_grad * factor_two, normed_two, inverse_two)
    branch_one_grad = (gate_one * residual_grad).astype(bf16)
    attention_grad = einsum("ld,rdf->rfl", branch_one_grad, out_full).astype(bf16)

    up_grad = einsum("ld,tlf->tdf", hidden_two, pre_grad)
    down_grad = einsum("ld,tlf->tdf", branch_two_grad, activated)
    second_grad = jnp.concatenate([up_grad, down_grad], axis=2).astype(bf16)
    second_sum = reduce_weights(second_grad, dp_size, me, jnp.int32(0))
    up_out, down_out = second_sum[:, :hidden], second_sum[:, hidden:].T

    received = []
    for h in range(heads):
        pieces, lse = saved[h]
        grads = exchange(
            [attention_grad[r, h * HEAD_DIM : (h + 1) * HEAD_DIM] for r in range(GROUP)]
        )
        outs = attend_back(pieces, grads, lse, cosine, sine)
        received.append(exchange(outs))
    projected_grad = jnp.stack(
        [
            jnp.stack([received[h][r].reshape(3, HEAD_DIM, rows) for h in range(heads)], axis=1)
            for r in range(GROUP)
        ]
    ).reshape(GROUP, 3 * wide, rows)
    qkv_grad = einsum("ld,rcl->rdc", hidden_one, projected_grad)
    out_weight_grad = einsum("ld,rfl->rdf", branch_one_grad, attention)
    first_grad = jnp.concatenate([qkv_grad, out_weight_grad], axis=2).astype(bf16)
    first_sum = reduce_weights(first_grad, dp_size, me, position)
    qkv_out = jnp.stack(jnp.split(first_sum[:, : 3 * wide], 3, axis=1))
    out_out = first_sum[:, 3 * wide :].T

    hidden_one_grad = einsum("rcl,rdc->ld", projected_grad, qkv_full)
    input_grad = (
        residual_grad + norm_back(hidden_one_grad * factor_one, normed_one, inverse_one)
    ).astype(bf16)
    input_grad = from_group(input_grad, dp_size)

    def total(values):
        return jnp.sum(values, axis=0, keepdims=True)

    pull_one = total(hidden_one_grad * normed_one)
    pull_two = total(hidden_two_grad * normed_two)
    mine = jnp.concatenate(
        [
            total(hidden_one_grad),
            pull_one * gain_one,
            total(residual_grad * branch_one),
            total(hidden_two_grad),
            pull_two * gain_two,
            total(upstream * branch_two),
            pull_one * (1.0 + scale_one),
            pull_two * (1.0 + scale_two),
            total(branch_two_grad.astype(f32)),
            jnp.sum(pre_grad.astype(f32), axis=1).reshape(-1, width),
        ]
    )
    for_group = mine
    for r in range(1, GROUP):
        for_group = for_group + swap_dp(mine, dp_size, r)
    mod_grad = for_group[:6].astype(bf16).astype(f32)
    sums = for_group[6:9]
    bias_rows = for_group[9:].reshape(GROUP, -1, width)
    mods = [mod_grad]
    bias_sum = bias_rows[0]
    vector_sums = sums
    for t in range(1, GROUP):
        other = swap_z(jnp.concatenate([mod_grad, sums, bias_rows[t]]), dp_size, t)
        mods.append(other[:6])
        vector_sums = vector_sums + other[6:9]
        bias_sum = bias_sum + other[9:]
    mods = jnp.stack(mods)
    state = jnp.concatenate([mods.reshape(-1, width), vector_sums, bias_sum])
    quads = dp_size // GROUP
    if quads == 2:
        other = swap_dp(state, dp_size, GROUP)
        states = jnp.stack([state, other])
        quad_at = (me // GROUP) ^ jnp.arange(2)
    else:
        states = lax.all_gather(state, "dp", axis=0, tiled=False)
        states = states.reshape(quads, GROUP, *state.shape)
        states = lax.dynamic_index_in_dim(states, position, 1, keepdims=False)
        quad_at = jnp.arange(quads)
    tail = jnp.sum(states[:, 6 * GROUP :], axis=0)
    all_mods = states[:, : 6 * GROUP].reshape(quads * GROUP, 6 * width).astype(bf16)
    seq_at = seq_of(z ^ jnp.arange(GROUP))
    seq_at = (quad_at[:, None] * GROUP + seq_at[None, :]).reshape(-1)
    columns = ada_weight.shape[1]
    own_mods = lax.dynamic_slice_in_dim(all_mods, me * columns, columns, axis=1)
    pick = (seq_at[:, None] == jnp.arange(dp_size)[None, :]).astype(bf16)
    ada_out = einsum("sc,se->ce", jnp.dot(pick, embeds), own_mods)
    ada_bias_out = jnp.sum(own_mods.astype(f32), axis=0)
    mine_at = (seq_at == me).astype(f32)
    own_row = jnp.sum(all_mods.astype(f32) * mine_at[:, None], axis=0).astype(bf16)
    time_out = einsum("oe,oce->oc", own_row.reshape(dp_size, columns), ada_full)
    time_out = jnp.sum(time_out, axis=0, keepdims=True)

    def own_part(row):
        return lax.dynamic_slice_in_dim(row, me * per, per)

    bias_up_out = lax.dynamic_slice_in_dim(
        tail[3:].reshape(-1), me * up_bias.shape[0], up_bias.shape[0]
    )
    return (
        output,
        input_grad,
        time_out,
        ada_out,
        ada_bias_out,
        own_part(tail[0]),
        qkv_out,
        out_out,
        own_part(tail[1]),
        up_out,
        bias_up_out,
        down_out,
        own_part(tail[2]),
    )


def solution(mesh):
    placed = (
        P(("dp", "tensor"), None),
        P("dp", None),
        P(None, "dp"),
        P("dp"),
        P("dp"),
        P(None, "dp", "tensor"),
        P("tensor", "dp"),
        P("dp"),
        P("dp", "tensor"),
        P(("tensor", "dp")),
        P("tensor", "dp"),
        P("dp"),
        P(("dp", "tensor"), None),
    )
    return jax.shard_map(
        functools.partial(per_device, mesh.shape["dp"]),
        mesh=mesh,
        in_specs=placed,
        out_specs=(
            P(("dp", "tensor"), None),
            P(("dp", "tensor"), None),
            P("dp", None),
            P(None, "dp"),
            P("dp"),
            P("dp"),
            P(None, "dp", "tensor"),
            P("tensor", "dp"),
            P("dp"),
            P("dp", "tensor"),
            P(("tensor", "dp")),
            P("tensor", "dp"),
            P("dp"),
        ),
        check_vma=False,
    )
```

time: 1080 us -> 546 us (0.51)
  waiting for transfers between devices: 601 us -> 178 us
  starting transfers between devices: 7.89 us -> 153 us
  matrix products: 176 us -> 52.6 us
  blocking collectives: 93.6 us -> 0 us
  Pallas kernels: 0 us -> 74.5 us
  local copies, waits for them, and re-layouts: 97.6 us -> 41 us
  other arithmetic: 75.5 us -> 36.2 us
  between operations: 17.2 us -> 2.69 us
    reduce_scatter x6 -> x0, waiting for transfers between devices: 330 us -> none  [the longest x2 186 us: collect_grads(): lax.psum_scatter(term_fn(jnp.int32(0), row_total * lax.axis_size('tensor'...]
    all_gather x7 -> x0, waiting for transfers between devices: 253 us -> none  [the longest x2 123 us: spread_grads(): return lax.all_gather(local_part, 'tensor', axis=0, tiled=True)]
    ppermute x0 -> x111, waiting for transfers between devices: none -> 178 us  [permute(): return lax.ppermute(array, AXES, pairs)]
    ppermute x0 -> x111, starting transfers between devices: none -> 153 us  [permute(): return lax.ppermute(array, AXES, pairs)]
    dot_general x41 -> x15, matrix products: 168 us -> 52.6 us  [einsum(): return jnp.einsum(spec, a, b, preferred_element_type=f32)]
    pallas_call x0 -> x10, Pallas kernels: none -> 74.5 us  [the longest x3 34.3 us: attend_back(): pl.pallas_call(attend_back_kernel, out_shape=[jax.ShapeDtypeStruct((3 * H...]
    unnamed x2 -> x0, blocking collectives: 50.4 us -> none
    dynamic_update_slice x8 -> x0, local copies, waits for them, and re-layouts: 36.1 us -> none  [one_sequence(): lax.scan(one_block, (empty_grad, empty_grad), (query_seq.reshape(block_sh...]
  transfers between devices with their start and end apart: 17 -> 111, of which waited for: 14 -> 40; matrix products, arithmetic and copies ran while one was open for 23% -> 15% of each run, Pallas kernels for 0% -> 14%
where the time goes in v1:
time: 546 us; the launch traced here: 538 us
  waiting for transfers between devices  178 us (33%)
  starting transfers between devices  153 us (28%)
  Pallas kernels  74.5 us (14%)
  matrix products  52.6 us (10%)
  local copies, waits for them, and re-layouts  41 us (8%)
  other arithmetic  36.2 us (7%)
    ppermute x111, waiting for transfers between devices, permute(): return lax.ppermute(array, AXES, pairs)  178 us
    ppermute x111, starting transfers between devices, permute(): return lax.ppermute(array, AXES, pairs)  153 us
    dot_general x15, matrix products, einsum(): return jnp.einsum(spec, a, b, preferred_element_type=f32)  52.6 us
    pallas_call x3, Pallas kernels, attend_back(): pl.pallas_call(attend_back_kernel, out_shape=[jax.ShapeDtypeStruct((3 * H...  34.3 us
    pallas_call x3, Pallas kernels, attend(): pl.pallas_call(attend_kernel, out_shape=[jax.ShapeDtypeStruct((HEAD_DIM,...  20.3 us
    unnamed x117, local copies, waits for them, and re-layouts  17.5 us
  transfers between devices with their start and end apart: 111, of which 40 were waited for; matrix products, arithmetic and copies ran while one was open for 15% of the time, Pallas kernels for 14%

profile of v1, /device:TPU:0, one launch (start us, length us, event | category | flops | bytes accessed | tf_op | source)
XLA Modules:
  0.0 538.0 jit_solution(3506354577831880270)
XLA Ops:
  28.6 6.1 %collective-permute-start.15 = (bf16[96,768]{1,0:T(8,128)(2,1)}, bf16[96,768]{1,0:T(8,128)(2,1)S(1)}, u32[]{:S(2)}, u32[]{:S(2)}) collective-permute-start(bf16[96,768]{1,0:T(8,128)(2,1)} %pad_maximum_fusion.25), channel_id=1, source_target_pairs={{0,1},{1,0},{2,3},{3,2},{4,5},{5,4},{6,7},{7,6},{8,9},{9,8},{10,11... | collective-permute-start | bytes 442376 | tf_op jit(solution)/shard_map/ppermute | solution.py:28
  72.0 4.7 collective-permute-done.92
  90.7 23.6 %collective-permute-done.46 = bf16[96,1536]{1,0:T(8,128)(2,1)S(1)} collective-permute-done((bf16[96,1536]{1,0:T(8,128)(2,1)S(1)}, bf16[96,1536]{1,0:T(8,128)(2,1)S(1)}, u32[]{:S(2)}, u32[]{:S(2)}) %collective-permute-start.46) | collective-permute-done | bytes 294944 | tf_op jit(solution)/shard_map/ppermute | solution.py:28
  115.6 11.4 %collective-permute-start.24 = (bf16[4,96,768]{2,1,0:T(8,128)(2,1)S(1)}, bf16[4,96,768]{2,1,0:T(8,128)(2,1)S(1)}, u32[]{:S(2)}, u32[]{:S(2)}) collective-permute-start(bf16[4,96,768]{2,1,0:T(8,128)(2,1)S(1)} %collective-permute-done.19.y), channel_id=1, source_target_pairs={{0,4},{1,5},{2,6},{3,7},{4,0},{5,1},{6,2},{7,3},{8,12},{9,13},{10,... | collective-permute-start | bytes 1769480 | tf_op jit(solution)/shard_map/ppermute | solution.py:28
  131.7 7.2 %place.2 = bf16[4,768,768]{2,1,0:T(8,128)(2,1)S(1)} custom-call(s32[2]{0:T(128)S(1)} %pad_add_fusion.where_ref, bf16[4,96,768]{2,1,0:T(8,128)(2,1)S(1)} %pad_maximum_fusion.11.own, bf16[4,96,768]{2,1,0:T(8,128)(2,1)S(1)} %collective-permute-done.18.x, bf16[4,96,768]{2,1,0:T(8,128)(2,1)S(1)} %collective-permute-done.19.y, ...), custom_call_target="tpu_custom_call" | custom-call | tf_op jit(solution)/shard_map/place/pallas_call | solution.py:107
  146.4 11.4 %collective-permute-done.48.x = bf16[4,96,1536]{2,1,0:T(8,128)(2,1)S(1)} collective-permute-done((bf16[4,96,1536]{2,1,0:T(8,128)(2,1)S(1)}, bf16[4,96,1536]{2,1,0:T(8,128)(2,1)S(1)}, u32[]{:S(2)}, u32[]{:S(2)}) %collective-permute-start.48) | collective-permute-done | bytes 1179680 | tf_op jit(solution)/shard_map/ppermute | solution.py:28
  166.1 6.6 %attend.5 = (bf16[64,512]{1,0:T(8,128)(2,1)S(1)}, bf16[64,512]{1,0:T(8,128)(2,1)S(1)}, bf16[64,512]{1,0:T(8,128)(2,1)S(1)}, bf16[64,512]{1,0:T(8,128)(2,1)S(1)}, f32[4,512]{1,0:T(4,128)S(1)}) custom-call(bf16[192,512]{1,0:T(8,128)(2,1)S(1)} %get-tuple-element.147.a0.refs_0_, bf16[192,512]{1,0:T(8,128)(2,1)S(1)} %collective-permute-done.33.a1.refs_1_, ...), custom_call_target="tpu_custom_call" | custom-call | flops 4294967296 | bytes 1048576 | tf_op jit(solution)/shard_map/attend/pallas_call | solution.py:202
  176.5 7.0 %attend.4 = (bf16[64,512]{1,0:T(8,128)(2,1)S(1)}, bf16[64,512]{1,0:T(8,128)(2,1)S(1)}, bf16[64,512]{1,0:T(8,128)(2,1)S(1)}, bf16[64,512]{1,0:T(8,128)(2,1)S(1)}, f32[4,512]{1,0:T(4,128)S(1)}) custom-call(bf16[192,512]{1,0:T(8,128)(2,1)S(1)} %get-tuple-element.151.a0.refs_0_, bf16[192,512]{1,0:T(8,128)(2,1)S(1)} %collective-permute-done.30.a1.refs_1_, ...), custom_call_target="tpu_custom_call" | custom-call | flops 4294967296 | bytes 1048576 | tf_op jit(solution)/shard_map/attend/pallas_call | solution.py:202
  184.0 6.6 %attend.3 = (bf16[64,512]{1,0:T(8,128)(2,1)S(1)}, bf16[64,512]{1,0:T(8,128)(2,1)S(1)}, bf16[64,512]{1,0:T(8,128)(2,1)S(1)}, bf16[64,512]{1,0:T(8,128)(2,1)S(1)}, f32[4,512]{1,0:T(4,128)S(1)}) custom-call(bf16[192,512]{1,0:T(8,128)(2,1)S(1)} %get-tuple-element.154.a0.refs_0_, bf16[192,512]{1,0:T(8,128)(2,1)S(1)} %collective-permute-done.27.a1.refs_1_, ...), custom_call_target="tpu_custom_call" | custom-call | flops 4294967296 | bytes 1048576 | tf_op jit(solution)/shard_map/attend/pallas_call | solution.py:202
  204.9 9.8 %collective-permute-done.50.d0 = bf16[2,96,1536]{2,1,0:T(8,128)(2,1)S(1)} collective-permute-done((bf16[2,96,1536]{2,1,0:T(8,128)(2,1)S(1)}, bf16[2,96,1536]{2,1,0:T(8,128)(2,1)S(1)}, u32[]{:S(2)}, u32[]{:S(2)}) %collective-permute-start.50) | collective-permute-done | bytes 589856 | tf_op jit(solution)/shard_map/ppermute | solution.py:28
  223.2 6.4 %convert_reduce_fusion = (f32[4,768]{1,0:T(4,128)S(1)}, bf16[4,512,768]{2,1,0:T(8,128)(2,1)S(1)}) fusion(f32[4,768,512]{1,2,0:T(8,128)S(1)} %fusion.17, f32[4,768]{1,0:T(4,128)S(1)} %maximum_convert_fusion, bf16[4,768,1536]{2,1,0:T(8,128)(2,1)S(1)} %place.3, bf16[512,768]{1,0:T(8,128)(2,1)S(1)} %collective-permute-done.61, f32[768]{0:T(1024)S(1)} %get-tuple-element.116), kind=kOutput, calls=%fused_computation.17 | convolution fusion | flops 2453271552 | bytes 14970880 | tf_op jit(solution)/shard_map/ld,tdf->tlf/dot_general | solution.py:316
  229.7 4.6 convert_bitcast_fusion.1
  234.2 4.6 fusion.44
  238.9 8.0 %convert_reduce_fusion.2 = (f32[768]{0:T(1024)S(1)}, f32[768]{0:T(1024)S(1)}, bf16[512,768]{1,0:T(8,128)(2,1)}, f32[768]{0:T(1024)S(1)}, f32[512,768]{1,0:T(8,128)S(1)}) fusion(bf16[512,768]{1,0:T(8,128)(2,1)S(1)} %collective-permute-done.61, f32[768]{0:T(1024)S(1)} %get-tuple-element.116, f32[512,768]{1,0:T(8,128)S(1)} %get-tuple-element.132, ...), kind=kOutput, calls=%fused_computation.76 | convolution fusion | flops 2439902976 | bytes 18916352 | tf_op jit(solution)/shard_map/tlf,tdf->ld/dot_general | solution.py:316
  248.5 22.9 %collective-permute-start.68 = (bf16[64,512]{1,0:T(8,128)(2,1)S(1)}, bf16[64,512]{1,0:T(8,128)(2,1)S(1)}, u32[]{:S(2)}, u32[]{:S(2)}) collective-permute-start(bf16[64,512]{1,0:T(8,128)(2,1)S(1)} %get-tuple-element.172), channel_id=1, source_target_pairs={{0,4},{1,5},{2,6},{3,7},{4,0},{5,1},{6,2},{7,3},{8,12},{9,13},{10,... | collective-permute-start | bytes 196616 | tf_op jit(solution)/shard_map/ppermute | solution.py:28
  273.6 6.1 %convert_bitcast_fusion = bf16[4,768,768]{2,1,0:T(8,128)(2,1)S(1)} fusion(bf16[512,768]{1,0:T(8,128)(2,1)S(1)} %collective-permute-done.61, f32[768]{0:T(1024)S(1)} %get-tuple-element.116, f32[4,768,512]{1,2,0:T(8,128)} %copy-done.41, f32[4,768]{1,0:T(4,128)S(1)} %maximum_convert_fusion), kind=kOutput, calls=%fused_computation.19 | convolution fusion | flops 2435186688 | bytes 11811840 | tf_op jit(solution)/shard_map/ld,tlf->tdf/dot_general | solution.py:316
  286.0 11.3 %attend_back.5 = (bf16[192,512]{1,0:T(8,128)(2,1)S(1)}, bf16[192,512]{1,0:T(8,128)(2,1)S(1)}, bf16[192,512]{1,0:T(8,128)(2,1)S(1)}, bf16[192,512]{1,0:T(8,128)(2,1)S(1)}) custom-call(bf16[192,512]{1,0:T(8,128)(2,1)S(1)} %get-tuple-element.147.a0.refs_0_, bf16[192,512]{1,0:T(8,128)(2,1)S(1)} %collective-permute-done.33.a1.refs_1_, ...), custom_call_target="tpu_custom_call" | custom-call | flops 10737418240 | bytes 2097152 | tf_op jit(solution)/shard_map/attend_back/pallas_call | solution.py:273
  299.1 11.5 %attend_back.4 = (bf16[192,512]{1,0:T(8,128)(2,1)S(1)}, bf16[192,512]{1,0:T(8,128)(2,1)S(1)}, bf16[192,512]{1,0:T(8,128)(2,1)S(1)}, bf16[192,512]{1,0:T(8,128)(2,1)S(1)}) custom-call(bf16[192,512]{1,0:T(8,128)(2,1)S(1)} %get-tuple-element.151.a0.refs_0_, bf16[192,512]{1,0:T(8,128)(2,1)S(1)} %collective-permute-done.30.a1.refs_1_, ...), custom_call_target="tpu_custom_call" | custom-call | flops 10737418240 | bytes 2097152 | tf_op jit(solution)/shard_map/attend_back/pallas_call | solution.py:273
  312.0 11.5 %attend_back.3 = (bf16[192,512]{1,0:T(8,128)(2,1)S(1)}, bf16[192,512]{1,0:T(8,128)(2,1)S(1)}, bf16[192,512]{1,0:T(8,128)(2,1)S(1)}, bf16[192,512]{1,0:T(8,128)(2,1)S(1)}) custom-call(bf16[192,512]{1,0:T(8,128)(2,1)S(1)} %get-tuple-element.154.a0.refs_0_, bf16[192,512]{1,0:T(8,128)(2,1)S(1)} %collective-permute-done.27.a1.refs_1_, ...), custom_call_target="tpu_custom_call" | custom-call | flops 10737418240 | bytes 2097152 | tf_op jit(solution)/shard_map/attend_back/pallas_call | solution.py:273
  349.9 7.8 %collective-permute-start.60 = (bf16[512,768]{1,0:T(8,128)(2,1)}, bf16[512,768]{1,0:T(8,128)(2,1)}, u32[]{:S(2)}, u32[]{:S(2)}) collective-permute-start(bf16[512,768]{1,0:T(8,128)(2,1)} %get-tuple-element.155), channel_id=1, source_target_pairs={{0,0},{1,8},{2,12},{3,4},{4,1},{5,9},{6,13},{7,5},{8,2},{9,10},{10... | collective-permute-start | bytes 2359304 | tf_op jit(solution)/shard_map/ppermute | solution.py:28
  366.3 5.3 convolution_convert_fusion
  371.6 6.0 %copy.76 = bf16[4,576,768]{1,2,0:T(8,128)(2,1)} copy(bf16[4,576,768]{2,1,0:T(8,128)(2,1)} %convolution_convert_fusion) | data formatting | bytes 7077888 | tf_op jit(solution)/shard_map/convert.34
  380.9 7.0 %spread.2 = bf16[8,4,96,768]{3,2,1,0:T(8,128)(2,1)S(1)} custom-call(s32[2]{0:T(128)S(1)} %copy-done.5, bf16[4,768,768]{2,1,0:T(8,128)(2,1)S(1)} %pad_maximum_fusion.1.grad), custom_call_target="tpu_custom_call" | custom-call | tf_op jit(solution)/shard_map/spread/pallas_call | solution.py:148
  402.0 7.6 %collective-permute-start.80 = (bf16[512,768]{1,0:T(8,128)(2,1)}, bf16[512,768]{1,0:T(8,128)(2,1)}, u32[]{:S(2)}, u32[]{:S(2)}) collective-permute-start(bf16[512,768]{1,0:T(8,128)(2,1)} %fusion.39), channel_id=1, source_target_pairs={{0,0},{1,8},{2,12},{3,4},{4,1},{5,9},{6,13},{7,5},{8,2},{9,10},{10... | collective-permute-start | bytes 2359304 | tf_op jit(solution)/shard_map/ppermute | solution.py:28
  416.3 9.5 %collective-permute-done.98 = bf16[2,96,768]{2,1,0:T(8,128)(2,1)S(1)} collective-permute-done((bf16[2,96,768]{2,1,0:T(8,128)(2,1)S(1)}, bf16[2,96,768]{2,1,0:T(8,128)(2,1)S(1)}, u32[]{:S(2)}, u32[]{:S(2)}) %collective-permute-start.98) | collective-permute-done | bytes 294944 | tf_op jit(solution)/shard_map/ppermute | solution.py:28
  434.0 24.4 %collective-permute-done.106 = bf16[2,96,1536]{2,1,0:T(8,128)(2,1)S(1)} collective-permute-done((bf16[2,96,1536]{2,1,0:T(8,128)(2,1)S(1)}, bf16[2,96,1536]{2,1,0:T(8,128)(2,1)S(1)}, u32[]{:S(2)}, u32[]{:S(2)}) %collective-permute-start.106) | collective-permute-done | bytes 589856 | tf_op jit(solution)/shard_map/ppermute | solution.py:28
  459.7 12.3 %collective-permute-done.104 = bf16[2,96,1536]{2,1,0:T(8,128)(2,1)S(1)} collective-permute-done((bf16[2,96,1536]{2,1,0:T(8,128)(2,1)S(1)}, bf16[2,96,1536]{2,1,0:T(8,128)(2,1)S(1)}, u32[]{:S(2)}, u32[]{:S(2)}) %collective-permute-start.104) | collective-permute-done | bytes 589856 | tf_op jit(solution)/shard_map/ppermute | solution.py:28
  487.1 5.8 %collective-permute-done.101 = bf16[96,768]{1,0:T(8,128)(2,1)S(1)} collective-permute-done((bf16[96,768]{1,0:T(8,128)(2,1)S(1)}, bf16[96,768]{1,0:T(8,128)(2,1)S(1)}, u32[]{:S(2)}, u32[]{:S(2)}) %collective-permute-start.101) | collective-permute-done | bytes 147488 | tf_op jit(solution)/shard_map/ppermute | solution.py:28
  493.0 4.2 collective-permute-done.107
  503.5 4.1 collective-permute-start.110
  509.8 6.2 %collective-permute-done.110 = bf16[96,1536]{1,0:T(8,128)(2,1)} collective-permute-done((bf16[96,1536]{1,0:T(8,128)(2,1)}, bf16[96,1536]{1,0:T(8,128)(2,1)}, u32[]{:S(2)}, u32[]{:S(2)}) %collective-permute-start.110) | collective-permute-done | bytes 294944 | tf_op jit(solution)/shard_map/ppermute | solution.py:28
  515.9 15.7 %collective-permute-done.109 = bf16[96,1536]{1,0:T(8,128)(2,1)} collective-permute-done((bf16[96,1536]{1,0:T(8,128)(2,1)}, bf16[96,1536]{1,0:T(8,128)(2,1)}, u32[]{:S(2)}, u32[]{:S(2)}) %collective-permute-start.109) | collective-permute-done | bytes 294944 | tf_op jit(solution)/shard_map/ppermute | solution.py:28
  (496 shorter events, 238.2 us)
Async XLA Ops:
  16.9 63.7 %collective-permute-start.17 = (bf16[96,768]{1,0:T(8,128)(2,1)}, bf16[96,768]{1,0:T(8,128)(2,1)S(1)}, u32[]{:S(2)}, u32[]{:S(2)}) collective-permute-start(bf16[96,768]{1,0:T(8,128)(2,1)} %pad_maximum_fusion.25), channel_id=1, source_target_pairs={{0,3},{1,2},{2,1},{3,0},{4,7},{5,6},{6,5},{7,4},{8,11},{9,10},{10,... | collective-permute-start | bytes 442376 | tf_op jit(solution)/shard_map/ppermute | solution.py:28
  20.6 60.0 %collective-permute-start.16 = (bf16[96,768]{1,0:T(8,128)(2,1)}, bf16[96,768]{1,0:T(8,128)(2,1)S(1)}, u32[]{:S(2)}, u32[]{:S(2)}) collective-permute-start(bf16[96,768]{1,0:T(8,128)(2,1)} %pad_maximum_fusion.25), channel_id=1, source_target_pairs={{0,2},{1,3},{2,0},{3,1},{4,6},{5,7},{6,4},{7,5},{8,10},{9,11},{10,... | collective-permute-start | bytes 442376 | tf_op jit(solution)/shard_map/ppermute | solution.py:28
  28.6 54.0 %collective-permute-start.15 = (bf16[96,768]{1,0:T(8,128)(2,1)}, bf16[96,768]{1,0:T(8,128)(2,1)S(1)}, u32[]{:S(2)}, u32[]{:S(2)}) collective-permute-start(bf16[96,768]{1,0:T(8,128)(2,1)} %pad_maximum_fusion.25), channel_id=1, source_target_pairs={{0,1},{1,0},{2,3},{3,2},{4,5},{5,4},{6,7},{7,6},{8,9},{9,8},{10,11... | collective-permute-start | bytes 442376 | tf_op jit(solution)/shard_map/ppermute | solution.py:28
  34.6 26.9 %collective-permute-start.88 = (bf16[128,576]{0,1:T(8,128)(2,1)S(1)}, bf16[128,576]{0,1:T(8,128)(2,1)S(1)}, u32[]{:S(2)}, u32[]{:S(2)}) collective-permute-start(bf16[128,576]{0,1:T(8,128)(2,1)S(1)} %copy-done.14), channel_id=1, source_target_pairs={{0,4},{1,5},{2,6},{3,7},{4,0},{5,1},{6,2},{7,3},{8,12},{9,13},{10,... | collective-permute-start | bytes 442376 | tf_op jit(solution)/shard_map/ppermute | solution.py:28
  80.6 33.7 %collective-permute-start.46 = (bf16[96,1536]{1,0:T(8,128)(2,1)S(1)}, bf16[96,1536]{1,0:T(8,128)(2,1)S(1)}, u32[]{:S(2)}, u32[]{:S(2)}) collective-permute-start(bf16[96,1536]{1,0:T(8,128)(2,1)S(1)} %get-tuple-element.193), channel_id=1, source_target_pairs={{0,2},{1,3},{2,0},{3,1},{4,6},{5,7},{6,4},{7,5},{8,10},{9,11},{10,... | collective-permute-start | bytes 884744 | tf_op jit(solution)/shard_map/ppermute | solution.py:28
  80.7 33.6 %collective-permute-start.45 = (bf16[96,1536]{1,0:T(8,128)(2,1)S(1)}, bf16[96,1536]{1,0:T(8,128)(2,1)S(1)}, u32[]{:S(2)}, u32[]{:S(2)}) collective-permute-start(bf16[96,1536]{1,0:T(8,128)(2,1)S(1)} %get-tuple-element.193), channel_id=1, source_target_pairs={{0,1},{1,0},{2,3},{3,2},{4,5},{5,4},{6,7},{7,6},{8,9},{9,8},{10,11... | collective-permute-start | bytes 884744 | tf_op jit(solution)/shard_map/ppermute | solution.py:28
  82.6 33.0 %collective-permute-start = (bf16[512,768]{1,0:T(8,128)(2,1)S(1)}, bf16[512,768]{1,0:T(8,128)(2,1)S(1)}, u32[]{:S(2)}, u32[]{:S(2)}) collective-permute-start(bf16[512,768]{1,0:T(8,128)(2,1)S(1)} %copy-done.38), channel_id=1, source_target_pairs={{0,0},{1,4},{2,8},{3,12},{4,3},{5,7},{6,11},{7,15},{8,1},{9,5},{10... | collective-permute-start | bytes 2359304 | tf_op jit(solution)/shard_map/ppermute | solution.py:28
  83.5 30.9 %collective-permute-start.18 = (bf16[4,96,768]{2,1,0:T(8,128)(2,1)S(1)}, bf16[4,96,768]{2,1,0:T(8,128)(2,1)S(1)}, u32[]{:S(2)}, u32[]{:S(2)}) collective-permute-start(bf16[4,96,768]{2,1,0:T(8,128)(2,1)S(1)} %pad_maximum_fusion.11.own), channel_id=1, source_target_pairs={{0,8},{1,9},{2,10},{3,11},{4,12},{5,13},{6,14},{7,15},{8,0},{9,1},... | collective-permute-start | bytes 1769480 | tf_op jit(solution)/shard_map/ppermute | solution.py:28
  89.8 25.4 %collective-permute-start.19 = (bf16[4,96,768]{2,1,0:T(8,128)(2,1)S(1)}, bf16[4,96,768]{2,1,0:T(8,128)(2,1)S(1)}, u32[]{:S(2)}, u32[]{:S(2)}) collective-permute-start(bf16[4,96,768]{2,1,0:T(8,128)(2,1)S(1)} %pad_maximum_fusion.11.own), channel_id=1, source_target_pairs={{0,16},{1,17},{2,18},{3,19},{4,20},{5,21},{6,22},{7,23},{8,24},{9,... | collective-permute-start | bytes 1769480 | tf_op jit(solution)/shard_map/ppermute | solution.py:28
  128.5 29.4 %collective-permute-start.48 = (bf16[4,96,1536]{2,1,0:T(8,128)(2,1)S(1)}, bf16[4,96,1536]{2,1,0:T(8,128)(2,1)S(1)}, u32[]{:S(2)}, u32[]{:S(2)}) collective-permute-start(bf16[4,96,1536]{2,1,0:T(8,128)(2,1)S(1)} %pad_maximum_fusion.4.own), channel_id=1, source_target_pairs={{0,8},{1,9},{2,10},{3,11},{4,12},{5,13},{6,14},{7,15},{8,0},{9,1},... | collective-permute-start | bytes 3538952 | tf_op jit(solution)/shard_map/ppermute | solution.py:28
  131.0 28.0 %collective-permute-start.49 = (bf16[4,96,1536]{2,1,0:T(8,128)(2,1)S(1)}, bf16[4,96,1536]{2,1,0:T(8,128)(2,1)S(1)}, u32[]{:S(2)}, u32[]{:S(2)}) collective-permute-start(bf16[4,96,1536]{2,1,0:T(8,128)(2,1)S(1)} %pad_maximum_fusion.4.own), channel_id=1, source_target_pairs={{0,16},{1,17},{2,18},{3,19},{4,20},{5,21},{6,22},{7,23},{8,24},{9,... | collective-permute-start | bytes 3538952 | tf_op jit(solution)/shard_map/ppermute | solution.py:28
  143.5 22.3 %collective-permute-start.35 = (bf16[192,512]{1,0:T(8,128)(2,1)S(1)}, bf16[192,512]{1,0:T(8,128)(2,1)S(1)}, u32[]{:S(2)}, u32[]{:S(2)}) collective-permute-start(bf16[192,512]{1,0:T(8,128)(2,1)S(1)} %get-tuple-element.144), channel_id=1, source_target_pairs={{0,12},{1,13},{2,14},{3,15},{4,8},{5,9},{6,10},{7,11},{8,4},{9,5},... | collective-permute-start | bytes 589832 | tf_op jit(solution)/shard_map/ppermute | solution.py:28
  157.8 57.6 %collective-permute-start.52 = (bf16[4,96,1536]{2,1,0:T(8,128)(2,1)S(1)}, bf16[4,96,1536]{2,1,0:T(8,128)(2,1)S(1)}, u32[]{:S(2)}, u32[]{:S(2)}) collective-permute-start(bf16[4,96,1536]{2,1,0:T(8,128)(2,1)S(1)} %pad_maximum_fusion.4.own), channel_id=1, source_target_pairs={{0,4},{1,5},{2,6},{3,7},{4,0},{5,1},{6,2},{7,3},{8,12},{9,13},{10,... | collective-permute-start | bytes 3538952 | tf_op jit(solution)/shard_map/ppermute | solution.py:28
  248.5 35.3 %collective-permute-start.68 = (bf16[64,512]{1,0:T(8,128)(2,1)S(1)}, bf16[64,512]{1,0:T(8,128)(2,1)S(1)}, u32[]{:S(2)}, u32[]{:S(2)}) collective-permute-start(bf16[64,512]{1,0:T(8,128)(2,1)S(1)} %get-tuple-element.172), channel_id=1, source_target_pairs={{0,4},{1,5},{2,6},{3,7},{4,0},{5,1},{6,2},{7,3},{8,12},{9,13},{10,... | collective-permute-start | bytes 196616 | tf_op jit(solution)/shard_map/ppermute | solution.py:28
  272.8 24.5 %collective-permute-start.65 = (bf16[64,512]{1,0:T(8,128)(2,1)S(1)}, bf16[64,512]{1,0:T(8,128)(2,1)S(1)}, u32[]{:S(2)}, u32[]{:S(2)}) collective-permute-start(bf16[64,512]{1,0:T(8,128)(2,1)S(1)} %get-tuple-element.176), channel_id=1, source_target_pairs={{0,4},{1,5},{2,6},{3,7},{4,0},{5,1},{6,2},{7,3},{8,12},{9,13},{10,... | collective-permute-start | bytes 196616 | tf_op jit(solution)/shard_map/ppermute | solution.py:28
  273.5 25.1 %collective-permute-start.66 = (bf16[64,512]{1,0:T(8,128)(2,1)S(1)}, bf16[64,512]{1,0:T(8,128)(2,1)S(1)}, u32[]{:S(2)}, u32[]{:S(2)}) collective-permute-start(bf16[64,512]{1,0:T(8,128)(2,1)S(1)} %get-tuple-element.175), channel_id=1, source_target_pairs={{0,8},{1,9},{2,10},{3,11},{4,12},{5,13},{6,14},{7,15},{8,0},{9,1},... | collective-permute-start | bytes 196616 | tf_op jit(solution)/shard_map/ppermute | solution.py:28
  285.1 26.9 %collective-permute-start.62 = (bf16[64,512]{1,0:T(8,128)(2,1)S(1)}, bf16[64,512]{1,0:T(8,128)(2,1)S(1)}, u32[]{:S(2)}, u32[]{:S(2)}) collective-permute-start(bf16[64,512]{1,0:T(8,128)(2,1)S(1)} %get-tuple-element.179), channel_id=1, source_target_pairs={{0,4},{1,5},{2,6},{3,7},{4,0},{5,1},{6,2},{7,3},{8,12},{9,13},{10,... | collective-permute-start | bytes 196616 | tf_op jit(solution)/shard_map/ppermute | solution.py:28
  285.9 26.1 %collective-permute-start.63 = (bf16[64,512]{1,0:T(8,128)(2,1)S(1)}, bf16[64,512]{1,0:T(8,128)(2,1)S(1)}, u32[]{:S(2)}, u32[]{:S(2)}) collective-permute-start(bf16[64,512]{1,0:T(8,128)(2,1)S(1)} %get-tuple-element.178), channel_id=1, source_target_pairs={{0,8},{1,9},{2,10},{3,11},{4,12},{5,13},{6,14},{7,15},{8,0},{9,1},... | collective-permute-start | bytes 196616 | tf_op jit(solution)/shard_map/ppermute | solution.py:28
  298.6 43.6 %collective-permute-start.79 = (bf16[192,512]{1,0:T(8,128)(2,1)S(1)}, bf16[192,512]{1,0:T(8,128)(2,1)S(1)}, u32[]{:S(2)}, u32[]{:S(2)}) collective-permute-start(bf16[192,512]{1,0:T(8,128)(2,1)S(1)} %get-tuple-element.66), channel_id=1, source_target_pairs={{0,12},{1,13},{2,14},{3,15},{4,8},{5,9},{6,10},{7,11},{8,4},{9,5},... | collective-permute-start | bytes 589832 | tf_op jit(solution)/shard_map/ppermute | solution.py:28
  310.6 33.6 %collective-permute-start.78 = (bf16[192,512]{1,0:T(8,128)(2,1)S(1)}, bf16[192,512]{1,0:T(8,128)(2,1)}, u32[]{:S(2)}, u32[]{:S(2)}) collective-permute-start(bf16[192,512]{1,0:T(8,128)(2,1)S(1)} %get-tuple-element.65), channel_id=1, source_target_pairs={{0,12},{1,13},{2,14},{3,15},{4,8},{5,9},{6,10},{7,11},{8,4},{9,5},... | collective-permute-start | bytes 589832 | tf_op jit(solution)/shard_map/ppermute | solution.py:28
  324.0 20.8 %collective-permute-start.76 = (bf16[192,512]{1,0:T(8,128)(2,1)S(1)}, bf16[192,512]{1,0:T(8,128)(2,1)S(1)}, u32[]{:S(2)}, u32[]{:S(2)}) collective-permute-start(bf16[192,512]{1,0:T(8,128)(2,1)S(1)} %get-tuple-element.63), channel_id=1, source_target_pairs={{0,8},{1,9},{2,10},{3,11},{4,12},{5,13},{6,14},{7,15},{8,0},{9,1},... | collective-permute-start | bytes 589832 | tf_op jit(solution)/shard_map/ppermute | solution.py:28
  349.9 129.8 %collective-permute-start.60 = (bf16[512,768]{1,0:T(8,128)(2,1)}, bf16[512,768]{1,0:T(8,128)(2,1)}, u32[]{:S(2)}, u32[]{:S(2)}) collective-permute-start(bf16[512,768]{1,0:T(8,128)(2,1)} %get-tuple-element.155), channel_id=1, source_target_pairs={{0,0},{1,8},{2,12},{3,4},{4,1},{5,9},{6,13},{7,5},{8,2},{9,10},{10... | collective-permute-start | bytes 2359304 | tf_op jit(solution)/shard_map/ppermute | solution.py:28
  357.7 71.9 %collective-permute-start.103 = (bf16[4,4,96,1536]{3,2,1,0:T(8,128)(2,1)}, bf16[4,4,96,1536]{3,2,1,0:T(8,128)(2,1)}, u32[]{:S(2)}, u32[]{:S(2)}) collective-permute-start(bf16[4,4,96,1536]{3,2,1,0:T(8,128)(2,1)} %slice.662), channel_id=1, source_target_pairs={{0,4},{1,5},{2,6},{3,7},{4,0},{5,1},{6,2},{7,3},{8,12},{9,13},{10,... | collective-permute-start | bytes 14155784 | tf_op jit(solution)/shard_map/ppermute | solution.py:28
  390.8 22.3 %collective-permute-start.95 = (bf16[4,4,96,768]{3,2,1,0:T(8,128)(2,1)}, bf16[4,4,96,768]{3,2,1,0:T(8,128)(2,1)}, u32[]{:S(2)}, u32[]{:S(2)}) collective-permute-start(bf16[4,4,96,768]{3,2,1,0:T(8,128)(2,1)} %slice.641), channel_id=1, source_target_pairs={{0,4},{1,5},{2,6},{3,7},{4,0},{5,1},{6,2},{7,3},{8,12},{9,13},{10,... | collective-permute-start | bytes 7077896 | tf_op jit(solution)/shard_map/ppermute | solution.py:28
  402.0 78.9 %collective-permute-start.80 = (bf16[512,768]{1,0:T(8,128)(2,1)}, bf16[512,768]{1,0:T(8,128)(2,1)}, u32[]{:S(2)}, u32[]{:S(2)}) collective-permute-start(bf16[512,768]{1,0:T(8,128)(2,1)} %fusion.39), channel_id=1, source_target_pairs={{0,0},{1,8},{2,12},{3,4},{4,1},{5,9},{6,13},{7,5},{8,2},{9,10},{10... | collective-permute-start | bytes 2359304 | tf_op jit(solution)/shard_map/ppermute | solution.py:28
  426.0 47.2 %collective-permute-start.99 = (bf16[4,96,768]{2,1,0:T(8,128)(2,1)S(1)}, bf16[4,96,768]{2,1,0:T(8,128)(2,1)S(1)}, u32[]{:S(2)}, u32[]{:S(2)}) collective-permute-start(bf16[4,96,768]{2,1,0:T(8,128)(2,1)S(1)} %pad_maximum_fusion.17), channel_id=1, source_target_pairs={{0,16},{1,17},{2,18},{3,19},{4,20},{5,21},{6,22},{7,23},{8,24},{9,... | collective-permute-start | bytes 1769480 | tf_op jit(solution)/shard_map/ppermute | solution.py:28
  426.9 50.7 %collective-permute-start.97 = (bf16[4,96,768]{2,1,0:T(8,128)(2,1)S(1)}, bf16[4,96,768]{2,1,0:T(8,128)(2,1)}, u32[]{:S(2)}, u32[]{:S(2)}) collective-permute-start(bf16[4,96,768]{2,1,0:T(8,128)(2,1)S(1)} %pad_maximum_fusion.16), channel_id=1, source_target_pairs={{0,8},{1,9},{2,10},{3,11},{4,12},{5,13},{6,14},{7,15},{8,0},{9,1},... | collective-permute-start | bytes 1769480 | tf_op jit(solution)/shard_map/ppermute | solution.py:28
  433.8 24.6 %collective-permute-start.106 = (bf16[2,96,1536]{2,1,0:T(8,128)(2,1)S(1)}, bf16[2,96,1536]{2,1,0:T(8,128)(2,1)S(1)}, u32[]{:S(2)}, u32[]{:S(2)}) collective-permute-start(bf16[2,96,1536]{2,1,0:T(8,128)(2,1)S(1)} %get-tuple-element.162), channel_id=1, source_target_pairs={{0,8},{1,9},{2,10},{3,11},{4,12},{5,13},{6,14},{7,15},{8,0},{9,1},... | collective-permute-start | bytes 1769480 | tf_op jit(solution)/shard_map/ppermute | solution.py:28
  471.9 25.3 %collective-permute-start.107 = (bf16[4,96,1536]{2,1,0:T(8,128)(2,1)S(1)}, bf16[4,96,1536]{2,1,0:T(8,128)(2,1)}, u32[]{:S(2)}, u32[]{:S(2)}) collective-permute-start(bf16[4,96,1536]{2,1,0:T(8,128)(2,1)S(1)} %pad_maximum_fusion.9), channel_id=1, source_target_pairs={{0,16},{1,17},{2,18},{3,19},{4,20},{5,21},{6,22},{7,23},{8,24},{9,... | collective-permute-start | bytes 3538952 | tf_op jit(solution)/shard_map/ppermute | solution.py:28
  474.0 25.5 %collective-permute-start.105 = (bf16[4,96,1536]{2,1,0:T(8,128)(2,1)S(1)}, bf16[4,96,1536]{2,1,0:T(8,128)(2,1)}, u32[]{:S(2)}, u32[]{:S(2)}) collective-permute-start(bf16[4,96,1536]{2,1,0:T(8,128)(2,1)S(1)} %pad_maximum_fusion.8), channel_id=1, source_target_pairs={{0,8},{1,9},{2,10},{3,11},{4,12},{5,13},{6,14},{7,15},{8,0},{9,1},... | collective-permute-start | bytes 3538952 | tf_op jit(solution)/shard_map/ppermute | solution.py:28
  507.6 24.0 %collective-permute-start.109 = (bf16[96,1536]{1,0:T(8,128)(2,1)}, bf16[96,1536]{1,0:T(8,128)(2,1)}, u32[]{:S(2)}, u32[]{:S(2)}) collective-permute-start(bf16[96,1536]{1,0:T(8,128)(2,1)} %get-tuple-element.160), channel_id=1, source_target_pairs={{0,2},{1,3},{2,0},{3,1},{4,6},{5,7},{6,4},{7,5},{8,10},{9,11},{10,... | collective-permute-start | bytes 884744 | tf_op jit(solution)/shard_map/ppermute | solution.py:28
  507.6 24.0 %collective-permute-start.108 = (bf16[96,1536]{1,0:T(8,128)(2,1)S(1)}, bf16[96,1536]{1,0:T(8,128)(2,1)}, u32[]{:S(2)}, u32[]{:S(2)}) collective-permute-start(bf16[96,1536]{1,0:T(8,128)(2,1)S(1)} %get-tuple-element.158), channel_id=1, source_target_pairs={{0,1},{1,0},{2,3},{3,2},{4,5},{5,4},{6,7},{7,6},{8,9},{9,8},{10,11... | collective-permute-start | bytes 884744 | tf_op jit(solution)/shard_map/ppermute | solution.py:28
  (125 other events, 1634.1 us)

commit v2 on v1

v2 whole, which is shorter than its diff:
```python
import functools
import math

import jax
import jax.numpy as jnp
from jax import lax
from jax.experimental import pallas as pl
from jax.experimental.pallas import tpu as pltpu
from jax.sharding import PartitionSpec as P

HEAD_DIM = 64
EPSILON = 1e-05
ROPE_BASE = 10000.0
GROUP = 4
AXES = ("dp", "tensor")
f32 = jnp.float32
bf16 = jnp.bfloat16


def permute(array, dp_size, target):
    pairs = []
    for d in range(dp_size):
        for z in range(GROUP):
            to_d, to_z = target(d, z)
            pairs.append((d * GROUP + z, to_d * GROUP + to_z))
    return lax.ppermute(array, AXES, pairs)


def swap_dp(array, dp_size, mask):
    return permute(array, dp_size, lambda d, z: (d ^ mask, z))


def swap_z(array, dp_size, mask):
    return permute(array, dp_size, lambda d, z: (d, z ^ mask))


def swap_peer(array, dp_size, r):
    return permute(array, dp_size, lambda d, z: (d ^ (r >> 1), z ^ (r & 1)))


def regroup(array, dp_size):
    return permute(
        array, dp_size, lambda d, z: (d // 2 * 2 + z // 2, d % 2 * 2 + z % 2)
    )


def tie(arrays, *after):
    return lax.optimization_barrier((arrays, after))[0]


def reorder(array, index):
    count = array.shape[0]
    for k in range(count.bit_length() - 1):
        pairs = array.reshape(count >> (k + 1), 2, 1 << k, *array.shape[1:])
        pairs = jnp.concatenate([pairs[:, 1:], pairs[:, :1]], axis=1).reshape(array.shape)
        array = jnp.where((index >> k) % 2 == 1, pairs, array)
    return array


def gather_dp(array, dp_size):
    blocks = array[None]
    mask = 1
    while mask < dp_size:
        blocks = jnp.concatenate([blocks, swap_dp(blocks, dp_size, mask)])
        mask *= 2
    return blocks


PIECES = (
    (0, 0),
    (2, 0),
    (4, 0),
    (6, 0),
    (6, 2),
    (1, 0),
    (3, 0),
    (5, 0),
    (7, 0),
    (7, 2),
)


def stack_planes(shard, dp_size):
    return jnp.stack([shard] + [swap_z(shard, dp_size, t) for t in range(1, GROUP)])


def gather_weights(own, dp_size):
    if dp_size != 8:
        return (lax.all_gather(own, "dp", axis=1, tiled=True),)
    x = swap_dp(own, dp_size, 2)
    y = swap_dp(own, dp_size, 4)
    d0 = swap_dp(x[:2], dp_size, 4)
    d1 = swap_dp(y[2:], dp_size, 2)
    near = (own, x, y, d0, d1)
    return near + tuple(swap_dp(piece, dp_size, 1) for piece in near)


def load_weights(me, pieces, full, sems):
    if len(pieces) == 1:
        copies = [pltpu.make_async_copy(pieces[0], full, sems.at[0])]
    else:
        copies = []
        for i, (piece, (rel, first)) in enumerate(zip(pieces, PIECES)):
            count, rows = piece.shape[:2]
            start = pl.multiple_of((me ^ rel) * rows, rows)
            place = full.at[first : first + count, pl.ds(start, rows)]
            copies.append(pltpu.make_async_copy(piece, place, sems.at[i]))
    for copy in copies:
        copy.start()
    return copies


def store_blocks(me, outs, slot, value):
    if len(outs) == 1:
        outs[0][slot] = value
        return
    rows = outs[0].shape[2]
    for owner in range(2 * outs[0].shape[0]):
        rel = me ^ owner
        for parity, out in enumerate(outs):

            @pl.when((rel & 1) == parity)
            def _():
                out[rel >> 1, slot] = value[owner * rows : (owner + 1) * rows]


def grad_shapes(dp_size, width, columns):
    if dp_size != 8:
        return [jax.ShapeDtypeStruct((GROUP, width, columns), bf16)]
    return [jax.ShapeDtypeStruct((dp_size // 2, GROUP, width // dp_size, columns), bf16)] * 2


def plus(a, b):
    return (a.astype(f32) + b.astype(f32)).astype(bf16)


def reduce_cores(parts, dp_size):
    return swap_dp(parts[1], dp_size, 1) if dp_size == 8 else None


def reduce_first(parts, far, dp_size):
    if dp_size != 8:
        return None
    diagonal = plus(parts[0][3], far[3])
    return swap_dp(diagonal[:2], dp_size, 2), swap_dp(diagonal[2:], dp_size, 4)


def reduce_second(parts, far, half, dp_size):
    if dp_size != 8:
        total = lax.psum_scatter(parts[0], "dp", scatter_dimension=1, tiled=True)
        return total.astype(f32)
    near = parts[0]
    x = near[1].astype(f32) + far[1].astype(f32)
    y = near[2].astype(f32) + far[2].astype(f32)
    x = jnp.concatenate([x[:2], x[2:] + half[1].astype(f32)]).astype(bf16)
    y = jnp.concatenate([y[:2] + half[0].astype(f32), y[2:]]).astype(bf16)
    from_x = swap_dp(x, dp_size, 2)
    from_y = swap_dp(y, dp_size, 4)
    own = near[0].astype(f32) + far[0].astype(f32)
    return own + from_x.astype(f32) + from_y.astype(f32)


def reduce_planes(own, dp_size):
    total = own[0]
    for t in range(1, GROUP):
        total = total + swap_z(own[t].astype(bf16), dp_size, t).astype(f32)
    return total


def attend_kernel(a0, a1, a2, a3, o0, o1, o2, o3, lse, key_t, value_t, key):
    pieces = (a0, a1, a2, a3)
    block = a0.shape[1]
    for h in range(a0.shape[0] // (3 * HEAD_DIM)):
        at = 3 * HEAD_DIM * h
        for i, piece in enumerate(pieces):
            columns = slice(i * block, (i + 1) * block)
            key_t[:, columns] = piece[at + HEAD_DIM : at + 2 * HEAD_DIM]
            value_t[:, columns] = piece[at + 2 * HEAD_DIM : at + 3 * HEAD_DIM]
        key[...] = key_t[...].T
        for i, (piece, out) in enumerate(zip(pieces, (o0, o1, o2, o3))):
            query = piece[at : at + HEAD_DIM] * bf16(HEAD_DIM**-0.5)
            scores = jnp.dot(key[...], query, preferred_element_type=f32)
            highest = jnp.max(scores, axis=0, keepdims=True)
            exponent = jnp.exp(scores - highest)
            totals = jnp.sum(exponent, axis=0, keepdims=True)
            mixture = jnp.dot(value_t[...], exponent.astype(bf16), preferred_element_type=f32)
            out[h * HEAD_DIM : (h + 1) * HEAD_DIM] = (mixture / totals).astype(bf16)
            lse[h * GROUP + i : h * GROUP + i + 1, :] = highest + jnp.log(totals)


def attend(pieces):
    block = pieces[0].shape[1]
    heads = pieces[0].shape[0] // (3 * HEAD_DIM)
    length = GROUP * block
    vmem = pl.BlockSpec(memory_space=pltpu.VMEM)
    *outs, lse = pl.pallas_call(
        attend_kernel,
        out_shape=[jax.ShapeDtypeStruct((heads * HEAD_DIM, block), bf16)] * GROUP
        + [jax.ShapeDtypeStruct((heads * GROUP, block), f32)],
        in_specs=[vmem] * GROUP,
        out_specs=[vmem] * (GROUP + 1),
        scratch_shapes=[
            pltpu.VMEM((HEAD_DIM, length), bf16),
            pltpu.VMEM((HEAD_DIM, length), bf16),
            pltpu.VMEM((length, HEAD_DIM), bf16),
        ],
        compiler_params=pltpu.CompilerParams(vmem_limit_bytes=40 << 20),
        cost_estimate=pl.CostEstimate(
            flops=16 * heads * length * length * HEAD_DIM,
            bytes_accessed=8 * heads * length * HEAD_DIM,
            transcendentals=heads * length * length,
        ),
        name="attend",
    )(*pieces)
    return outs, lse


def attend_back_kernel(*refs):
    pieces, grads = refs[0:4], refs[4:8]
    lse, cosine, sine = refs[8:11]
    outs = refs[11:15]
    key_t, key, value_t, query_grad, key_grad, value_grad = refs[15:]
    block = pieces[0].shape[1]
    rows = min(256, block)
    half = HEAD_DIM // 2
    for h in range(grads[0].shape[0] // HEAD_DIM):
        at = 3 * HEAD_DIM * h
        for i, piece in enumerate(pieces):
            columns = slice(i * block, (i + 1) * block)
            key_t[:, columns] = piece[at + HEAD_DIM : at + 2 * HEAD_DIM]
            value_t[:, columns] = piece[at + 2 * HEAD_DIM : at + 3 * HEAD_DIM]
            key[columns, :] = piece[at + HEAD_DIM : at + 2 * HEAD_DIM].T
        for i, (piece, grad) in enumerate(zip(pieces, grads)):
            log_total = lse[h * GROUP + i : h * GROUP + i + 1, :].T
            for c in range(block // rows):
                own = slice(c * rows, (c + 1) * rows)
                query_t = piece[at : at + HEAD_DIM, own] * bf16(HEAD_DIM**-0.5)
                grad_t = grad[h * HEAD_DIM : (h + 1) * HEAD_DIM, own]
                scores = jnp.dot(query_t.T, key_t[...], preferred_element_type=f32)
                weights = jnp.exp(scores - log_total[own])
                pull = jnp.dot(grad_t.T, value_t[...], preferred_element_type=f32)
                centre = jnp.sum(weights * pull, axis=1, keepdims=True)
                score_grad = (weights * (pull - centre)).astype(bf16)
                value_term = jnp.dot(grad_t, weights.astype(bf16), preferred_element_type=f32)
                key_term = jnp.dot(query_t, score_grad, preferred_element_type=f32)
                if i == 0 and c == 0:
                    value_grad[...] = value_term
                    key_grad[...] = key_term
                else:
                    value_grad[...] += value_term
                    key_grad[...] += key_term
                query_grad[:, i * block + c * rows : i * block + (c + 1) * rows] = (
                    jnp.dot(score_grad, key[...], preferred_element_type=f32) * HEAD_DIM**-0.5
                ).T
        for i, out in enumerate(outs):
            columns = slice(i * block, (i + 1) * block)
            cos, sin = cosine[:, columns], sine[:, columns]
            for first, source in ((at, query_grad), (at + HEAD_DIM, key_grad)):
                upper, lower = source[:half, columns], source[half:, columns]
                out[first : first + half] = (upper * cos + lower * sin).astype(bf16)
                out[first + half : first + HEAD_DIM] = (lower * cos - upper * sin).astype(bf16)
            out[at + 2 * HEAD_DIM : at + 3 * HEAD_DIM] = value_grad[:, columns].astype(bf16)


def attend_back(pieces, grads, lse, cosine, sine):
    block = pieces[0].shape[1]
    heads = pieces[0].shape[0] // (3 * HEAD_DIM)
    length = GROUP * block
    vmem = pl.BlockSpec(memory_space=pltpu.VMEM)
    return pl.pallas_call(
        attend_back_kernel,
        out_shape=[jax.ShapeDtypeStruct((heads * 3 * HEAD_DIM, block), bf16)] * GROUP,
        in_specs=[vmem] * 11,
        out_specs=[vmem] * GROUP,
        scratch_shapes=[
            pltpu.VMEM((HEAD_DIM, length), bf16),
            pltpu.VMEM((length, HEAD_DIM), bf16),
            pltpu.VMEM((HEAD_DIM, length), bf16),
            pltpu.VMEM((HEAD_DIM, length), f32),
            pltpu.VMEM((HEAD_DIM, length), f32),
            pltpu.VMEM((HEAD_DIM, length), f32),
        ],
        compiler_params=pltpu.CompilerParams(vmem_limit_bytes=48 << 20),
        cost_estimate=pl.CostEstimate(
            flops=40 * heads * length * length * HEAD_DIM,
            bytes_accessed=16 * heads * length * HEAD_DIM,
            transcendentals=heads * length * length,
        ),
        name="attend_back",
    )(*pieces, *grads, lse, cosine, sine)


def normalize(rows):
    center = jnp.mean(rows, axis=1, keepdims=True)
    shifted = rows - center
    inverse = lax.rsqrt(jnp.mean(shifted * shifted, axis=1, keepdims=True) + EPSILON)
    return shifted * inverse, inverse


def norm_back(scaled, normed, inverse):
    return inverse * (
        scaled
        - jnp.mean(scaled, axis=1, keepdims=True)
        - normed * jnp.mean(scaled * normed, axis=1, keepdims=True)
    )


def dot(a, b):
    return jnp.dot(a, b, preferred_element_type=f32)


def dot_nt(a, b):
    return lax.dot_general(a, b, (((1,), (1,)), ((), ())), preferred_element_type=f32)


def total(values):
    return jnp.sum(values, axis=0, keepdims=True)


VMEM = pl.BlockSpec(memory_space=pltpu.VMEM)
SMEM = pl.BlockSpec(memory_space=pltpu.SMEM)
ANY = pl.BlockSpec(memory_space=pl.ANY)
HALF = HEAD_DIM // 2


def parts_of(heads):
    return (range(0, 1), range(1, heads)) if heads > 1 else (range(0, 1),)


def project_kernel(count, heads, *refs):
    where, tokens, vectors, cosine, sine = refs[:5]
    pieces, refs = refs[5 : 5 + count], refs[5 + count :]
    parts = parts_of(heads)
    hidden, packed = refs[0], refs[1 : 1 + GROUP * len(parts)]
    full, sems = refs[1 + GROUP * len(parts) :]
    me, base = where[0], where[1]
    wide = heads * HEAD_DIM
    copies = load_weights(me, pieces, full, sems)
    gain, scale, shift = vectors[0:1], vectors[1:2], vectors[2:3]
    normed, _ = normalize(tokens[...].astype(f32))
    hidden[...] = (normed * gain * (1.0 + scale) + shift).astype(bf16)
    cos, sin = cosine[...], sine[...]
    for copy in copies:
        copy.wait()
    for r in range(GROUP):
        projected = dot(hidden[...], full[base ^ r]).T
        for n, part in enumerate(parts):
            out = packed[r * len(parts) + n]
            for i, h in enumerate(part):
                at = 3 * HEAD_DIM * i
                for c in range(2):
                    first = c * wide + h * HEAD_DIM
                    upper = projected[first : first + HALF]
                    lower = projected[first + HALF : first + HEAD_DIM]
                    out[at : at + HALF] = (upper * cos - lower * sin).astype(bf16)
                    out[at + HALF : at + HEAD_DIM] = (lower * cos + upper * sin).astype(bf16)
                    at += HEAD_DIM
                first = 2 * wide + h * HEAD_DIM
                out[at : at + HEAD_DIM] = projected[first : first + HEAD_DIM].astype(bf16)


def project(where, tokens, vectors, cosine, sine, pieces, heads):
    rows, width = tokens.shape
    columns = pieces[0].shape[2]
    parts = parts_of(heads)
    outs = pl.pallas_call(
        functools.partial(project_kernel, len(pieces), heads),
        out_shape=[jax.ShapeDtypeStruct((rows, width), bf16)]
        + [jax.ShapeDtypeStruct((3 * HEAD_DIM * len(part), rows), bf16) for part in parts] * GROUP,
        in_specs=[SMEM] + [VMEM] * 4 + [ANY] * len(pieces),
        out_specs=[VMEM] * (1 + GROUP * len(parts)),
        scratch_shapes=[
            pltpu.VMEM((GROUP, width, columns), bf16),
            pltpu.SemaphoreType.DMA((len(pieces),)),
        ],
        compiler_params=pltpu.CompilerParams(vmem_limit_bytes=32 << 20),
        cost_estimate=pl.CostEstimate(
            flops=2 * rows * width * GROUP * columns,
            bytes_accessed=2 * GROUP * (width + rows) * columns,
            transcendentals=0,
        ),
        name="project",
    )(where, tokens, vectors, cosine, sine, *pieces)
    return outs[0], [outs[1 + n :: len(parts)] for n in range(len(parts))]


GELU_A = math.sqrt(2.0 / math.pi)
GELU_B = 0.044715


def feed_kernel(count, heads, *refs):
    where, tokens, upstream, vectors, bias_up = refs[:5]
    parts = parts_of(heads)
    used = GROUP * len(parts)
    mixtures, refs = refs[5 : 5 + used], refs[5 + used :]
    pieces, refs = refs[:count], refs[count:]
    output, residual_grad, out_hidden, out_branch_one, out_branch_two = refs[:5]
    activated, pre_grad, attention, sums, bias_sums = refs[5:10]
    mixture_grads = refs[10 : 10 + used]
    full, slope, keep_one, keep_two, sems = refs[10 + used :]
    me, base = where[0], where[1]
    wide = heads * HEAD_DIM
    hidden = bias_up.shape[1]
    of_out = slice(0, wide)
    of_up = slice(wide, wide + hidden)
    of_down = slice(wide + hidden, wide + 2 * hidden)
    copies = load_weights(me, pieces, full, sems)
    gain, scale, shift = vectors[0:1], vectors[1:2], vectors[2:3]
    gate_one, gate_two, bias_down = vectors[3:4], vectors[4:5], vectors[5:6]
    for r in range(GROUP):
        own = jnp.concatenate([mixtures[n * GROUP + r][...] for n in range(len(parts))])
        attention[r] = own.T
    for copy in copies:
        copy.wait()
    branch_one = dot_nt(attention[0], full[base, :, of_out])
    for r in range(1, GROUP):
        branch_one = branch_one + dot_nt(attention[r], full[base ^ r, :, of_out])
    keep_one[...] = branch_one
    residual = tokens[...].astype(f32) + gate_one * branch_one
    normed, _ = normalize(residual)
    out_hidden[...] = (normed * gain * (1.0 + scale) + shift).astype(bf16)

    keep_two[...] = jnp.broadcast_to(bias_down, keep_two.shape)

    def forward(t, carry):
        pre = dot(out_hidden[...], full[t, :, of_up]) + bias_up[pl.ds(t, 1)]
        inner = jnp.tanh(GELU_A * (pre + GELU_B * pre * pre * pre))
        activated[t] = (0.5 * pre * (1.0 + inner)).astype(bf16)
        slope[t] = 0.5 * (1.0 + inner) + (
            0.5 * GELU_A * pre * (1.0 - inner * inner) * (1.0 + 3.0 * GELU_B * pre * pre)
        )
        keep_two[...] += dot_nt(activated[t], full[t, :, of_down])
        return carry

    lax.fori_loop(0, GROUP, forward, 0)
    branch_two = keep_two[...]
    residual = tokens[...].astype(f32) + gate_one * keep_one[...]
    output[...] = (residual + gate_two * branch_two).astype(bf16)
    grad = upstream[...].astype(f32)
    branch_two_grad = gate_two * grad
    out_branch_two[...] = branch_two_grad.astype(bf16)
    sums[2:3] = total(grad * branch_two)
    sums[4:5] = total(out_branch_two[...].astype(f32))

    keep_two[...] = jnp.zeros_like(keep_two)

    def backward(t, carry):
        act_grad = dot(out_branch_two[...], full[t, :, of_down])
        pre_grad[t] = (act_grad * slope[t]).astype(bf16)
        bias_sums[pl.ds(t, 1)] = total(pre_grad[t].astype(f32))
        keep_two[...] += dot_nt(pre_grad[t], full[t, :, of_up])
        return carry

    lax.fori_loop(0, GROUP, backward, 0)
    hidden_grad = keep_two[...]
    residual = tokens[...].astype(f32) + gate_one * keep_one[...]
    normed, inverse = normalize(residual)
    sums[0:1] = total(hidden_grad)
    sums[1:2] = total(hidden_grad * normed)
    grad = upstream[...].astype(f32) + norm_back(
        hidden_grad * gain * (1.0 + scale), normed, inverse
    )
    residual_grad[...] = grad
    sums[3:4] = total(grad * keep_one[...])
    out_branch_one[...] = (gate_one * grad).astype(bf16)
    for r in range(GROUP):
        back = dot(out_branch_one[...], full[base ^ r, :, of_out]).astype(bf16).T
        for n, part in enumerate(parts):
            own = slice(part[0] * HEAD_DIM, (part[-1] + 1) * HEAD_DIM)
            mixture_grads[n * GROUP + r][...] = back[own]


def feed(where, tokens, upstream, vectors, bias_up, mixtures, pieces, heads):
    rows, width = tokens.shape
    wide = heads * HEAD_DIM
    hidden = bias_up.shape[1]
    columns = pieces[0].shape[2]
    parts = parts_of(heads)
    count = GROUP * len(parts)

    def shape(dtype, *lengths):
        return jax.ShapeDtypeStruct(lengths, dtype)

    outs = pl.pallas_call(
        functools.partial(feed_kernel, len(pieces), heads),
        out_shape=[
            shape(bf16, rows, width),
            shape(f32, rows, width),
            shape(bf16, rows, width),
            shape(bf16, rows, width),
            shape(bf16, rows, width),
            shape(bf16, GROUP, rows, hidden),
            shape(bf16, GROUP, rows, hidden),
            shape(bf16, GROUP, rows, wide),
            shape(f32, 5, width),
            shape(f32, GROUP, hidden),
        ]
        + [shape(bf16, len(part) * HEAD_DIM, rows) for part in parts for _ in range(GROUP)],
        in_specs=[SMEM] + [VMEM] * (4 + count) + [ANY] * len(pieces),
        out_specs=[VMEM] * (10 + count),
        scratch_shapes=[
            pltpu.VMEM((GROUP, width, columns), bf16),
            pltpu.VMEM((GROUP, rows, hidden), f32),
            pltpu.VMEM((rows, width), f32),
            pltpu.VMEM((rows, width), f32),
            pltpu.SemaphoreType.DMA((len(pieces),)),
        ],
        compiler_params=pltpu.CompilerParams(vmem_limit_bytes=56 << 20),
        cost_estimate=pl.CostEstimate(
            flops=4 * rows * width * GROUP * columns,
            bytes_accessed=2 * GROUP * (width + rows) * columns,
            transcendentals=GROUP * rows * hidden,
        ),
        name="feed",
    )(where, tokens, upstream, vectors, bias_up, *sum(mixtures, []), *pieces)
    grads = outs[10:]
    return outs[:10], [grads[n * GROUP : (n + 1) * GROUP] for n in range(len(parts))]


def feed_grads_kernel(where, hidden, branch_one, branch_two, act, pre, attention, *outs):
    me, base = where[0], where[1]
    t = pl.program_id(0)
    up = dot(hidden[...].T, pre[0]).astype(bf16)
    down = dot(branch_two[...].T, act[0]).astype(bf16)
    own = dot(branch_one[...].T, attention[base ^ t]).astype(bf16)
    store_blocks(me, outs, 0, jnp.concatenate([own, up, down], axis=1))


def feed_grads(dp_size, where, hidden, branch_one, branch_two, act, pre, attention):
    rows, width = hidden.shape
    wide, inner = attention.shape[2], act.shape[2]
    columns = wide + 2 * inner
    shapes = grad_shapes(dp_size, width, columns)
    if dp_size == 8:
        out_spec = pl.BlockSpec((4, 1, width // 8, columns), lambda t: (0, t, 0, 0))
    else:
        out_spec = pl.BlockSpec((1, width, columns), lambda t: (t, 0, 0))
    return pl.pallas_call(
        feed_grads_kernel,
        out_shape=shapes,
        grid=(GROUP,),
        in_specs=[SMEM]
        + [VMEM] * 3
        + [pl.BlockSpec((1, rows, inner), lambda t: (t, 0, 0))] * 2
        + [VMEM],
        out_specs=[out_spec] * len(shapes),
        compiler_params=pltpu.CompilerParams(vmem_limit_bytes=40 << 20),
        cost_estimate=pl.CostEstimate(
            flops=2 * rows * width * GROUP * columns,
            bytes_accessed=2 * GROUP * (width + rows) * columns,
            transcendentals=0,
        ),
        name="feed_grads",
    )(where, hidden, branch_one, branch_two, act, pre, attention)


def join_heads(pieces, heads, r):
    rows = []
    for c in range(3):
        for n, part in enumerate(parts_of(heads)):
            for i in range(len(part)):
                first = (3 * i + c) * HEAD_DIM
                rows.append(pieces[n * GROUP + r][first : first + HEAD_DIM])
    return jnp.concatenate(rows)


def project_grads_kernel(heads, used, where, hidden, *refs):
    pieces, outs = refs[:used], refs[used:]
    me, base = where[0], where[1]
    hidden_t = hidden[...].T
    for r in range(GROUP):
        value = dot_nt(hidden_t, join_heads(pieces, heads, r)).astype(bf16)
        store_blocks(me, outs, base ^ r, value)


def project_grads(dp_size, where, hidden, received, heads):
    rows, width = hidden.shape
    columns = 3 * heads * HEAD_DIM
    received = sum(received, [])
    shapes = grad_shapes(dp_size, width, columns)
    return pl.pallas_call(
        functools.partial(project_grads_kernel, heads, len(received)),
        out_shape=shapes,
        in_specs=[SMEM] + [VMEM] * (1 + len(received)),
        out_specs=[VMEM] * len(shapes),
        compiler_params=pltpu.CompilerParams(vmem_limit_bytes=32 << 20),
        cost_estimate=pl.CostEstimate(
            flops=2 * rows * width * GROUP * columns,
            bytes_accessed=2 * GROUP * (width + rows) * columns,
            transcendentals=0,
        ),
        name="project_grads",
    )(where, hidden, *received)


def project_back_kernel(count, heads, *refs):
    where, tokens, vectors, residual_grad = refs[:4]
    used = GROUP * len(parts_of(heads))
    received, refs = refs[4 : 4 + used], refs[4 + used :]
    pieces, (input_grad, sums, full, sems) = refs[:count], refs[count:]
    me, base = where[0], where[1]
    copies = load_weights(me, pieces, full, sems)
    gain, scale = vectors[0:1], vectors[1:2]
    normed, inverse = normalize(tokens[...].astype(f32))
    for copy in copies:
        copy.wait()
    hidden_grad = None
    for r in range(GROUP):
        term = dot_nt(join_heads(received, heads, r).T, full[base ^ r])
        hidden_grad = term if hidden_grad is None else hidden_grad + term
    sums[0:1] = total(hidden_grad)
    sums[1:2] = total(hidden_grad * normed)
    input_grad[...] = (
        residual_grad[...] + norm_back(hidden_grad * gain * (1.0 + scale), normed, inverse)
    ).astype(bf16)


def project_back(where, tokens, vectors, residual_grad, received, pieces, heads):
    rows, width = tokens.shape
    columns = pieces[0].shape[2]
    received = sum(received, [])
    return pl.pallas_call(
        functools.partial(project_back_kernel, len(pieces), heads),
        out_shape=[
            jax.ShapeDtypeStruct((rows, width), bf16),
            jax.ShapeDtypeStruct((2, width), f32),
        ],
        in_specs=[SMEM] + [VMEM] * (3 + len(received)) + [ANY] * len(pieces),
        out_specs=[VMEM] * 2,
        scratch_shapes=[
            pltpu.VMEM((GROUP, width, columns), bf16),
            pltpu.SemaphoreType.DMA((len(pieces),)),
        ],
        compiler_params=pltpu.CompilerParams(vmem_limit_bytes=32 << 20),
        cost_estimate=pl.CostEstimate(
            flops=2 * rows * width * GROUP * columns,
            bytes_accessed=2 * GROUP * (width + rows) * columns,
            transcendentals=0,
        ),
        name="project_back",
    )(where, tokens, vectors, residual_grad, *received, *pieces)


def einsum(spec, a, b):
    return jnp.einsum(spec, a, b, preferred_element_type=f32)


def per_device(
    dp_size,
    tokens,
    time_embed,
    ada_weight,
    ada_bias,
    norm1_gain,
    qkv_weight,
    out_weight,
    norm2_gain,
    up_weight,
    up_bias,
    down_weight,
    down_bias,
    out_grad,
):
    me = lax.axis_index("dp")
    z = lax.axis_index("tensor")
    position = me % 2 * 2 + z % 2
    base = z ^ position
    where = jnp.stack([me, base]).astype(jnp.int32)
    rows, width = tokens.shape
    heads = qkv_weight.shape[2] // HEAD_DIM
    wide = heads * HEAD_DIM
    hidden = up_weight.shape[1]
    cond = time_embed.shape[1]
    per = norm1_gain.shape[0]

    first_own = stack_planes(jnp.concatenate([*qkv_weight], axis=1), dp_size)
    first_pieces = gather_weights(first_own, dp_size)
    moved = regroup(tie(tokens, first_own), dp_size)
    second_shard = jnp.concatenate([out_weight.T, up_weight, down_weight.T], axis=1)
    second_own = stack_planes(tie(second_shard, moved), dp_size)
    second_pieces = gather_weights(second_own, dp_size)
    upstream = regroup(tie(out_grad, second_own), dp_size)

    lanes = max(per, cond, up_bias.shape[0])

    def fit(row):
        return jnp.pad(row, (0, lanes - row.shape[0]))

    small = jnp.stack(
        [fit(time_embed[0]), fit(norm1_gain), fit(norm2_gain), fit(down_bias), fit(up_bias)]
    )
    small = reorder(gather_dp(small, dp_size), me)
    embeds = small[:, 0, :cond]
    slices = einsum("sc,ce->se", embeds, ada_weight) + ada_bias.astype(f32)
    slices = gather_dp(slices, dp_size)
    sequence = me // 2 * 2 + z // 2
    modulation = reorder(lax.dynamic_index_in_dim(slices, sequence, 1), me).reshape(6, 1, width)
    shift_one, scale_one, gate_one, shift_two, scale_two, gate_two = modulation
    gain_one = small[:, 1, :per].reshape(1, width).astype(f32)
    gain_two = small[:, 2, :per].reshape(1, width).astype(f32)
    bias_down = small[:, 3, :per].reshape(1, width).astype(f32)
    bias_up = tie(small[:, 4, : up_bias.shape[0]].reshape(1, hidden), moved)
    bias_up = jnp.concatenate([bias_up, swap_z(bias_up, dp_size, 1)])
    bias_up = jnp.concatenate([bias_up, swap_z(bias_up, dp_size, 2)]).astype(f32)
    vectors_one = jnp.concatenate([gain_one, scale_one, shift_one])
    vectors_two = jnp.concatenate([gain_two, scale_two, shift_two, gate_one, gate_two, bias_down])
    ada_full = gather_dp(tie(ada_weight, second_pieces[1:3]), dp_size)

    frequency = jnp.exp(
        jnp.arange(HALF, dtype=f32) * (-2.0 * math.log(ROPE_BASE) / HEAD_DIM)
    )
    quarter = position ^ jnp.arange(GROUP, dtype=jnp.int32)
    places = (quarter[:, None] * rows + jnp.arange(rows, dtype=jnp.int32)[None, :]).reshape(-1)
    angles = frequency[:, None] * places.astype(f32)[None, :]
    cosine, sine = jnp.cos(angles), jnp.sin(angles)

    def exchange(blocks):
        return [blocks[0]] + [swap_peer(blocks[r], dp_size, r) for r in range(1, GROUP)]

    hidden_one, packed = project(
        where, moved, vectors_one, cosine[:, :rows], sine[:, :rows], first_pieces, heads
    )
    saved, mixtures = [], []
    for blocks in packed:
        pieces = exchange(blocks)
        outs, lse = attend(pieces)
        saved.append((pieces, lse))
        mixtures.append(exchange(outs))

    outs, mixture_grads = feed(
        where, moved, upstream, vectors_two, bias_up, mixtures, second_pieces, heads
    )
    output, residual_grad, hidden_two, branch_one_grad, branch_two_grad = outs[:5]
    activated, pre_grad, attention, feed_sums, bias_sums = outs[5:]
    second_grad = feed_grads(
        dp_size, where, hidden_two, branch_one_grad, branch_two_grad, activated, pre_grad, attention
    )
    second_far = reduce_cores(second_grad, dp_size)

    received = [None] * len(saved)
    order = list(reversed(range(len(saved))))
    incoming = {n: exchange(mixture_grads[n]) for n in order}
    output = regroup(tie(output, incoming[order[-1]]), dp_size)
    gates = [(second_grad,), (second_far,)]
    for n in order:
        pieces, lse = saved[n]
        grads = tie(incoming[n], *gates.pop(0))
        received[n] = exchange(attend_back(pieces, grads, lse, cosine, sine))
    second_half = reduce_first(second_grad, second_far, dp_size)
    first_grad = project_grads(dp_size, where, hidden_one, received, heads)
    first_far = reduce_cores(first_grad, dp_size)
    input_grad, project_sums = project_back(
        where, moved, vectors_one, residual_grad, received, first_pieces, heads
    )
    input_grad = regroup(input_grad, dp_size)
    second_sum = reduce_second(second_grad, second_far, second_half, dp_size)
    first_half = reduce_first(first_grad, first_far, dp_size)
    first_sum = reduce_second(first_grad, first_far, first_half, dp_size)
    second_sum = reduce_planes(second_sum, dp_size)
    first_sum = reduce_planes(first_sum, dp_size)
    out_out = second_sum[:, :wide].T
    up_out = second_sum[:, wide : wide + hidden]
    down_out = second_sum[:, wide + hidden :].T
    qkv_out = jnp.stack(jnp.split(first_sum, 3, axis=1))

    pull_one, pull_two = project_sums[1:2], feed_sums[1:2]
    mine = jnp.concatenate(
        [
            project_sums[:1],
            pull_one * gain_one,
            feed_sums[3:4],
            feed_sums[:1],
            pull_two * gain_two,
            feed_sums[2:3],
            pull_one * (1.0 + scale_one),
            pull_two * (1.0 + scale_two),
            feed_sums[4:5],
        ]
    )
    bias_sums = bias_sums.reshape(GROUP, hidden // width, width)
    other = swap_z(jnp.concatenate([mine, bias_sums.reshape(-1, width)]), dp_size, 1)
    other_bias = other[9:].reshape(bias_sums.shape)
    mine = jnp.concatenate(
        [mine + other[:9], bias_sums[0] + other_bias[1], bias_sums[2] + other_bias[3]]
    )
    mine = mine + swap_dp(mine, dp_size, 1)
    mods = mine[:6].astype(bf16).astype(f32)[None]
    other = swap_z(jnp.concatenate([mods[0], mine[6:]]), dp_size, 2)
    mods = jnp.concatenate([mods, other[None, :6]])
    flat = hidden // width
    tail = jnp.concatenate([mine[6:9] + other[6:9], mine[9 : 9 + flat] + other[9 + flat :]])
    mask = 2
    while mask < dp_size:
        other = swap_dp(jnp.concatenate([mods.reshape(-1, width), tail]), dp_size, mask)
        mods = jnp.concatenate([mods, other[: -tail.shape[0]].reshape(mods.shape)])
        tail = tail + other[-tail.shape[0] :]
        mask *= 2
    rel = jnp.arange(dp_size)
    seq_at = (me // 2 ^ rel // 2) * 2 + (z // 2 ^ rel % 2)
    mods = mods.reshape(dp_size, 6 * width).astype(bf16)
    columns = ada_weight.shape[1]
    own_mods = lax.dynamic_slice_in_dim(mods, me * columns, columns, axis=1)
    pick = (seq_at[:, None] == jnp.arange(dp_size)[None, :]).astype(bf16)
    ada_out = einsum("sc,se->ce", jnp.dot(pick, embeds), own_mods)
    ada_bias_out = jnp.sum(own_mods.astype(f32), axis=0)
    mine_at = (seq_at == me).astype(f32)
    own_row = jnp.sum(mods.astype(f32) * mine_at[:, None], axis=0).astype(bf16)
    own_row = reorder(own_row.reshape(dp_size, columns), me)
    time_out = jnp.sum(einsum("oe,oce->oc", own_row, ada_full), axis=0, keepdims=True)

    def own_part(row):
        return lax.dynamic_slice_in_dim(row, me * per, per)

    bias_up_out = lax.dynamic_slice_in_dim(
        tail[3:].reshape(-1), me * up_bias.shape[0], up_bias.shape[0]
    )
    return (
        output,
        input_grad,
        time_out,
        ada_out,
        ada_bias_out,
        own_part(tail[0]),
        qkv_out,
        out_out,
        own_part(tail[1]),
        up_out,
        bias_up_out,
        down_out,
        own_part(tail[2]),
    )


def solution(mesh):
    placed = (
        P(("dp", "tensor"), None),
        P("dp", None),
        P(None, "dp"),
        P("dp"),
        P("dp"),
        P(None, "dp", "tensor"),
        P("tensor", "dp"),
        P("dp"),
        P("dp", "tensor"),
        P(("tensor", "dp")),
        P("tensor", "dp"),
        P("dp"),
        P(("dp", "tensor"), None),
    )
    return jax.shard_map(
        functools.partial(per_device, mesh.shape["dp"]),
        mesh=mesh,
        in_specs=placed,
        out_specs=(
            P(("dp", "tensor"), None),
            P(("dp", "tensor"), None),
            P("dp", None),
            P(None, "dp"),
            P("dp"),
            P("dp"),
            P(None, "dp", "tensor"),
            P("tensor", "dp"),
            P("dp"),
            P("dp", "tensor"),
            P(("tensor", "dp")),
            P("tensor", "dp"),
            P("dp"),
        ),
        check_vma=False,
    )
```

time: 546 us -> 442 us (0.81)
  starting transfers between devices: 153 us -> 84.1 us
  matrix products: 52.6 us -> 3.27 us
  Pallas kernels: 74.5 us -> 110 us
  waiting for transfers between devices: 178 us -> 155 us
  local copies, waits for them, and re-layouts: 41 us -> 51.7 us
  other arithmetic: 36.2 us -> 29.5 us
    ppermute x111 -> x84, starting transfers between devices: 153 us -> 84.1 us  [permute(): return lax.ppermute(array, AXES, pairs)]
    dot_general x15 -> x3, matrix products: 52.6 us -> 3.27 us  [einsum(): return jnp.einsum(spec, a, b, preferred_element_type=f32)]
    pallas_call x10 -> x9, Pallas kernels: 74.5 us -> 110 us  [the longest x2 35.1 us: attend_back(): pl.pallas_call(attend_back_kernel, out_shape=[jax.ShapeDtypeStruct((heads...]
    ppermute x111 -> x84, waiting for transfers between devices: 178 us -> 155 us  [permute(): return lax.ppermute(array, AXES, pairs)]
    unnamed x117 -> x220, local copies, waits for them, and re-layouts: 17.5 us -> 28.6 us
    another operation x14 -> x4, local copies, waits for them, and re-layouts: 9.75 us -> 1.7 us  [the longest x1 0.91 us: per_device(): first_own = stack_planes(jnp.concatenate([*qkv_weight], axis=1), dp_size)]
  transfers between devices with their start and end apart: 111 -> 84, of which waited for: 40 -> 29; matrix products, arithmetic and copies ran while one was open for 15% -> 12% of each run, Pallas kernels for 14% -> 16%
where the time goes in v2:
time: 442 us; the launch traced here: 437 us
  waiting for transfers between devices  155 us (35%)
  Pallas kernels  110 us (25%)
  starting transfers between devices  84.1 us (19%)
  local copies, waits for them, and re-layouts  51.7 us (12%)
  other arithmetic  29.5 us (7%)
    ppermute x84, waiting for transfers between devices, permute(): return lax.ppermute(array, AXES, pairs)  155 us
    ppermute x84, starting transfers between devices, permute(): return lax.ppermute(array, AXES, pairs)  84.1 us
    pallas_call x2, Pallas kernels, attend_back(): pl.pallas_call(attend_back_kernel, out_shape=[jax.ShapeDtypeStruct((heads...  35.1 us
    pallas_call x1, Pallas kernels, feed(): pl.pallas_call(functools.partial(feed_kernel, len(pieces), heads), out_sh...  28.7 us
    unnamed x220, local copies, waits for them, and re-layouts  28.6 us
    pallas_call x2, Pallas kernels, attend(): pl.pallas_call(attend_kernel, out_shape=[jax.ShapeDtypeStruct((heads * HE...  19.3 us
    pallas_call x1, Pallas kernels, feed_grads(): pl.pallas_call(feed_grads_kernel, out_shape=shapes, grid=(GROUP,), in_spe...  10 us
  transfers between devices with their start and end apart: 84, of which 29 were waited for; matrix products, arithmetic and copies ran while one was open for 12% of the time, Pallas kernels for 16%

profile of v2, /device:TPU:0, one launch (start us, length us, event | category | flops | bytes accessed | tf_op | source)
XLA Modules:
  0.0 436.8 jit_solution(656477209968034574)
XLA Ops:
  1.7 4.1 collective-permute-start.1
  30.2 9.0 %collective-permute-done.17.refs_7_.refs_14_ = bf16[4,96,576]{2,1,0:T(8,128)(2,1)S(1)} collective-permute-done((bf16[4,96,576]{2,1,0:T(8,128)(2,1)S(1)}, bf16[4,96,576]{2,1,0:T(8,128)(2,1)S(1)}, u32[]{:S(2)}, u32[]{:S(2)}) %collective-permute-start.17) | collective-permute-done | bytes 442400 | tf_op jit(solution)/shard_map/ppermute | solution.py:26
  42.1 4.9 %collective-permute-done.19.refs_9_.refs_16_ = bf16[2,96,576]{2,1,0:T(8,128)(2,1)} collective-permute-done((bf16[2,96,576]{2,1,0:T(8,128)(2,1)S(1)}, bf16[2,96,576]{2,1,0:T(8,128)(2,1)}, u32[]{:S(2)}, u32[]{:S(2)}) %collective-permute-start.19) | collective-permute-done | bytes 221216 | tf_op jit(solution)/shard_map/ppermute | solution.py:26
  50.8 3.2 collective-permute-start.6
  58.5 5.1 %project.1 = (bf16[512,768]{1,0:T(8,128)(2,1)S(1)}, bf16[192,512]{1,0:T(8,128)(2,1)S(1)}, bf16[384,512]{1,0:T(8,128)(2,1)S(1)}, bf16[192,512]{1,0:T(8,128)(2,1)S...) custom-call(s32[2]{0:T(128)S(1)} %pad_add_fusion.refs_0_.where, ...), custom_call_target="tpu_custom_call" | custom-call | flops 1811939328 | bytes 5898240 | tf_op jit(solution)/shard_map/project/pallas_call | solution.py:366
  64.9 18.0 %collective-permute-done.5 = bf16[96,1728]{1,0:T(8,128)(2,1)S(1)} collective-permute-done((bf16[96,1728]{1,0:T(8,128)(2,1)}, bf16[96,1728]{1,0:T(8,128)(2,1)S(1)}, u32[]{:S(2)}, u32[]{:S(2)}) %collective-permute-start.5) | collective-permute-done | bytes 331808 | tf_op jit(solution)/shard_map/ppermute | solution.py:26
  92.9 6.6 %attend.2 = (bf16[64,512]{1,0:T(8,128)(2,1)S(1)}, bf16[64,512]{1,0:T(8,128)(2,1)S(1)}, bf16[64,512]{1,0:T(8,128)(2,1)S(1)}, bf16[64,512]{1,0:T(8,128)(2,1)S(1)}, f32[4,512]{1,0:T(4,128)S(1)}) custom-call(bf16[192,512]{1,0:T(8,128)(2,1)S(1)} %get-tuple-element.82.a0.refs_0_, bf16[192,512]{1,0:T(8,128)(2,1)S(1)} %collective-permute-done.25.a1.refs_1_, ...), custom_call_target="tpu_custom_call" | custom-call | flops 4294967296 | bytes 1048576 | tf_op jit(solution)/shard_map/attend/pallas_call | solution.py:196
  99.5 3.2 collective-permute-done.31.a1.refs_1_
  103.8 5.0 %collective-permute-done.33.a3.refs_3_ = bf16[384,512]{1,0:T(8,128)(2,1)S(1)} collective-permute-done((bf16[384,512]{1,0:T(8,128)(2,1)S(1)}, bf16[384,512]{1,0:T(8,128)(2,1)S(1)}, u32[]{:S(2)}, u32[]{:S(2)}) %collective-permute-start.33) | collective-permute-done | bytes 393248 | tf_op jit(solution)/shard_map/ppermute | solution.py:26
  110.0 12.8 %attend.3 = (bf16[128,512]{1,0:T(8,128)(2,1)S(1)}, bf16[128,512]{1,0:T(8,128)(2,1)S(1)}, bf16[128,512]{1,0:T(8,128)(2,1)S(1)}, bf16[128,512]{1,0:T(8,128)(2,1)S(1)}, f32[8,512]{1,0:T(8,128)S(1)}) custom-call(bf16[384,512]{1,0:T(8,128)(2,1)S(1)} %get-tuple-element.90.a0.refs_0_, bf16[384,512]{1,0:T(8,128)(2,1)S(1)} %collective-permute-done.31.a1.refs_1_, ...), custom_call_target="tpu_custom_call" | custom-call | flops 8589934592 | bytes 2097152 | tf_op jit(solution)/shard_map/attend/pallas_call | solution.py:196
  123.4 3.6 collective-permute-start.35
  131.4 8.4 %collective-permute-done.30.refs_8_ = bf16[64,512]{1,0:T(8,128)(2,1)S(1)} collective-permute-done((bf16[64,512]{1,0:T(8,128)(2,1)S(1)}, bf16[64,512]{1,0:T(8,128)(2,1)S(1)}, u32[]{:S(2)}, u32[]{:S(2)}) %collective-permute-start.30) | collective-permute-done | bytes 65568 | tf_op jit(solution)/shard_map/ppermute | solution.py:26
  142.6 15.2 %collective-permute-done.40.refs_17_ = bf16[2,96,1728]{2,1,0:T(8,128)(2,1)} collective-permute-done((bf16[2,96,1728]{2,1,0:T(8,128)(2,1)S(1)}, bf16[2,96,1728]{2,1,0:T(8,128)(2,1)}, u32[]{:S(2)}, u32[]{:S(2)}) %collective-permute-start.40) | collective-permute-done | bytes 663584 | tf_op jit(solution)/shard_map/ppermute | solution.py:26
  161.4 28.7 %feed.1 = (bf16[512,768]{1,0:T(8,128)(2,1)}, f32[512,768]{1,0:T(8,128)}, bf16[512,768]{1,0:T(8,128)(2,1)}, bf16[512,768]{1,0:T(8,128)(2,1)}, bf16[512,768]{1,0:T...) custom-call(s32[2]{0:T(128)} %copy-done.25, ...), custom_call_target="tpu_custom_call" | custom-call | flops 10871635968 | bytes 17694720 | tf_op jit(solution)/shard_map/feed/pallas_call | solution.py:484
  198.5 10.0 %feed_grads.1 = (bf16[4,4,96,1728]{3,2,1,0:T(8,128)(2,1)}, bf16[4,4,96,1728]{3,2,1,0:T(8,128)(2,1)}) custom-call(s32[2]{0:T(128)S(1)} %copy-done.26, bf16[512,768]{1,0:T(8,128)(2,1)S(1)} %copy-done.49, bf16[512,768]{1,0:T(8,128)(2,1)S(1)} %copy-done.50, bf16[512,768]{1,0:T(8,128)(2,1)S(1)} %copy-done.51, bf16[4,512,768]{2,1,0:T(8,128)(2,1)S(1)} %copy-done.46, ...), custom_call_target="tpu_custom_call" | custom-call | flops 5435817984 | bytes 17694720 | tf_op jit(solution)/shard_map/feed_grads/pallas_call | solution.py:538
  209.0 4.7 %collective-permute-done.66 = bf16[1,128,576]{1,2,0:T(8,128)(2,1)S(1)} collective-permute-done((bf16[1,128,576]{1,2,0:T(8,128)(2,1)S(1)}, bf16[1,128,576]{1,2,0:T(8,128)(2,1)S(1)}, u32[]{:S(2)}, u32[]{:S(2)}) %collective-permute-start.66) | collective-permute-done | bytes 147488 | tf_op jit(solution)/shard_map/ppermute | solution.py:26
  217.1 6.0 %collective-permute-done.67 = bf16[2,128,576]{1,2,0:T(8,128)(2,1)S(1)} collective-permute-done((bf16[2,128,576]{1,2,0:T(8,128)(2,1)S(1)}, bf16[2,128,576]{1,2,0:T(8,128)(2,1)S(1)}, u32[]{:S(2)}, u32[]{:S(2)}) %collective-permute-start.67) | collective-permute-done | bytes 294944 | tf_op jit(solution)/shard_map/ppermute | solution.py:26
  237.5 22.9 %attend_back.3 = (bf16[384,512]{1,0:T(8,128)(2,1)S(1)}, bf16[384,512]{1,0:T(8,128)(2,1)S(1)}, bf16[384,512]{1,0:T(8,128)(2,1)S(1)}, bf16[384,512]{1,0:T(8,128)(2,1)S(1)}) custom-call(bf16[384,512]{1,0:T(8,128)(2,1)S(1)} %copy-done.43, bf16[384,512]{1,0:T(8,128)(2,1)S(1)} %collective-permute-done.31.a1.refs_1_, bf16[384,512]{1,0:T(8,128)(2,1)S(1)} %copy-done.29, ...), custom_call_target="tpu_custom_call" | custom-call | flops 21474836480 | bytes 4194304 | tf_op jit(solution)/shard_map/attend_back/pallas_call | solution.py:270
  263.6 12.2 %attend_back.2 = (bf16[192,512]{1,0:T(8,128)(2,1)S(1)}, bf16[192,512]{1,0:T(8,128)(2,1)S(1)}, bf16[192,512]{1,0:T(8,128)(2,1)S(1)}, bf16[192,512]{1,0:T(8,128)(2,1)S(1)}) custom-call(bf16[192,512]{1,0:T(8,128)(2,1)S(1)} %copy-done.45, bf16[192,512]{1,0:T(8,128)(2,1)S(1)} %copy-done.33, bf16[192,512]{1,0:T(8,128)(2,1)S(1)} %copy-done.35, ...), custom_call_target="tpu_custom_call" | custom-call | flops 10737418240 | bytes 2097152 | tf_op jit(solution)/shard_map/attend_back/pallas_call | solution.py:270
  278.1 5.5 %convert_add_fusion.1 = (f32[1,4,96,1728]{3,2,1,0:T(8,128)}, f32[1,4,96,1728]{3,2,1,0:T(8,128)}, bf16[1,4,96,1728]{3,2,1,0:T(8,128)(2,1)}) fusion(bf16[4,4,96,1728]{3,2,1,0:T(8,128)(2,1)} %collective-permute-done.50, bf16[4,4,96,1728]{3,2,1,0:T(8,128)(2,1)S(1)} %bitcast.207), kind=kLoop, calls=%fused_computation.4 | loop fusion | flops 6635520 | bytes 14598144 | tf_op jit(solution)/shard_map/add | solution.py:153
  285.1 3.7 collective-permute-done.53.refs_7_.refs_3_
  288.8 6.7 %project_back.1 = (bf16[512,768]{1,0:T(8,128)(2,1)}, f32[2,768]{1,0:T(2,128)S(1)}) custom-call(s32[2]{0:T(128)S(1)} %copy-done.26, bf16[512,768]{1,0:T(8,128)(2,1)S(1)} %copy-done.2, f32[3,768]{1,0:T(4,128)S(1)} %pad_maximum_fusion.26.refs_2_, f32[512,768]{1,0:T(8,128)S(1)} %copy-done, bf16[192,512]{1,0:T(8,128)(2,1)S(1)} %get-tuple-element.117.refs_4_.refs_0_, ...), custom_call_target="tpu_custom_call" | custom-call | flops 1811939328 | bytes 5898240 | tf_op jit(solution)/shard_map/project_back/pallas_call | solution.py:622
  308.8 7.4 %collective-permute-start.60 = (bf16[512,768]{1,0:T(8,128)(2,1)}, bf16[512,768]{1,0:T(8,128)(2,1)}, u32[]{:S(2)}, u32[]{:S(2)}) collective-permute-start(bf16[512,768]{1,0:T(8,128)(2,1)} %get-tuple-element.135), channel_id=1, source_target_pairs={{0,0},{1,1},{2,4},{3,5},{4,2},{5,3},{6,6},{7,7},{8,8},{9,9},{10,12... | collective-permute-start | bytes 2359304 | tf_op jit(solution)/shard_map/ppermute | solution.py:26
  322.6 5.5 %project_grads.1 = (bf16[4,4,96,576]{3,2,1,0:T(8,128)(2,1)S(1)}, bf16[4,4,96,576]{3,2,1,0:T(8,128)(2,1)S(1)}) custom-call(s32[2]{0:T(128)S(1)} %copy-done.26, bf16[512,768]{1,0:T(8,128)(2,1)S(1)} %copy-done.41, bf16[192,512]{1,0:T(8,128)(2,1)S(1)} %copy-done.16, bf16[192,512]{1,0:T(8,128)(2,1)S(1)} %copy-done.18, bf16[192,512]{1,0:T(8,128)(2,1)S(1)} %copy-done.20, ...), custom_call_target="tpu_custom_call" | custom-call | flops 1811939328 | bytes 5898240 | tf_op jit(solution)/shard_map/project_grads/pallas_call | solution.py:581
  356.0 22.3 %collective-permute-done.80 = bf16[4,96,1728]{2,1,0:T(8,128)(2,1)S(1)} collective-permute-done((bf16[4,96,1728]{2,1,0:T(8,128)(2,1)}, bf16[4,96,1728]{2,1,0:T(8,128)(2,1)S(1)}, u32[]{:S(2)}, u32[]{:S(2)}) %collective-permute-start.80) | collective-permute-done | bytes 1327136 | tf_op jit(solution)/shard_map/ppermute | solution.py:26
  378.3 3.8 collective-permute-done.78
  382.2 2.9 fusion.67
  391.3 7.9 %collective-permute-done.81 = bf16[96,1728]{1,0:T(8,128)(2,1)S(1)} collective-permute-done((bf16[96,1728]{1,0:T(8,128)(2,1)S(1)}, bf16[96,1728]{1,0:T(8,128)(2,1)S(1)}, u32[]{:S(2)}, u32[]{:S(2)}) %collective-permute-start.81) | collective-permute-done | bytes 331808 | tf_op jit(solution)/shard_map/ppermute | solution.py:26
  399.2 4.6 %collective-permute-done.83 = bf16[96,1728]{1,0:T(8,128)(2,1)S(1)} collective-permute-done((bf16[96,1728]{1,0:T(8,128)(2,1)S(1)}, bf16[96,1728]{1,0:T(8,128)(2,1)S(1)}, u32[]{:S(2)}, u32[]{:S(2)}) %collective-permute-start.83) | collective-permute-done | bytes 331808 | tf_op jit(solution)/shard_map/ppermute | solution.py:26
  403.8 13.6 %collective-permute-done.82 = bf16[96,1728]{1,0:T(8,128)(2,1)S(1)} collective-permute-done((bf16[96,1728]{1,0:T(8,128)(2,1)S(1)}, bf16[96,1728]{1,0:T(8,128)(2,1)S(1)}, u32[]{:S(2)}, u32[]{:S(2)}) %collective-permute-start.82) | collective-permute-done | bytes 331808 | tf_op jit(solution)/shard_map/ppermute | solution.py:26
  424.3 2.7 collective-permute-done.74
  427.8 4.6 %collective-permute-done.75 = bf16[96,576]{1,0:T(8,128)(2,1)S(1)} collective-permute-done((bf16[96,576]{1,0:T(8,128)(2,1)S(1)}, bf16[96,576]{1,0:T(8,128)(2,1)S(1)}, u32[]{:S(2)}, u32[]{:S(2)}) %collective-permute-start.75) | collective-permute-done | bytes 110624 | tf_op jit(solution)/shard_map/ppermute | solution.py:26
  (507 shorter events, 159.2 us)
Async XLA Ops:
  1.7 23.7 %collective-permute-start.1 = (bf16[96,576]{1,0:T(8,128)(2,1)S(1)}, bf16[96,576]{1,0:T(8,128)(2,1)S(1)}, u32[]{:S(2)}, u32[]{:S(2)}) collective-permute-start(bf16[96,576]{1,0:T(8,128)(2,1)S(1)} %pad_maximum_fusion.9), channel_id=1, source_target_pairs={{0,2},{1,3},{2,0},{3,1},{4,6},{5,7},{6,4},{7,5},{8,10},{9,11},{10,... | collective-permute-start | bytes 331784 | tf_op jit(solution)/shard_map/ppermute | solution.py:26
  5.8 19.6 %collective-permute-start = (bf16[96,576]{1,0:T(8,128)(2,1)S(1)}, bf16[96,576]{1,0:T(8,128)(2,1)S(1)}, u32[]{:S(2)}, u32[]{:S(2)}) collective-permute-start(bf16[96,576]{1,0:T(8,128)(2,1)S(1)} %pad_maximum_fusion.9), channel_id=1, source_target_pairs={{0,1},{1,0},{2,3},{3,2},{4,5},{5,4},{6,7},{7,6},{8,9},{9,8},{10,11... | collective-permute-start | bytes 331784 | tf_op jit(solution)/shard_map/ppermute | solution.py:26
  25.6 25.2 %collective-permute-start.20 = (bf16[4,96,576]{2,1,0:T(8,128)(2,1)S(1)}, bf16[4,96,576]{2,1,0:T(8,128)(2,1)S(1)}, u32[]{:S(2)}, u32[]{:S(2)}) collective-permute-start(bf16[4,96,576]{2,1,0:T(8,128)(2,1)S(1)} %pad_maximum_fusion.4.refs_5_.refs_12_), channel_id=1, source_target_pairs={{0,4},{1,5},{2,6},{3,7},{4,0},{5,1},{6,2},{7,3},{8,12},{9,13},{10,... | collective-permute-start | bytes 1327112 | tf_op jit(solution)/shard_map/ppermute | solution.py:26
  28.0 21.7 %collective-permute-start.3 = (bf16[512,768]{1,0:T(8,128)(2,1)}, bf16[512,768]{1,0:T(8,128)(2,1)S(1)}, u32[]{:S(2)}, u32[]{:S(2)}) collective-permute-start(bf16[512,768]{1,0:T(8,128)(2,1)} %param.13), channel_id=1, source_target_pairs={{0,0},{1,1},{2,4},{3,5},{4,2},{5,3},{6,6},{7,7},{8,8},{9,9},{10,12... | collective-permute-start | bytes 2359304 | tf_op jit(solution)/shard_map/ppermute | solution.py:26
  54.0 28.9 %collective-permute-start.5 = (bf16[96,1728]{1,0:T(8,128)(2,1)}, bf16[96,1728]{1,0:T(8,128)(2,1)S(1)}, u32[]{:S(2)}, u32[]{:S(2)}) collective-permute-start(bf16[96,1728]{1,0:T(8,128)(2,1)} %concatenate.144), channel_id=1, source_target_pairs={{0,2},{1,3},{2,0},{3,1},{4,6},{5,7},{6,4},{7,5},{8,10},{9,11},{10,... | collective-permute-start | bytes 995336 | tf_op jit(solution)/shard_map/ppermute | solution.py:26
  54.0 28.9 %collective-permute-start.4 = (bf16[96,1728]{1,0:T(8,128)(2,1)}, bf16[96,1728]{1,0:T(8,128)(2,1)S(1)}, u32[]{:S(2)}, u32[]{:S(2)}) collective-permute-start(bf16[96,1728]{1,0:T(8,128)(2,1)} %concatenate.144), channel_id=1, source_target_pairs={{0,1},{1,0},{2,3},{3,2},{4,5},{5,4},{6,7},{7,6},{8,9},{9,8},{10,11... | collective-permute-start | bytes 995336 | tf_op jit(solution)/shard_map/ppermute | solution.py:26
  55.8 29.6 %collective-permute-start.14 = (bf16[1,768]{1,0:T(2,128)(2,1)S(1)}, bf16[1,768]{1,0:T(2,128)(2,1)S(1)}, u32[]{:S(2)}, u32[]{:S(2)}) collective-permute-start(bf16[1,768]{1,0:T(2,128)(2,1)S(1)} %reshape_squeeze.2), channel_id=1, source_target_pairs={{0,1},{1,0},{2,3},{3,2},{4,5},{5,4},{6,7},{7,6},{8,9},{9,8},{10,11... | collective-permute-start | bytes 4616 | tf_op jit(solution)/shard_map/ppermute | solution.py:26
  63.7 27.0 %collective-permute-start.25 = (bf16[192,512]{1,0:T(8,128)(2,1)S(1)}, bf16[192,512]{1,0:T(8,128)(2,1)S(1)}, u32[]{:S(2)}, u32[]{:S(2)}) collective-permute-start(bf16[192,512]{1,0:T(8,128)(2,1)S(1)} %get-tuple-element.83), channel_id=1, source_target_pairs={{0,1},{1,0},{2,3},{3,2},{4,5},{5,4},{6,7},{7,6},{8,9},{9,8},{10,11... | collective-permute-start | bytes 589832 | tf_op jit(solution)/shard_map/ppermute | solution.py:26
  64.9 26.9 %collective-permute-start.26 = (bf16[192,512]{1,0:T(8,128)(2,1)S(1)}, bf16[192,512]{1,0:T(8,128)(2,1)S(1)}, u32[]{:S(2)}, u32[]{:S(2)}) collective-permute-start(bf16[192,512]{1,0:T(8,128)(2,1)S(1)} %get-tuple-element.84), channel_id=1, source_target_pairs={{0,4},{1,5},{2,6},{3,7},{4,0},{5,1},{6,2},{7,3},{8,12},{9,13},{10,... | collective-permute-start | bytes 589832 | tf_op jit(solution)/shard_map/ppermute | solution.py:26
  84.2 42.9 %collective-permute-start.38 = (bf16[4,96,1728]{2,1,0:T(8,128)(2,1)}, bf16[4,96,1728]{2,1,0:T(8,128)(2,1)}, u32[]{:S(2)}, u32[]{:S(2)}) collective-permute-start(bf16[4,96,1728]{2,1,0:T(8,128)(2,1)} %pad_maximum_fusion.refs_13_), channel_id=1, source_target_pairs={{0,16},{1,17},{2,18},{3,19},{4,20},{5,21},{6,22},{7,23},{8,24},{9,... | collective-permute-start | bytes 3981320 | tf_op jit(solution)/shard_map/ppermute | solution.py:26
  90.0 37.5 %collective-permute-start.37 = (bf16[4,96,1728]{2,1,0:T(8,128)(2,1)}, bf16[4,96,1728]{2,1,0:T(8,128)(2,1)}, u32[]{:S(2)}, u32[]{:S(2)}) collective-permute-start(bf16[4,96,1728]{2,1,0:T(8,128)(2,1)} %pad_maximum_fusion.refs_13_), channel_id=1, source_target_pairs={{0,8},{1,9},{2,10},{3,11},{4,12},{5,13},{6,14},{7,15},{8,0},{9,1},... | collective-permute-start | bytes 3981320 | tf_op jit(solution)/shard_map/ppermute | solution.py:26
  102.8 20.0 %collective-permute-start.28 = (bf16[64,512]{1,0:T(8,128)(2,1)S(1)}, bf16[64,512]{1,0:T(8,128)(2,1)S(1)}, u32[]{:S(2)}, u32[]{:S(2)}) collective-permute-start(bf16[64,512]{1,0:T(8,128)(2,1)S(1)} %get-tuple-element.87), channel_id=1, source_target_pairs={{0,1},{1,0},{2,3},{3,2},{4,5},{5,4},{6,7},{7,6},{8,9},{9,8},{10,11... | collective-permute-start | bytes 196616 | tf_op jit(solution)/shard_map/ppermute | solution.py:26
  103.8 19.5 %collective-permute-start.29 = (bf16[64,512]{1,0:T(8,128)(2,1)S(1)}, bf16[64,512]{1,0:T(8,128)(2,1)S(1)}, u32[]{:S(2)}, u32[]{:S(2)}) collective-permute-start(bf16[64,512]{1,0:T(8,128)(2,1)S(1)} %get-tuple-element.88), channel_id=1, source_target_pairs={{0,4},{1,5},{2,6},{3,7},{4,0},{5,1},{6,2},{7,3},{8,12},{9,13},{10,... | collective-permute-start | bytes 196616 | tf_op jit(solution)/shard_map/ppermute | solution.py:26
  108.8 33.3 %collective-permute-start.7 = (bf16[512,768]{1,0:T(8,128)(2,1)S(1)}, bf16[512,768]{1,0:T(8,128)(2,1)S(1)}, u32[]{:S(2)}, u32[]{:S(2)}) collective-permute-start(bf16[512,768]{1,0:T(8,128)(2,1)S(1)} %copy-done.95), channel_id=1, source_target_pairs={{0,0},{1,1},{2,4},{3,5},{4,2},{5,3},{6,6},{7,7},{8,8},{9,9},{10,12... | collective-permute-start | bytes 2359304 | tf_op jit(solution)/shard_map/ppermute | solution.py:26
  139.8 20.6 %collective-permute-start.41 = (bf16[4,96,1728]{2,1,0:T(8,128)(2,1)}, bf16[4,96,1728]{2,1,0:T(8,128)(2,1)}, u32[]{:S(2)}, u32[]{:S(2)}) collective-permute-start(bf16[4,96,1728]{2,1,0:T(8,128)(2,1)} %pad_maximum_fusion.refs_13_), channel_id=1, source_target_pairs={{0,4},{1,5},{2,6},{3,7},{4,0},{5,1},{6,2},{7,3},{8,12},{9,13},{10,... | collective-permute-start | bytes 3981320 | tf_op jit(solution)/shard_map/ppermute | solution.py:26
  142.1 18.3 %collective-permute-start.43 = (bf16[4,96,1728]{2,1,0:T(8,128)(2,1)}, bf16[4,96,1728]{2,1,0:T(8,128)(2,1)}, u32[]{:S(2)}, u32[]{:S(2)}) collective-permute-start(bf16[4,96,1728]{2,1,0:T(8,128)(2,1)} %collective-permute-done.38.refs_15_), channel_id=1, source_target_pairs={{0,4},{1,5},{2,6},{3,7},{4,0},{5,1},{6,2},{7,3},{8,12},{9,13},{10,... | collective-permute-start | bytes 3981320 | tf_op jit(solution)/shard_map/ppermute | solution.py:26
  142.1 19.3 %collective-permute-start.42 = (bf16[4,96,1728]{2,1,0:T(8,128)(2,1)}, bf16[4,96,1728]{2,1,0:T(8,128)(2,1)}, u32[]{:S(2)}, u32[]{:S(2)}) collective-permute-start(bf16[4,96,1728]{2,1,0:T(8,128)(2,1)} %collective-permute-done.37.refs_14_), channel_id=1, source_target_pairs={{0,4},{1,5},{2,6},{3,7},{4,0},{5,1},{6,2},{7,3},{8,12},{9,13},{10,... | collective-permute-start | bytes 3981320 | tf_op jit(solution)/shard_map/ppermute | solution.py:26
  208.5 55.1 %collective-permute-start.50 = (bf16[4,4,96,1728]{3,2,1,0:T(8,128)(2,1)}, bf16[4,4,96,1728]{3,2,1,0:T(8,128)(2,1)}, u32[]{:S(2)}, u32[]{:S(2)}) collective-permute-start(bf16[4,4,96,1728]{3,2,1,0:T(8,128)(2,1)} %get-tuple-element.111), channel_id=1, source_target_pairs={{0,4},{1,5},{2,6},{3,7},{4,0},{5,1},{6,2},{7,3},{8,12},{9,13},{10,... | collective-permute-start | bytes 15925256 | tf_op jit(solution)/shard_map/ppermute | solution.py:26
  230.7 32.0 %collective-permute-start.49 = (bf16[512,768]{1,0:T(8,128)(2,1)}, bf16[512,768]{1,0:T(8,128)(2,1)S(1)}, u32[]{:S(2)}, u32[]{:S(2)}) collective-permute-start(bf16[512,768]{1,0:T(8,128)(2,1)} %get-tuple-element.103), channel_id=1, source_target_pairs={{0,0},{1,1},{2,4},{3,5},{4,2},{5,3},{6,6},{7,7},{8,8},{9,9},{10,12... | collective-permute-start | bytes 2359304 | tf_op jit(solution)/shard_map/ppermute | solution.py:26
  261.1 22.5 %collective-permute-start.58 = (bf16[384,512]{1,0:T(8,128)(2,1)S(1)}, bf16[384,512]{1,0:T(8,128)(2,1)S(1)}, u32[]{:S(2)}, u32[]{:S(2)}) collective-permute-start(bf16[384,512]{1,0:T(8,128)(2,1)S(1)} %get-tuple-element.133), channel_id=1, source_target_pairs={{0,4},{1,5},{2,6},{3,7},{4,0},{5,1},{6,2},{7,3},{8,12},{9,13},{10,... | collective-permute-start | bytes 1179656 | tf_op jit(solution)/shard_map/ppermute | solution.py:26
  262.3 22.0 %collective-permute-start.59 = (bf16[384,512]{1,0:T(8,128)(2,1)S(1)}, bf16[384,512]{1,0:T(8,128)(2,1)S(1)}, u32[]{:S(2)}, u32[]{:S(2)}) collective-permute-start(bf16[384,512]{1,0:T(8,128)(2,1)S(1)} %get-tuple-element.134), channel_id=1, source_target_pairs={{0,5},{1,4},{2,7},{3,6},{4,1},{5,0},{6,3},{7,2},{8,13},{9,12},{10,... | collective-permute-start | bytes 1179656 | tf_op jit(solution)/shard_map/ppermute | solution.py:26
  283.6 56.9 %collective-permute-start.68 = (bf16[4,128,576]{1,2,0:T(8,128)(2,1)}, bf16[4,128,576]{1,2,0:T(8,128)(2,1)}, u32[]{:S(2)}, u32[]{:S(2)}) collective-permute-start(bf16[4,128,576]{1,2,0:T(8,128)(2,1)} %pad_maximum_fusion.3), channel_id=1, source_target_pairs={{0,16},{1,17},{2,18},{3,19},{4,20},{5,21},{6,22},{7,23},{8,24},{9,... | collective-permute-start | bytes 1769480 | tf_op jit(solution)/shard_map/ppermute | solution.py:26
  306.7 39.6 %collective-permute-start.77 = (bf16[2,96,1728]{2,1,0:T(8,128)(2,1)}, bf16[2,96,1728]{2,1,0:T(8,128)(2,1)}, u32[]{:S(2)}, u32[]{:S(2)}) collective-permute-start(bf16[2,96,1728]{2,1,0:T(8,128)(2,1)} %get-tuple-element.189), channel_id=1, source_target_pairs={{0,16},{1,17},{2,18},{3,19},{4,20},{5,21},{6,22},{7,23},{8,24},{9,... | collective-permute-start | bytes 1990664 | tf_op jit(solution)/shard_map/ppermute | solution.py:26
  307.6 35.0 %collective-permute-start.79 = (bf16[2,96,1728]{2,1,0:T(8,128)(2,1)}, bf16[2,96,1728]{2,1,0:T(8,128)(2,1)}, u32[]{:S(2)}, u32[]{:S(2)}) collective-permute-start(bf16[2,96,1728]{2,1,0:T(8,128)(2,1)} %get-tuple-element.190), channel_id=1, source_target_pairs={{0,8},{1,9},{2,10},{3,11},{4,12},{5,13},{6,14},{7,15},{8,0},{9,1},... | collective-permute-start | bytes 1990664 | tf_op jit(solution)/shard_map/ppermute | solution.py:26
  308.8 43.6 %collective-permute-start.60 = (bf16[512,768]{1,0:T(8,128)(2,1)}, bf16[512,768]{1,0:T(8,128)(2,1)}, u32[]{:S(2)}, u32[]{:S(2)}) collective-permute-start(bf16[512,768]{1,0:T(8,128)(2,1)} %get-tuple-element.135), channel_id=1, source_target_pairs={{0,0},{1,1},{2,4},{3,5},{4,2},{5,3},{6,6},{7,7},{8,8},{9,9},{10,12... | collective-permute-start | bytes 2359304 | tf_op jit(solution)/shard_map/ppermute | solution.py:26
  345.2 33.2 %collective-permute-start.80 = (bf16[4,96,1728]{2,1,0:T(8,128)(2,1)}, bf16[4,96,1728]{2,1,0:T(8,128)(2,1)S(1)}, u32[]{:S(2)}, u32[]{:S(2)}) collective-permute-start(bf16[4,96,1728]{2,1,0:T(8,128)(2,1)} %pad_maximum_fusion.2), channel_id=1, source_target_pairs={{0,16},{1,17},{2,18},{3,19},{4,20},{5,21},{6,22},{7,23},{8,24},{9,... | collective-permute-start | bytes 3981320 | tf_op jit(solution)/shard_map/ppermute | solution.py:26
  348.8 33.3 %collective-permute-start.78 = (bf16[4,96,1728]{2,1,0:T(8,128)(2,1)}, bf16[4,96,1728]{2,1,0:T(8,128)(2,1)}, u32[]{:S(2)}, u32[]{:S(2)}) collective-permute-start(bf16[4,96,1728]{2,1,0:T(8,128)(2,1)} %pad_maximum_fusion.1), channel_id=1, source_target_pairs={{0,8},{1,9},{2,10},{3,11},{4,12},{5,13},{6,14},{7,15},{8,0},{9,1},... | collective-permute-start | bytes 3981320 | tf_op jit(solution)/shard_map/ppermute | solution.py:26
  354.1 35.7 %collective-permute-start.70 = (bf16[2,96,576]{2,1,0:T(8,128)(2,1)S(1)}, bf16[2,96,576]{2,1,0:T(8,128)(2,1)S(1)}, u32[]{:S(2)}, u32[]{:S(2)}) collective-permute-start(bf16[2,96,576]{2,1,0:T(8,128)(2,1)S(1)} %get-tuple-element.196), channel_id=1, source_target_pairs={{0,16},{1,17},{2,18},{3,19},{4,20},{5,21},{6,22},{7,23},{8,24},{9,... | collective-permute-start | bytes 663560 | tf_op jit(solution)/shard_map/ppermute | solution.py:26
  355.2 33.5 %collective-permute-start.72 = (bf16[2,96,576]{2,1,0:T(8,128)(2,1)S(1)}, bf16[2,96,576]{2,1,0:T(8,128)(2,1)S(1)}, u32[]{:S(2)}, u32[]{:S(2)}) collective-permute-start(bf16[2,96,576]{2,1,0:T(8,128)(2,1)S(1)} %get-tuple-element.197), channel_id=1, source_target_pairs={{0,8},{1,9},{2,10},{3,11},{4,12},{5,13},{6,14},{7,15},{8,0},{9,1},... | collective-permute-start | bytes 663560 | tf_op jit(solution)/shard_map/ppermute | solution.py:26
  387.3 30.1 %collective-permute-start.82 = (bf16[96,1728]{1,0:T(8,128)(2,1)S(1)}, bf16[96,1728]{1,0:T(8,128)(2,1)S(1)}, u32[]{:S(2)}, u32[]{:S(2)}) collective-permute-start(bf16[96,1728]{1,0:T(8,128)(2,1)S(1)} %get-tuple-element.188), channel_id=1, source_target_pairs={{0,2},{1,3},{2,0},{3,1},{4,6},{5,7},{6,4},{7,5},{8,10},{9,11},{10,... | collective-permute-start | bytes 995336 | tf_op jit(solution)/shard_map/ppermute | solution.py:26
  388.8 29.8 %collective-permute-start.73 = (bf16[4,96,576]{2,1,0:T(8,128)(2,1)S(1)}, bf16[4,96,576]{2,1,0:T(8,128)(2,1)S(1)}, u32[]{:S(2)}, u32[]{:S(2)}) collective-permute-start(bf16[4,96,576]{2,1,0:T(8,128)(2,1)S(1)} %pad_maximum_fusion.6), channel_id=1, source_target_pairs={{0,16},{1,17},{2,18},{3,19},{4,20},{5,21},{6,22},{7,23},{8,24},{9,... | collective-permute-start | bytes 1327112 | tf_op jit(solution)/shard_map/ppermute | solution.py:26
  390.0 28.6 %collective-permute-start.71 = (bf16[4,96,576]{2,1,0:T(8,128)(2,1)S(1)}, bf16[4,96,576]{2,1,0:T(8,128)(2,1)S(1)}, u32[]{:S(2)}, u32[]{:S(2)}) collective-permute-start(bf16[4,96,576]{2,1,0:T(8,128)(2,1)S(1)} %pad_maximum_fusion.5), channel_id=1, source_target_pairs={{0,8},{1,9},{2,10},{3,11},{4,12},{5,13},{6,14},{7,15},{8,0},{9,1},... | collective-permute-start | bytes 1327112 | tf_op jit(solution)/shard_map/ppermute | solution.py:26
  (158 other events, 1815.8 us)

commit v3 on v2

--- a/solution.py
+++ b/solution.py
@@ -59,40 +59,50 @@
 
 def gather_dp(array, dp_size):
     blocks = array[None]
-    mask = 1
+    mask = 2
     while mask < dp_size:
         blocks = jnp.concatenate([blocks, swap_dp(blocks, dp_size, mask)])
         mask *= 2
-    return blocks
-
-
-PIECES = (
-    (0, 0),
-    (2, 0),
-    (4, 0),
-    (6, 0),
-    (6, 2),
-    (1, 0),
-    (3, 0),
-    (5, 0),
-    (7, 0),
-    (7, 2),
-)
+    blocks = jnp.stack([blocks, swap_dp(blocks, dp_size, 1)], axis=1)
+    return blocks.reshape(dp_size, *array.shape)
+
+
+WHOLE = ((0, 0), (2, 0), (4, 0), (6, 0), (1, 0), (3, 0), (5, 0), (7, 0))
+HALVES = WHOLE[:4] + ((6, 2),) + WHOLE[4:] + ((7, 2),)
 
 
 def stack_planes(shard, dp_size):
     return jnp.stack([shard] + [swap_z(shard, dp_size, t) for t in range(1, GROUP)])
 
 
-def gather_weights(own, dp_size):
+def gather_weights(own, dp_size, way):
     if dp_size != 8:
         return (lax.all_gather(own, "dp", axis=1, tiled=True),)
     x = swap_dp(own, dp_size, 2)
     y = swap_dp(own, dp_size, 4)
-    d0 = swap_dp(x[:2], dp_size, 4)
-    d1 = swap_dp(y[2:], dp_size, 2)
-    near = (own, x, y, d0, d1)
+    if way == 2:
+        near = (own, x, y, swap_dp(x, dp_size, 4))
+    elif way == 4:
+        near = (own, x, y, swap_dp(y, dp_size, 2))
+    else:
+        near = (own, x, y, swap_dp(x[:2], dp_size, 4), swap_dp(y[2:], dp_size, 2))
     return near + tuple(swap_dp(piece, dp_size, 1) for piece in near)
+
+
+def load_gathered(gathered, full, sems):
+    if len(gathered.shape) == 3:
+        copies = [pltpu.make_async_copy(gathered, full, sems.at[0])]
+    else:
+        count, _, rows, _ = gathered.shape
+        copies = [
+            pltpu.make_async_copy(
+                gathered.at[i], full.at[:, i * rows : (i + 1) * rows], sems.at[i]
+            )
+            for i in range(count)
+        ]
+    for copy in copies:
+        copy.start()
+    return copies
 
 
 def load_weights(me, pieces, full, sems):
@@ -100,7 +110,9 @@
         copies = [pltpu.make_async_copy(pieces[0], full, sems.at[0])]
     else:
         copies = []
-        for i, (piece, (rel, first)) in enumerate(zip(pieces, PIECES)):
+        for i, (piece, (rel, first)) in enumerate(
+            zip(pieces, HALVES if len(pieces) == len(HALVES) else WHOLE)
+        ):
             count, rows = piece.shape[:2]
             start = pl.multiple_of((me ^ rel) * rows, rows)
             place = full.at[first : first + count, pl.ds(start, rows)]
@@ -138,25 +150,32 @@
     return swap_dp(parts[1], dp_size, 1) if dp_size == 8 else None
 
 
-def reduce_first(parts, far, dp_size):
+def reduce_diagonal(parts, far, dp_size):
+    return plus(parts[0][3], far[3]) if dp_size == 8 else None
+
+
+def reduce_first(diagonal, dp_size):
     if dp_size != 8:
         return None
-    diagonal = plus(parts[0][3], far[3])
     return swap_dp(diagonal[:2], dp_size, 2), swap_dp(diagonal[2:], dp_size, 4)
 
 
-def reduce_second(parts, far, half, dp_size):
+def reduce_sides(parts, far, half, dp_size):
     if dp_size != 8:
-        total = lax.psum_scatter(parts[0], "dp", scatter_dimension=1, tiled=True)
-        return total.astype(f32)
-    near = parts[0]
-    x = near[1].astype(f32) + far[1].astype(f32)
-    y = near[2].astype(f32) + far[2].astype(f32)
+        return None
+    x = parts[0][1].astype(f32) + far[1].astype(f32)
+    y = parts[0][2].astype(f32) + far[2].astype(f32)
     x = jnp.concatenate([x[:2], x[2:] + half[1].astype(f32)]).astype(bf16)
     y = jnp.concatenate([y[:2] + half[0].astype(f32), y[2:]]).astype(bf16)
-    from_x = swap_dp(x, dp_size, 2)
-    from_y = swap_dp(y, dp_size, 4)
-    own = near[0].astype(f32) + far[0].astype(f32)
+    return x, y
+
+
+def reduce_second(parts, far, sides, dp_size):
+    if dp_size != 8:
+        return lax.psum_scatter(parts[0], "dp", scatter_dimension=1, tiled=True).astype(f32)
+    from_x = swap_dp(sides[0], dp_size, 2)
+    from_y = swap_dp(sides[1], dp_size, 4)
+    own = parts[0][0].astype(f32) + far[0].astype(f32)
     return own + from_x.astype(f32) + from_y.astype(f32)
 
 
@@ -215,7 +234,7 @@
     return outs, lse
 
 
-def attend_back_kernel(*refs):
+def attend_back_kernel(first_head, *refs):
     pieces, grads = refs[0:4], refs[4:8]
     lse, cosine, sine = refs[8:11]
     outs = refs[11:15]
@@ -223,7 +242,8 @@
     block = pieces[0].shape[1]
     rows = min(256, block)
     half = HEAD_DIM // 2
-    for h in range(grads[0].shape[0] // HEAD_DIM):
+    for h in range(pieces[0].shape[0] // (3 * HEAD_DIM)):
+        of_grad = slice((first_head + h) * HEAD_DIM, (first_head + h + 1) * HEAD_DIM)
         at = 3 * HEAD_DIM * h
         for i, piece in enumerate(pieces):
             columns = slice(i * block, (i + 1) * block)
@@ -235,7 +255,7 @@
             for c in range(block // rows):
                 own = slice(c * rows, (c + 1) * rows)
                 query_t = piece[at : at + HEAD_DIM, own] * bf16(HEAD_DIM**-0.5)
-                grad_t = grad[h * HEAD_DIM : (h + 1) * HEAD_DIM, own]
+                grad_t = grad[of_grad, own]
                 scores = jnp.dot(query_t.T, key_t[...], preferred_element_type=f32)
                 weights = jnp.exp(scores - log_total[own])
                 pull = jnp.dot(grad_t.T, value_t[...], preferred_element_type=f32)
@@ -262,13 +282,13 @@
             out[at + 2 * HEAD_DIM : at + 3 * HEAD_DIM] = value_grad[:, columns].astype(bf16)
 
 
-def attend_back(pieces, grads, lse, cosine, sine):
+def attend_back(pieces, grads, first_head, lse, cosine, sine):
     block = pieces[0].shape[1]
     heads = pieces[0].shape[0] // (3 * HEAD_DIM)
     length = GROUP * block
     vmem = pl.BlockSpec(memory_space=pltpu.VMEM)
     return pl.pallas_call(
-        attend_back_kernel,
+        functools.partial(attend_back_kernel, first_head),
         out_shape=[jax.ShapeDtypeStruct((heads * 3 * HEAD_DIM, block), bf16)] * GROUP,
         in_specs=[vmem] * 11,
         out_specs=[vmem] * GROUP,
@@ -324,7 +344,7 @@
 
 
 def parts_of(heads):
-    return (range(0, 1), range(1, heads)) if heads > 1 else (range(0, 1),)
+    return tuple(range(h, h + 1) for h in range(heads))
 
 
 def project_kernel(count, heads, *refs):
@@ -388,23 +408,23 @@
 GELU_B = 0.044715
 
 
-def feed_kernel(count, heads, *refs):
+def feed_kernel(heads, *refs):
     where, tokens, upstream, vectors, bias_up = refs[:5]
     parts = parts_of(heads)
     used = GROUP * len(parts)
     mixtures, refs = refs[5 : 5 + used], refs[5 + used :]
-    pieces, refs = refs[:count], refs[count:]
+    gathered, refs = refs[0], refs[1:]
     output, residual_grad, out_hidden, out_branch_one, out_branch_two = refs[:5]
     activated, pre_grad, attention, sums, bias_sums = refs[5:10]
-    mixture_grads = refs[10 : 10 + used]
-    full, slope, keep_one, keep_two, sems = refs[10 + used :]
-    me, base = where[0], where[1]
+    mixture_grads = refs[10 : 10 + GROUP]
+    full, slope, keep_one, keep_two, sems = refs[10 + GROUP :]
+    me, own_block = where[0], where[1]
     wide = heads * HEAD_DIM
     hidden = bias_up.shape[1]
     of_out = slice(0, wide)
     of_up = slice(wide, wide + hidden)
     of_down = slice(wide + hidden, wide + 2 * hidden)
-    copies = load_weights(me, pieces, full, sems)
+    copies = load_gathered(gathered, full, sems)
     gain, scale, shift = vectors[0:1], vectors[1:2], vectors[2:3]
     gate_one, gate_two, bias_down = vectors[3:4], vectors[4:5], vectors[5:6]
     for r in range(GROUP):
@@ -412,9 +432,9 @@
         attention[r] = own.T
     for copy in copies:
         copy.wait()
-    branch_one = dot_nt(attention[0], full[base, :, of_out])
+    branch_one = dot_nt(attention[0], full[own_block, :, of_out])
     for r in range(1, GROUP):
-        branch_one = branch_one + dot_nt(attention[r], full[base ^ r, :, of_out])
+        branch_one = branch_one + dot_nt(attention[r], full[own_block ^ r, :, of_out])
     keep_one[...] = branch_one
     residual = tokens[...].astype(f32) + gate_one * branch_one
     normed, _ = normalize(residual)
@@ -464,17 +484,15 @@
     sums[3:4] = total(grad * keep_one[...])
     out_branch_one[...] = (gate_one * grad).astype(bf16)
     for r in range(GROUP):
-        back = dot(out_branch_one[...], full[base ^ r, :, of_out]).astype(bf16).T
-        for n, part in enumerate(parts):
-            own = slice(part[0] * HEAD_DIM, (part[-1] + 1) * HEAD_DIM)
-            mixture_grads[n * GROUP + r][...] = back[own]
-
-
-def feed(where, tokens, upstream, vectors, bias_up, mixtures, pieces, heads):
+        back = dot(out_branch_one[...], full[own_block ^ r, :, of_out])
+        mixture_grads[r][...] = back.astype(bf16).T
+
+
+def feed(where, tokens, upstream, vectors, bias_up, mixtures, gathered, heads):
     rows, width = tokens.shape
     wide = heads * HEAD_DIM
     hidden = bias_up.shape[1]
-    columns = pieces[0].shape[2]
+    columns = gathered.shape[-1]
     parts = parts_of(heads)
     count = GROUP * len(parts)
 
@@ -482,7 +500,7 @@
         return jax.ShapeDtypeStruct(lengths, dtype)
 
     outs = pl.pallas_call(
-        functools.partial(feed_kernel, len(pieces), heads),
+        functools.partial(feed_kernel, heads),
         out_shape=[
             shape(bf16, rows, width),
             shape(f32, rows, width),
@@ -495,15 +513,15 @@
             shape(f32, 5, width),
             shape(f32, GROUP, hidden),
         ]
-        + [shape(bf16, len(part) * HEAD_DIM, rows) for part in parts for _ in range(GROUP)],
-        in_specs=[SMEM] + [VMEM] * (4 + count) + [ANY] * len(pieces),
-        out_specs=[VMEM] * (10 + count),
+        + [shape(bf16, wide, rows)] * GROUP,
+        in_specs=[SMEM] + [VMEM] * (4 + count) + [ANY],
+        out_specs=[VMEM] * (10 + GROUP),
         scratch_shapes=[
             pltpu.VMEM((GROUP, width, columns), bf16),
             pltpu.VMEM((GROUP, rows, hidden), f32),
             pltpu.VMEM((rows, width), f32),
             pltpu.VMEM((rows, width), f32),
-            pltpu.SemaphoreType.DMA((len(pieces),)),
+            pltpu.SemaphoreType.DMA((gathered.shape[0],)),
         ],
         compiler_params=pltpu.CompilerParams(vmem_limit_bytes=56 << 20),
         cost_estimate=pl.CostEstimate(
@@ -512,38 +530,42 @@
             transcendentals=GROUP * rows * hidden,
         ),
         name="feed",
-    )(where, tokens, upstream, vectors, bias_up, *sum(mixtures, []), *pieces)
-    grads = outs[10:]
-    return outs[:10], [grads[n * GROUP : (n + 1) * GROUP] for n in range(len(parts))]
-
-
-def feed_grads_kernel(where, hidden, branch_one, branch_two, act, pre, attention, *outs):
-    me, base = where[0], where[1]
+    )(where, tokens, upstream, vectors, bias_up, *sum(mixtures, []), gathered)
+    return outs[:10], outs[10:]
+
+
+def feed_grads_kernel(where, hidden, branch_one, branch_two, act, pre, attention, out):
+    own_block = where[1]
     t = pl.program_id(0)
     up = dot(hidden[...].T, pre[0]).astype(bf16)
     down = dot(branch_two[...].T, act[0]).astype(bf16)
-    own = dot(branch_one[...].T, attention[base ^ t]).astype(bf16)
-    store_blocks(me, outs, 0, jnp.concatenate([own, up, down], axis=1))
+    own = dot(branch_one[...].T, attention[own_block ^ t]).astype(bf16)
+    value = jnp.concatenate([own, up, down], axis=1)
+    if len(out.shape) == 3:
+        out[0] = value
+    else:
+        out[...] = value.reshape(out.shape)
 
 
 def feed_grads(dp_size, where, hidden, branch_one, branch_two, act, pre, attention):
     rows, width = hidden.shape
     wide, inner = attention.shape[2], act.shape[2]
     columns = wide + 2 * inner
-    shapes = grad_shapes(dp_size, width, columns)
     if dp_size == 8:
-        out_spec = pl.BlockSpec((4, 1, width // 8, columns), lambda t: (0, t, 0, 0))
+        shape = (dp_size, GROUP, width // dp_size, columns)
+        out_spec = pl.BlockSpec((dp_size, 1, width // dp_size, columns), lambda t: (0, t, 0, 0))
     else:
+        shape = (GROUP, width, columns)
         out_spec = pl.BlockSpec((1, width, columns), lambda t: (t, 0, 0))
     return pl.pallas_call(
         feed_grads_kernel,
-        out_shape=shapes,
+        out_shape=jax.ShapeDtypeStruct(shape, bf16),
         grid=(GROUP,),
         in_specs=[SMEM]
         + [VMEM] * 3
         + [pl.BlockSpec((1, rows, inner), lambda t: (t, 0, 0))] * 2
         + [VMEM],
-        out_specs=[out_spec] * len(shapes),
+        out_specs=out_spec,
         compiler_params=pltpu.CompilerParams(vmem_limit_bytes=40 << 20),
         cost_estimate=pl.CostEstimate(
             flops=2 * rows * width * GROUP * columns,
@@ -666,6 +688,7 @@
     position = me % 2 * 2 + z % 2
     base = z ^ position
     where = jnp.stack([me, base]).astype(jnp.int32)
+    where_whole = jnp.stack([me, position]).astype(jnp.int32)
     rows, width = tokens.shape
     heads = qkv_weight.shape[2] // HEAD_DIM
     wide = heads * HEAD_DIM
@@ -673,38 +696,46 @@
     cond = time_embed.shape[1]
     per = norm1_gain.shape[0]
 
+    columns = ada_weight.shape[1]
+    small = jnp.concatenate([time_embed[0], norm1_gain, norm2_gain, down_bias, up_bias])
+    lines = -(-small.shape[0] // columns)
+    small = jnp.pad(small, (0, lines * columns - small.shape[0])).reshape(lines, columns)
+    pack = jnp.concatenate([ada_weight, ada_bias[None], small])
+    pack = jnp.pad(pack, ((0, -pack.shape[0] % 16), (0, 0)))
+    pack = gather_dp(pack, dp_size)
+    ada_full = pack[:, :cond]
+
     first_own = stack_planes(jnp.concatenate([*qkv_weight], axis=1), dp_size)
-    first_pieces = gather_weights(first_own, dp_size)
+    first_pieces = gather_weights(first_own, dp_size, 0)
     moved = regroup(tie(tokens, first_own), dp_size)
     second_shard = jnp.concatenate([out_weight.T, up_weight, down_weight.T], axis=1)
-    second_own = stack_planes(tie(second_shard, moved), dp_size)
-    second_pieces = gather_weights(second_own, dp_size)
-    upstream = regroup(tie(out_grad, second_own), dp_size)
-
-    lanes = max(per, cond, up_bias.shape[0])
-
-    def fit(row):
-        return jnp.pad(row, (0, lanes - row.shape[0]))
-
-    small = jnp.stack(
-        [fit(time_embed[0]), fit(norm1_gain), fit(norm2_gain), fit(down_bias), fit(up_bias)]
-    )
-    small = reorder(gather_dp(small, dp_size), me)
-    embeds = small[:, 0, :cond]
-    slices = einsum("sc,ce->se", embeds, ada_weight) + ada_bias.astype(f32)
-    slices = gather_dp(slices, dp_size)
+    if dp_size == 8:
+        gathered = lax.all_gather(second_shard, AXES, axis=0, tiled=False)
+        gathered = gathered.reshape(dp_size, GROUP, *second_shard.shape)
+    else:
+        gathered = lax.all_gather(second_shard, "tensor", axis=0, tiled=False)
+        gathered = lax.all_gather(gathered, "dp", axis=1, tiled=True)
+    upstream = regroup(tie(out_grad, moved), dp_size)
+
+    small = reorder(pack[:, cond + 1 : cond + 1 + lines], me).reshape(dp_size, lines * columns)
+    embeds = small[:, :cond]
     sequence = me // 2 * 2 + z // 2
-    modulation = reorder(lax.dynamic_index_in_dim(slices, sequence, 1), me).reshape(6, 1, width)
+    embed = lax.dynamic_slice_in_dim(embeds, sequence, 1)
+    modulation = einsum("sc,oce->soe", embed, ada_full)[0] + pack[:, cond].astype(f32)
+    modulation = reorder(modulation, me).reshape(6, 1, width)
     shift_one, scale_one, gate_one, shift_two, scale_two, gate_two = modulation
-    gain_one = small[:, 1, :per].reshape(1, width).astype(f32)
-    gain_two = small[:, 2, :per].reshape(1, width).astype(f32)
-    bias_down = small[:, 3, :per].reshape(1, width).astype(f32)
-    bias_up = tie(small[:, 4, : up_bias.shape[0]].reshape(1, hidden), moved)
+
+    def vector(n):
+        return small[:, cond + n * per : cond + (n + 1) * per].reshape(1, width).astype(f32)
+
+    gain_one, gain_two, bias_down = vector(0), vector(1), vector(2)
+    bias_up = small[:, cond + 3 * per : cond + 3 * per + up_bias.shape[0]].reshape(1, hidden)
+    bias_up = tie(bias_up, moved)
     bias_up = jnp.concatenate([bias_up, swap_z(bias_up, dp_size, 1)])
     bias_up = jnp.concatenate([bias_up, swap_z(bias_up, dp_size, 2)]).astype(f32)
+    bias_up = reorder(bias_up, z)
     vectors_one = jnp.concatenate([gain_one, scale_one, shift_one])
     vectors_two = jnp.concatenate([gain_two, scale_two, shift_two, gate_one, gate_two, bias_down])
-    ada_full = gather_dp(tie(ada_weight, second_pieces[1:3]), dp_size)
 
     frequency = jnp.exp(
         jnp.arange(HALF, dtype=f32) * (-2.0 * math.log(ROPE_BASE) / HEAD_DIM)
@@ -728,35 +759,44 @@
         mixtures.append(exchange(outs))
 
     outs, mixture_grads = feed(
-        where, moved, upstream, vectors_two, bias_up, mixtures, second_pieces, heads
+        where_whole, moved, upstream, vectors_two, bias_up, mixtures, gathered, heads
     )
     output, residual_grad, hidden_two, branch_one_grad, branch_two_grad = outs[:5]
     activated, pre_grad, attention, feed_sums, bias_sums = outs[5:]
+    incoming = exchange(mixture_grads)
     second_grad = feed_grads(
-        dp_size, where, hidden_two, branch_one_grad, branch_two_grad, activated, pre_grad, attention
-    )
-    second_far = reduce_cores(second_grad, dp_size)
-
-    received = [None] * len(saved)
-    order = list(reversed(range(len(saved))))
-    incoming = {n: exchange(mixture_grads[n]) for n in order}
-    output = regroup(tie(output, incoming[order[-1]]), dp_size)
-    gates = [(second_grad,), (second_far,)]
-    for n in order:
-        pieces, lse = saved[n]
-        grads = tie(incoming[n], *gates.pop(0))
-        received[n] = exchange(attend_back(pieces, grads, lse, cosine, sine))
-    second_half = reduce_first(second_grad, second_far, dp_size)
+        dp_size,
+        where_whole,
+        hidden_two,
+        branch_one_grad,
+        branch_two_grad,
+        activated,
+        pre_grad,
+        attention,
+    )
+    if dp_size == 8:
+        second_sum = lax.psum_scatter(second_grad, "dp", scatter_dimension=0, tiled=False)
+    else:
+        second_sum = lax.psum_scatter(second_grad, "dp", scatter_dimension=1, tiled=True)
+    second_sum = lax.psum_scatter(second_sum, "tensor", scatter_dimension=0, tiled=False)
+    second_sum = second_sum.astype(f32)
+    output = regroup(tie(output, incoming), dp_size)
+
+    received = []
+    gates = [second_grad]
+    for n, (pieces, lse) in enumerate(saved):
+        grads = tie(incoming, gates[n]) if n < len(gates) else incoming
+        received.append(exchange(attend_back(pieces, grads, n, lse, cosine, sine)))
     first_grad = project_grads(dp_size, where, hidden_one, received, heads)
     first_far = reduce_cores(first_grad, dp_size)
     input_grad, project_sums = project_back(
-        where, moved, vectors_one, residual_grad, received, first_pieces, heads
-    )
+        where, moved, vectors_one, residual_grad, tie(received, first_grad), first_pieces, heads
+    )
+    first_diagonal = reduce_diagonal(first_grad, first_far, dp_size)
+    first_half = reduce_first(first_diagonal, dp_size)
     input_grad = regroup(input_grad, dp_size)
-    second_sum = reduce_second(second_grad, second_far, second_half, dp_size)
-    first_half = reduce_first(first_grad, first_far, dp_size)
-    first_sum = reduce_second(first_grad, first_far, first_half, dp_size)
-    second_sum = reduce_planes(second_sum, dp_size)
+    first_sides = reduce_sides(first_grad, first_far, first_half, dp_size)
+    first_sum = reduce_second(first_grad, first_far, first_sides, dp_size)
     first_sum = reduce_planes(first_sum, dp_size)
     out_out = second_sum[:, :wide].T
     up_out = second_sum[:, wide : wide + hidden]
@@ -777,7 +817,7 @@
             feed_sums[4:5],
         ]
     )
-    bias_sums = bias_sums.reshape(GROUP, hidden // width, width)
+    bias_sums = reorder(bias_sums, z).reshape(GROUP, hidden // width, width)
     other = swap_z(jnp.concatenate([mine, bias_sums.reshape(-1, width)]), dp_size, 1)
     other_bias = other[9:].reshape(bias_sums.shape)
     mine = jnp.concatenate(
@@ -798,7 +838,6 @@
     rel = jnp.arange(dp_size)
     seq_at = (me // 2 ^ rel // 2) * 2 + (z // 2 ^ rel % 2)
     mods = mods.reshape(dp_size, 6 * width).astype(bf16)
-    columns = ada_weight.shape[1]
     own_mods = lax.dynamic_slice_in_dim(mods, me * columns, columns, axis=1)
     pick = (seq_at[:, None] == jnp.arange(dp_size)[None, :]).astype(bf16)
     ada_out = einsum("sc,se->ce", jnp.dot(pick, embeds), own_mods)

time: 442 us -> 398 us (0.900)
  waiting for transfers between devices: 155 us -> 96.7 us
  starting transfers between devices: 84.1 us -> 99.6 us
  between operations: 2.96 us -> 15.7 us
  other arithmetic: 29.5 us -> 19.3 us
  local copies, waits for them, and re-layouts: 51.7 us -> 41.6 us
    ppermute x84 -> x64, waiting for transfers between devices: 155 us -> 96.7 us  [permute(): return lax.ppermute(array, AXES, pairs)]
    ppermute x84 -> x64, starting transfers between devices: 84.1 us -> 99 us  [permute(): return lax.ppermute(array, AXES, pairs)]
    add x2, other arithmetic: 7.09 us -> 1.65 us  [the longest x1 1.63 us: reduce_sides(): x = parts[0][1].astype(f32) + far[1].astype(f32)]
    slice x10 -> x6, local copies, waits for them, and re-layouts: 6.98 us -> 2.45 us  [the longest x2 1.43 us: gather_weights(): near = (own, x, y, swap_dp(x[:2], dp_size, 4), swap_dp(y[2:], dp_size, 2))]
    pallas_call x4 -> x5, Pallas kernels: 73.8 us -> 75.8 us  [the longest x3 37 us: attend_back(): pl.pallas_call(functools.partial(attend_back_kernel, first_head), out_sha...]
    unnamed x220 -> x158, local copies, waits for them, and re-layouts: 28.6 us -> 28 us
    pallas_call x2 -> x3, Pallas kernels: 19.3 us -> 19.9 us  [attend(): pl.pallas_call(attend_kernel, out_shape=[jax.ShapeDtypeStruct((heads * HE...]
  transfers between devices with their start and end apart: 84 -> 67, of which waited for: 29 -> 23; matrix products, arithmetic and copies ran while one was open for 12% -> 9% of each run, Pallas kernels for 16% -> 19%
where the time goes in v3:
time: 398 us; the launch traced here: 391 us
  Pallas kernels  113 us (28%)
  starting transfers between devices  99.6 us (25%)
  waiting for transfers between devices  96.7 us (24%)
  local copies, waits for them, and re-layouts  41.6 us (10%)
  other arithmetic  19.3 us (5%)
  between operations  15.7 us (4%)
  matrix products  5.98 us (2%)
    ppermute x64, starting transfers between devices, permute(): return lax.ppermute(array, AXES, pairs)  99 us
    ppermute x64, waiting for transfers between devices, permute(): return lax.ppermute(array, AXES, pairs)  96.7 us
    pallas_call x3, Pallas kernels, attend_back(): pl.pallas_call(functools.partial(attend_back_kernel, first_head), out_sha...  37 us
    pallas_call x1, Pallas kernels, feed(): pl.pallas_call(functools.partial(feed_kernel, heads), out_shape=[shape(bf...  29.8 us
    unnamed x158, local copies, waits for them, and re-layouts  28 us
    pallas_call x3, Pallas kernels, attend(): pl.pallas_call(attend_kernel, out_shape=[jax.ShapeDtypeStruct((heads * HE...  19.9 us
    pallas_call x1, Pallas kernels, feed_grads(): pl.pallas_call(feed_grads_kernel, out_shape=jax.ShapeDtypeStruct(shape, b...  8.99 us
  transfers between devices with their start and end apart: 67, of which 23 were waited for; matrix products, arithmetic and copies ran while one was open for 9% of the time, Pallas kernels for 19%

profile of v3, /device:TPU:0, one launch (start us, length us, event | category | flops | bytes accessed | tf_op | source)
XLA Modules:
  0.0 391.4 jit_solution(7844515858595111305)
XLA Ops:
  19.2 4.0 %collective-permute-done.5 = bf16[1,144,576]{2,1,0:T(8,128)(2,1)S(1)} collective-permute-done((bf16[1,144,576]{2,1,0:T(8,128)(2,1)S(1)}, bf16[1,144,576]{2,1,0:T(8,128)(2,1)S(1)}, u32[]{:S(2)}, u32[]{:S(2)}) %collective-permute-start.5) | collective-permute-done | bytes 165920 | tf_op jit(solution)/shard_map/ppermute | solution.py:26
  32.7 3.3 collective-permute-done.6
  37.2 5.5 %collective-permute-start.7 = (bf16[4,144,576]{2,1,0:T(8,128)(2,1)}, bf16[4,144,576]{2,1,0:T(8,128)(2,1)}, u32[]{:S(2)}, u32[]{:S(2)}) collective-permute-start(bf16[4,144,576]{2,1,0:T(8,128)(2,1)} %get-tuple-element.221), channel_id=1, source_target_pairs={{0,4},{1,5},{2,6},{3,7},{4,0},{5,1},{6,2},{7,3},{8,12},{9,13},{10,... | collective-permute-start | bytes 1990664 | tf_op jit(solution)/shard_map/ppermute | solution.py:26
  49.0 20.7 %collective-permute-start.15 = (bf16[4,96,576]{2,1,0:T(8,128)(2,1)S(1)}, bf16[4,96,576]{2,1,0:T(8,128)(2,1)S(1)}, u32[]{:S(2)}, u32[]{:S(2)}) collective-permute-start(bf16[4,96,576]{2,1,0:T(8,128)(2,1)S(1)} %collective-permute-done.10.refs_6_.refs_17_), channel_id=1, source_target_pairs={{0,4},{1,5},{2,6},{3,7},{4,0},{5,1},{6,2},{7,3},{8,12},{9,13},{10,... | collective-permute-start | bytes 1327112 | tf_op jit(solution)/shard_map/ppermute | solution.py:26
  83.1 3.2 collective-permute-done.8
  86.5 7.5 %collective-permute-start.4 = (bf16[512,768]{1,0:T(8,128)(2,1)}, bf16[512,768]{1,0:T(8,128)(2,1)}, u32[]{:S(2)}, u32[]{:S(2)}) collective-permute-start(bf16[512,768]{1,0:T(8,128)(2,1)} %param.25), channel_id=1, source_target_pairs={{0,0},{1,1},{2,4},{3,5},{4,2},{5,3},{6,6},{7,7},{8,8},{9,9},{10,12... | collective-permute-start | bytes 2359304 | tf_op jit(solution)/shard_map/ppermute | solution.py:26
  94.1 6.0 %project.1 = (bf16[512,768]{1,0:T(8,128)(2,1)S(1)}, bf16[192,512]{1,0:T(8,128)(2,1)S(1)}, bf16[192,512]{1,0:T(8,128)(2,1)S(1)}, bf16[192,512]{1,0:T(8,128)(2,1)S...) custom-call(s32[2]{0:T(128)S(1)} %pad_add_fusion.1.refs_0_.where, ...), custom_call_target="tpu_custom_call" | custom-call | flops 1811939328 | bytes 5898240 | tf_op jit(solution)/shard_map/project/pallas_call | solution.py:386
  107.2 3.1 collective-permute-start.32
  111.2 13.1 %collective-permute-done.9 = bf16[2,768]{1,0:T(2,128)(2,1)S(1)} collective-permute-done((bf16[2,768]{1,0:T(2,128)(2,1)S(1)}, bf16[2,768]{1,0:T(2,128)(2,1)S(1)}, u32[]{:S(2)}, u32[]{:S(2)}) %collective-permute-start.9) | collective-permute-done | bytes 3104 | tf_op jit(solution)/shard_map/ppermute | solution.py:26
  130.1 6.6 %attend.5 = (bf16[64,512]{1,0:T(8,128)(2,1)S(1)}, bf16[64,512]{1,0:T(8,128)(2,1)S(1)}, bf16[64,512]{1,0:T(8,128)(2,1)S(1)}, bf16[64,512]{1,0:T(8,128)(2,1)S(1)}, f32[4,512]{1,0:T(4,128)S(1)}) custom-call(bf16[192,512]{1,0:T(8,128)(2,1)S(1)} %copy-done.45, bf16[192,512]{1,0:T(8,128)(2,1)S(1)} %collective-permute-done.31.a1.refs_1_, ...), custom_call_target="tpu_custom_call" | custom-call | flops 4294967296 | bytes 1048576 | tf_op jit(solution)/shard_map/attend/pallas_call | solution.py:215
  139.0 6.7 %attend.4 = (bf16[64,512]{1,0:T(8,128)(2,1)S(1)}, bf16[64,512]{1,0:T(8,128)(2,1)S(1)}, bf16[64,512]{1,0:T(8,128)(2,1)S(1)}, bf16[64,512]{1,0:T(8,128)(2,1)S(1)}, f32[4,512]{1,0:T(4,128)S(1)}) custom-call(bf16[192,512]{1,0:T(8,128)(2,1)S(1)} %copy-done.42, bf16[192,512]{1,0:T(8,128)(2,1)S(1)} %collective-permute-done.25.a1.refs_1_, ...), custom_call_target="tpu_custom_call" | custom-call | flops 4294967296 | bytes 1048576 | tf_op jit(solution)/shard_map/attend/pallas_call | solution.py:215
  148.7 6.6 %attend.3 = (bf16[64,512]{1,0:T(8,128)(2,1)S(1)}, bf16[64,512]{1,0:T(8,128)(2,1)S(1)}, bf16[64,512]{1,0:T(8,128)(2,1)S(1)}, bf16[64,512]{1,0:T(8,128)(2,1)S(1)}, f32[4,512]{1,0:T(4,128)S(1)}) custom-call(bf16[192,512]{1,0:T(8,128)(2,1)S(1)} %copy-done.39, bf16[192,512]{1,0:T(8,128)(2,1)S(1)} %collective-permute-done.19.a1.refs_1_, ...), custom_call_target="tpu_custom_call" | custom-call | flops 4294967296 | bytes 1048576 | tf_op jit(solution)/shard_map/attend/pallas_call | solution.py:215
  163.4 29.8 %feed.1 = (bf16[512,768]{1,0:T(8,128)(2,1)}, f32[512,768]{1,0:T(8,128)}, bf16[512,768]{1,0:T(8,128)(2,1)}, bf16[512,768]{1,0:T(8,128)(2,1)}, bf16[512,768]{1,0:T...) custom-call(s32[2]{0:T(128)} %pad_add_fusion.refs_0_.where, ...), custom_call_target="tpu_custom_call" | custom-call | flops 10871635968 | bytes 17694720 | tf_op jit(solution)/shard_map/feed/pallas_call | solution.py:502
  201.7 9.0 %feed_grads.1 = bf16[8,4,96,1728]{3,2,1,0:T(8,128)(2,1)} custom-call(s32[2]{0:T(128)S(1)} %copy-done.21, bf16[512,768]{1,0:T(8,128)(2,1)S(1)} %copy-done.4, bf16[512,768]{1,0:T(8,128)(2,1)S(1)} %copy-done.5, bf16[512,768]{1,0:T(8,128)(2,1)S(1)} %copy-done.6, bf16[4,512,768]{2,1,0:T(8,128)(2,1)S(1)} %copy-done, bf16[4,512,768]{2,1,0:T(8,128)(2,1)S(1)} %copy-done.1, ...), custom_call_target="tpu_custom_call" | custom-call | flops 5435817984 | bytes 17694720 | tf_op jit(solution)/shard_map/feed_grads/pallas_call | solution.py:560
  213.5 5.7 %collective-permute-done.37.refs_5_ = bf16[192,512]{1,0:T(8,128)(2,1)} collective-permute-done((bf16[192,512]{1,0:T(8,128)(2,1)}, bf16[192,512]{1,0:T(8,128)(2,1)}, u32[]{:S(2)}, u32[]{:S(2)}) %collective-permute-start.37) | collective-permute-done | bytes 196640 | tf_op jit(solution)/shard_map/ppermute | solution.py:26
  219.2 3.3 collective-permute-done.39.refs_7_
  224.6 12.3 %attend_back.5 = (bf16[192,512]{1,0:T(8,128)(2,1)S(1)}, bf16[192,512]{1,0:T(8,128)(2,1)S(1)}, bf16[192,512]{1,0:T(8,128)(2,1)S(1)}, bf16[192,512]{1,0:T(8,128)(2,1)S(1)}) custom-call(bf16[192,512]{1,0:T(8,128)(2,1)S(1)} %copy-done.46, bf16[192,512]{1,0:T(8,128)(2,1)S(1)} %collective-permute-done.31.a1.refs_1_, ...), custom_call_target="tpu_custom_call" | custom-call | flops 10737418240 | bytes 2097152 | tf_op jit(solution)/shard_map/attend_back/pallas_call | solution.py:290
  239.1 12.3 %attend_back.4 = (bf16[192,512]{1,0:T(8,128)(2,1)S(1)}, bf16[192,512]{1,0:T(8,128)(2,1)S(1)}, bf16[192,512]{1,0:T(8,128)(2,1)S(1)}, bf16[192,512]{1,0:T(8,128)(2,1)S(1)}) custom-call(bf16[192,512]{1,0:T(8,128)(2,1)S(1)} %copy-done.43, bf16[192,512]{1,0:T(8,128)(2,1)S(1)} %collective-permute-done.25.a1.refs_1_, ...), custom_call_target="tpu_custom_call" | custom-call | flops 10737418240 | bytes 2097152 | tf_op jit(solution)/shard_map/attend_back/pallas_call | solution.py:290
  253.0 12.4 %attend_back.3 = (bf16[192,512]{1,0:T(8,128)(2,1)S(1)}, bf16[192,512]{1,0:T(8,128)(2,1)S(1)}, bf16[192,512]{1,0:T(8,128)(2,1)S(1)}, bf16[192,512]{1,0:T(8,128)(2,1)S(1)}) custom-call(bf16[192,512]{1,0:T(8,128)(2,1)S(1)} %copy-done.40, bf16[192,512]{1,0:T(8,128)(2,1)S(1)} %collective-permute-done.19.a1.refs_1_, bf16[192,512]{1,0:T(8,128)(2,1)S(1)} %copy-done.25, ...), custom_call_target="tpu_custom_call" | custom-call | flops 10737418240 | bytes 2097152 | tf_op jit(solution)/shard_map/attend_back/pallas_call | solution.py:290
  268.3 3.7 collective-permute-done.46.refs_7_.refs_11_
  272.1 5.5 %collective-permute-done.41.refs_1_.refs_5_ = bf16[192,512]{1,0:T(8,128)(2,1)S(1)} collective-permute-done((bf16[192,512]{1,0:T(8,128)(2,1)S(1)}, bf16[192,512]{1,0:T(8,128)(2,1)S(1)}, u32[]{:S(2)}, u32[]{:S(2)}) %collective-permute-start.41) | collective-permute-done | bytes 196640 | tf_op jit(solution)/shard_map/ppermute | solution.py:26
  280.5 5.4 %project_grads.1 = (bf16[4,4,96,576]{3,2,1,0:T(8,128)(2,1)S(1)}, bf16[4,4,96,576]{3,2,1,0:T(8,128)(2,1)S(1)}) custom-call(s32[2]{0:T(128)S(1)} %pad_add_fusion.1.refs_0_.where, bf16[512,768]{1,0:T(8,128)(2,1)S(1)} %copy-done.37, bf16[192,512]{1,0:T(8,128)(2,1)S(1)} %get-tuple-element.153.refs_0_.refs_4_, ...), custom_call_target="tpu_custom_call" | custom-call | flops 1811939328 | bytes 5898240 | tf_op jit(solution)/shard_map/project_grads/pallas_call | solution.py:603
  286.1 5.4 %project_back.1 = (bf16[512,768]{1,0:T(8,128)(2,1)S(1)}, f32[2,768]{1,0:T(2,128)S(1)}) custom-call(s32[2]{0:T(128)S(1)} %pad_add_fusion.1.refs_0_.where, bf16[512,768]{1,0:T(8,128)(2,1)S(1)} %copy-done.8, f32[3,768]{1,0:T(4,128)S(1)} %pad_maximum_fusion.20.refs_2_, f32[512,768]{1,0:T(8,128)S(1)} %copy-done.2, ...), custom_call_target="tpu_custom_call" | custom-call | flops 1811939328 | bytes 5898240 | tf_op jit(solution)/shard_map/project_back/pallas_call | solution.py:644
  294.0 3.8 collective-permute-done.51
  300.3 4.7 %collective-permute-done.53 = f32[11,768]{1,0:T(8,128)S(1)} collective-permute-done((f32[11,768]{1,0:T(8,128)S(1)}, f32[11,768]{1,0:T(8,128)S(1)}, u32[]{:S(2)}, u32[]{:S(2)}) %collective-permute-start.53) | collective-permute-done | bytes 33824 | tf_op jit(solution)/shard_map/ppermute | solution.py:26
  305.9 7.4 %collective-permute-start.40 = (bf16[512,768]{1,0:T(8,128)(2,1)}, bf16[512,768]{1,0:T(8,128)(2,1)}, u32[]{:S(2)}, u32[]{:S(2)}) collective-permute-start(bf16[512,768]{1,0:T(8,128)(2,1)} %get-tuple-element.123), channel_id=1, source_target_pairs={{0,0},{1,1},{2,4},{3,5},{4,2},{5,3},{6,6},{7,7},{8,8},{9,9},{10,12... | collective-permute-start | bytes 2359304 | tf_op jit(solution)/shard_map/ppermute | solution.py:26
  313.3 7.4 %collective-permute-start.50 = (bf16[512,768]{1,0:T(8,128)(2,1)}, bf16[512,768]{1,0:T(8,128)(2,1)}, u32[]{:S(2)}, u32[]{:S(2)}) collective-permute-start(bf16[512,768]{1,0:T(8,128)(2,1)} %copy-done.23), channel_id=1, source_target_pairs={{0,0},{1,1},{2,4},{3,5},{4,2},{5,3},{6,6},{7,7},{8,8},{9,9},{10,12... | collective-permute-start | bytes 2359304 | tf_op jit(solution)/shard_map/ppermute | solution.py:26
  321.8 3.8 collective-permute-done.55
  332.2 5.9 %collective-permute-done.57 = bf16[2,96,576]{2,1,0:T(8,128)(2,1)} collective-permute-done((bf16[2,96,576]{2,1,0:T(8,128)(2,1)}, bf16[2,96,576]{2,1,0:T(8,128)(2,1)}, u32[]{:S(2)}, u32[]{:S(2)}) %collective-permute-start.57) | collective-permute-done | bytes 221216 | tf_op jit(solution)/shard_map/ppermute | solution.py:26
  348.4 3.2 collective-permute-done.60
  358.0 7.9 %collective-permute-done.61 = bf16[96,576]{1,0:T(8,128)(2,1)S(1)} collective-permute-done((bf16[96,576]{1,0:T(8,128)(2,1)S(1)}, bf16[96,576]{1,0:T(8,128)(2,1)S(1)}, u32[]{:S(2)}, u32[]{:S(2)}) %collective-permute-start.61) | collective-permute-done | bytes 110624 | tf_op jit(solution)/shard_map/ppermute | solution.py:26
  365.9 10.8 %collective-permute-done.62 = bf16[96,576]{1,0:T(8,128)(2,1)S(1)} collective-permute-done((bf16[96,576]{1,0:T(8,128)(2,1)S(1)}, bf16[96,576]{1,0:T(8,128)(2,1)S(1)}, u32[]{:S(2)}, u32[]{:S(2)}) %collective-permute-start.62) | collective-permute-done | bytes 110624 | tf_op jit(solution)/shard_map/ppermute | solution.py:26
  (436 shorter events, 129.7 us)
Async XLA Ops:
  7.3 155.5 %all-gather.3.cloned.1.call-start = ((), (), s32[]{:S(2)}) async-start(), calls=%async_computation.4 | async-start | bytes 11354112 | tf_op jit(solution)/shard_map/all_gather | solution.py:713
  10.3 321.9 %reduce-scatter.3.cloned.1.call-start = ((), (), s32[]{:S(2)}) async-start(), calls=%async_computation.2 | async-start | bytes 12386304 | tf_op jit(solution)/shard_map/reduce_scatter | solution.py:778
  11.3 13.7 %collective-permute-start = (bf16[96,576]{1,0:T(8,128)(2,1)S(1)}, bf16[96,576]{1,0:T(8,128)(2,1)S(1)}, u32[]{:S(2)}, u32[]{:S(2)}) collective-permute-start(bf16[96,576]{1,0:T(8,128)(2,1)S(1)} %pad_maximum_fusion.7), channel_id=1, source_target_pairs={{0,1},{1,0},{2,3},{3,2},{4,5},{5,4},{6,7},{7,6},{8,9},{9,8},{10,11... | collective-permute-start | bytes 331784 | tf_op jit(solution)/shard_map/ppermute | solution.py:26
  14.4 13.2 %collective-permute-start.1 = (bf16[96,576]{1,0:T(8,128)(2,1)S(1)}, bf16[96,576]{1,0:T(8,128)(2,1)S(1)}, u32[]{:S(2)}, u32[]{:S(2)}) collective-permute-start(bf16[96,576]{1,0:T(8,128)(2,1)S(1)} %pad_maximum_fusion.7), channel_id=1, source_target_pairs={{0,2},{1,3},{2,0},{3,1},{4,6},{5,7},{6,4},{7,5},{8,10},{9,11},{10,... | collective-permute-start | bytes 331784 | tf_op jit(solution)/shard_map/ppermute | solution.py:26
  27.7 17.5 %collective-permute-start.10 = (bf16[4,96,576]{2,1,0:T(8,128)(2,1)S(1)}, bf16[4,96,576]{2,1,0:T(8,128)(2,1)S(1)}, u32[]{:S(2)}, u32[]{:S(2)}) collective-permute-start(bf16[4,96,576]{2,1,0:T(8,128)(2,1)S(1)} %pad_maximum_fusion.2.refs_5_.refs_16_), channel_id=1, source_target_pairs={{0,8},{1,9},{2,10},{3,11},{4,12},{5,13},{6,14},{7,15},{8,0},{9,1},... | collective-permute-start | bytes 1327112 | tf_op jit(solution)/shard_map/ppermute | solution.py:26
  29.2 17.9 %collective-permute-start.11 = (bf16[4,96,576]{2,1,0:T(8,128)(2,1)S(1)}, bf16[4,96,576]{2,1,0:T(8,128)(2,1)S(1)}, u32[]{:S(2)}, u32[]{:S(2)}) collective-permute-start(bf16[4,96,576]{2,1,0:T(8,128)(2,1)S(1)} %pad_maximum_fusion.2.refs_5_.refs_16_), channel_id=1, source_target_pairs={{0,16},{1,17},{2,18},{3,19},{4,20},{5,21},{6,22},{7,23},{8,24},{9,... | collective-permute-start | bytes 1327112 | tf_op jit(solution)/shard_map/ppermute | solution.py:26
  30.9 18.1 %collective-permute-start.3 = (bf16[512,768]{1,0:T(8,128)(2,1)}, bf16[512,768]{1,0:T(8,128)(2,1)S(1)}, u32[]{:S(2)}, u32[]{:S(2)}) collective-permute-start(bf16[512,768]{1,0:T(8,128)(2,1)} %param.13), channel_id=1, source_target_pairs={{0,0},{1,1},{2,4},{3,5},{4,2},{5,3},{6,6},{7,7},{8,8},{9,9},{10,12... | collective-permute-start | bytes 2359304 | tf_op jit(solution)/shard_map/ppermute | solution.py:26
  37.2 32.5 %collective-permute-start.7 = (bf16[4,144,576]{2,1,0:T(8,128)(2,1)}, bf16[4,144,576]{2,1,0:T(8,128)(2,1)}, u32[]{:S(2)}, u32[]{:S(2)}) collective-permute-start(bf16[4,144,576]{2,1,0:T(8,128)(2,1)} %get-tuple-element.221), channel_id=1, source_target_pairs={{0,4},{1,5},{2,6},{3,7},{4,0},{5,1},{6,2},{7,3},{8,12},{9,13},{10,... | collective-permute-start | bytes 1990664 | tf_op jit(solution)/shard_map/ppermute | solution.py:26
  45.2 41.4 %collective-permute-start.14 = (bf16[4,96,576]{2,1,0:T(8,128)(2,1)S(1)}, bf16[4,96,576]{2,1,0:T(8,128)(2,1)S(1)}, u32[]{:S(2)}, u32[]{:S(2)}) collective-permute-start(bf16[4,96,576]{2,1,0:T(8,128)(2,1)S(1)} %pad_maximum_fusion.2.refs_5_.refs_16_), channel_id=1, source_target_pairs={{0,4},{1,5},{2,6},{3,7},{4,0},{5,1},{6,2},{7,3},{8,12},{9,13},{10,... | collective-permute-start | bytes 1327112 | tf_op jit(solution)/shard_map/ppermute | solution.py:26
  45.9 36.5 %collective-permute-start.12 = (bf16[2,96,576]{2,1,0:T(8,128)(2,1)}, bf16[2,96,576]{2,1,0:T(8,128)(2,1)}, u32[]{:S(2)}, u32[]{:S(2)}) collective-permute-start(bf16[2,96,576]{2,1,0:T(8,128)(2,1)} %slice.408), channel_id=1, source_target_pairs={{0,16},{1,17},{2,18},{3,19},{4,20},{5,21},{6,22},{7,23},{8,24},{9,... | collective-permute-start | bytes 663560 | tf_op jit(solution)/shard_map/ppermute | solution.py:26
  47.8 34.7 %collective-permute-start.13 = (bf16[2,96,576]{2,1,0:T(8,128)(2,1)}, bf16[2,96,576]{2,1,0:T(8,128)(2,1)}, u32[]{:S(2)}, u32[]{:S(2)}) collective-permute-start(bf16[2,96,576]{2,1,0:T(8,128)(2,1)} %slice.409), channel_id=1, source_target_pairs={{0,8},{1,9},{2,10},{3,11},{4,12},{5,13},{6,14},{7,15},{8,0},{9,1},... | collective-permute-start | bytes 663560 | tf_op jit(solution)/shard_map/ppermute | solution.py:26
  49.0 45.1 %collective-permute-start.15 = (bf16[4,96,576]{2,1,0:T(8,128)(2,1)S(1)}, bf16[4,96,576]{2,1,0:T(8,128)(2,1)S(1)}, u32[]{:S(2)}, u32[]{:S(2)}) collective-permute-start(bf16[4,96,576]{2,1,0:T(8,128)(2,1)S(1)} %collective-permute-done.10.refs_6_.refs_17_), channel_id=1, source_target_pairs={{0,4},{1,5},{2,6},{3,7},{4,0},{5,1},{6,2},{7,3},{8,12},{9,13},{10,... | collective-permute-start | bytes 1327112 | tf_op jit(solution)/shard_map/ppermute | solution.py:26
  69.6 24.4 %collective-permute-start.16 = (bf16[4,96,576]{2,1,0:T(8,128)(2,1)S(1)}, bf16[4,96,576]{2,1,0:T(8,128)(2,1)}, u32[]{:S(2)}, u32[]{:S(2)}) collective-permute-start(bf16[4,96,576]{2,1,0:T(8,128)(2,1)S(1)} %collective-permute-done.11.refs_7_.refs_18_), channel_id=1, source_target_pairs={{0,4},{1,5},{2,6},{3,7},{4,0},{5,1},{6,2},{7,3},{8,12},{9,13},{10,... | collective-permute-start | bytes 1327112 | tf_op jit(solution)/shard_map/ppermute | solution.py:26
  86.5 76.2 %collective-permute-start.4 = (bf16[512,768]{1,0:T(8,128)(2,1)}, bf16[512,768]{1,0:T(8,128)(2,1)}, u32[]{:S(2)}, u32[]{:S(2)}) collective-permute-start(bf16[512,768]{1,0:T(8,128)(2,1)} %param.25), channel_id=1, source_target_pairs={{0,0},{1,1},{2,4},{3,5},{4,2},{5,3},{6,6},{7,7},{8,8},{9,9},{10,12... | collective-permute-start | bytes 2359304 | tf_op jit(solution)/shard_map/ppermute | solution.py:26
  94.0 30.2 %collective-permute-start.9 = (bf16[2,768]{1,0:T(2,128)(2,1)S(1)}, bf16[2,768]{1,0:T(2,128)(2,1)S(1)}, u32[]{:S(2)}, u32[]{:S(2)}) collective-permute-start(bf16[2,768]{1,0:T(2,128)(2,1)S(1)} %pad_maximum_fusion.29), channel_id=1, source_target_pairs={{0,2},{1,3},{2,0},{3,1},{4,6},{5,7},{6,4},{7,5},{8,10},{9,11},{10,... | collective-permute-start | bytes 9224 | tf_op jit(solution)/shard_map/ppermute | solution.py:26
  107.2 17.4 %collective-permute-start.31 = (bf16[192,512]{1,0:T(8,128)(2,1)}, bf16[192,512]{1,0:T(8,128)(2,1)S(1)}, u32[]{:S(2)}, u32[]{:S(2)}) collective-permute-start(bf16[192,512]{1,0:T(8,128)(2,1)} %get-tuple-element.111), channel_id=1, source_target_pairs={{0,1},{1,0},{2,3},{3,2},{4,5},{5,4},{6,7},{7,6},{8,9},{9,8},{10,11... | collective-permute-start | bytes 589832 | tf_op jit(solution)/shard_map/ppermute | solution.py:26
  107.2 17.6 %collective-permute-start.32 = (bf16[192,512]{1,0:T(8,128)(2,1)}, bf16[192,512]{1,0:T(8,128)(2,1)S(1)}, u32[]{:S(2)}, u32[]{:S(2)}) collective-permute-start(bf16[192,512]{1,0:T(8,128)(2,1)} %get-tuple-element.112), channel_id=1, source_target_pairs={{0,4},{1,5},{2,6},{3,7},{4,0},{5,1},{6,2},{7,3},{8,12},{9,13},{10,... | collective-permute-start | bytes 589832 | tf_op jit(solution)/shard_map/ppermute | solution.py:26
  110.3 18.8 %collective-permute-start.33 = (bf16[192,512]{1,0:T(8,128)(2,1)}, bf16[192,512]{1,0:T(8,128)(2,1)S(1)}, u32[]{:S(2)}, u32[]{:S(2)}) collective-permute-start(bf16[192,512]{1,0:T(8,128)(2,1)} %get-tuple-element.113), channel_id=1, source_target_pairs={{0,5},{1,4},{2,7},{3,6},{4,1},{5,0},{6,3},{7,2},{8,13},{9,12},{10,... | collective-permute-start | bytes 589832 | tf_op jit(solution)/shard_map/ppermute | solution.py:26
  124.8 14.2 %collective-permute-start.27 = (bf16[192,512]{1,0:T(8,128)(2,1)}, bf16[192,512]{1,0:T(8,128)(2,1)S(1)}, u32[]{:S(2)}, u32[]{:S(2)}) collective-permute-start(bf16[192,512]{1,0:T(8,128)(2,1)} %copy-done.33), channel_id=1, source_target_pairs={{0,5},{1,4},{2,7},{3,6},{4,1},{5,0},{6,3},{7,2},{8,13},{9,12},{10,... | collective-permute-start | bytes 589832 | tf_op jit(solution)/shard_map/ppermute | solution.py:26
  129.2 17.2 %collective-permute-start.19 = (bf16[192,512]{1,0:T(8,128)(2,1)}, bf16[192,512]{1,0:T(8,128)(2,1)S(1)}, u32[]{:S(2)}, u32[]{:S(2)}) collective-permute-start(bf16[192,512]{1,0:T(8,128)(2,1)} %copy-done.32), channel_id=1, source_target_pairs={{0,1},{1,0},{2,3},{3,2},{4,5},{5,4},{6,7},{7,6},{8,9},{9,8},{10,11... | collective-permute-start | bytes 589832 | tf_op jit(solution)/shard_map/ppermute | solution.py:26
  210.7 166.8 %reduce-scatter.5.cloned.1.call-start = ((), (), s32[]{:S(2)}) async-start(), calls=%async_computation.3 | async-start | bytes 1720320 | tf_op jit(solution)/shard_map/reduce_scatter | solution.py:781
  236.9 28.5 %collective-permute-start.47 = (bf16[192,512]{1,0:T(8,128)(2,1)S(1)}, bf16[192,512]{1,0:T(8,128)(2,1)S(1)}, u32[]{:S(2)}, u32[]{:S(2)}) collective-permute-start(bf16[192,512]{1,0:T(8,128)(2,1)S(1)} %get-tuple-element.147), channel_id=1, source_target_pairs={{0,1},{1,0},{2,3},{3,2},{4,5},{5,4},{6,7},{7,6},{8,9},{9,8},{10,11... | collective-permute-start | bytes 589832 | tf_op jit(solution)/shard_map/ppermute | solution.py:26
  238.4 27.7 %collective-permute-start.48 = (bf16[192,512]{1,0:T(8,128)(2,1)S(1)}, bf16[192,512]{1,0:T(8,128)(2,1)S(1)}, u32[]{:S(2)}, u32[]{:S(2)}) collective-permute-start(bf16[192,512]{1,0:T(8,128)(2,1)S(1)} %get-tuple-element.148), channel_id=1, source_target_pairs={{0,4},{1,5},{2,6},{3,7},{4,0},{5,1},{6,2},{7,3},{8,12},{9,13},{10,... | collective-permute-start | bytes 589832 | tf_op jit(solution)/shard_map/ppermute | solution.py:26
  238.5 29.1 %collective-permute-start.49 = (bf16[192,512]{1,0:T(8,128)(2,1)S(1)}, bf16[192,512]{1,0:T(8,128)(2,1)S(1)}, u32[]{:S(2)}, u32[]{:S(2)}) collective-permute-start(bf16[192,512]{1,0:T(8,128)(2,1)S(1)} %get-tuple-element.149), channel_id=1, source_target_pairs={{0,5},{1,4},{2,7},{3,6},{4,1},{5,0},{6,3},{7,2},{8,13},{9,12},{10,... | collective-permute-start | bytes 589832 | tf_op jit(solution)/shard_map/ppermute | solution.py:26
  251.5 16.1 %collective-permute-start.44 = (bf16[192,512]{1,0:T(8,128)(2,1)S(1)}, bf16[192,512]{1,0:T(8,128)(2,1)S(1)}, u32[]{:S(2)}, u32[]{:S(2)}) collective-permute-start(bf16[192,512]{1,0:T(8,128)(2,1)S(1)} %get-tuple-element.142), channel_id=1, source_target_pairs={{0,1},{1,0},{2,3},{3,2},{4,5},{5,4},{6,7},{7,6},{8,9},{9,8},{10,11... | collective-permute-start | bytes 589832 | tf_op jit(solution)/shard_map/ppermute | solution.py:26
  253.0 15.3 %collective-permute-start.45 = (bf16[192,512]{1,0:T(8,128)(2,1)S(1)}, bf16[192,512]{1,0:T(8,128)(2,1)S(1)}, u32[]{:S(2)}, u32[]{:S(2)}) collective-permute-start(bf16[192,512]{1,0:T(8,128)(2,1)S(1)} %get-tuple-element.143), channel_id=1, source_target_pairs={{0,4},{1,5},{2,6},{3,7},{4,0},{5,1},{6,2},{7,3},{8,12},{9,13},{10,... | collective-permute-start | bytes 589832 | tf_op jit(solution)/shard_map/ppermute | solution.py:26
  305.2 15.6 %collective-permute-start.54 = (f32[16,768]{1,0:T(8,128)S(1)}, f32[16,768]{1,0:T(8,128)S(1)}, u32[]{:S(2)}, u32[]{:S(2)}) collective-permute-start(f32[16,768]{1,0:T(8,128)S(1)} %pad_maximum_fusion.14), channel_id=1, source_target_pairs={{0,8},{1,9},{2,10},{3,11},{4,12},{5,13},{6,14},{7,15},{8,0},{9,1},... | collective-permute-start | bytes 147464 | tf_op jit(solution)/shard_map/ppermute | solution.py:26
  305.9 52.1 %collective-permute-start.40 = (bf16[512,768]{1,0:T(8,128)(2,1)}, bf16[512,768]{1,0:T(8,128)(2,1)}, u32[]{:S(2)}, u32[]{:S(2)}) collective-permute-start(bf16[512,768]{1,0:T(8,128)(2,1)} %get-tuple-element.123), channel_id=1, source_target_pairs={{0,0},{1,1},{2,4},{3,5},{4,2},{5,3},{6,6},{7,7},{8,8},{9,9},{10,12... | collective-permute-start | bytes 2359304 | tf_op jit(solution)/shard_map/ppermute | solution.py:26
  313.3 14.8 %collective-permute-start.56 = (bf16[4,4,96,576]{3,2,1,0:T(8,128)(2,1)}, bf16[4,4,96,576]{3,2,1,0:T(8,128)(2,1)}, u32[]{:S(2)}, u32[]{:S(2)}) collective-permute-start(bf16[4,4,96,576]{3,2,1,0:T(8,128)(2,1)} %copy-done.22), channel_id=1, source_target_pairs={{0,4},{1,5},{2,6},{3,7},{4,0},{5,1},{6,2},{7,3},{8,12},{9,13},{10,... | collective-permute-start | bytes 5308424 | tf_op jit(solution)/shard_map/ppermute | solution.py:26
  313.3 44.6 %collective-permute-start.50 = (bf16[512,768]{1,0:T(8,128)(2,1)}, bf16[512,768]{1,0:T(8,128)(2,1)}, u32[]{:S(2)}, u32[]{:S(2)}) collective-permute-start(bf16[512,768]{1,0:T(8,128)(2,1)} %copy-done.23), channel_id=1, source_target_pairs={{0,0},{1,1},{2,4},{3,5},{4,2},{5,3},{6,6},{7,7},{8,8},{9,9},{10,12... | collective-permute-start | bytes 2359304 | tf_op jit(solution)/shard_map/ppermute | solution.py:26
  353.0 23.6 %collective-permute-start.62 = (bf16[96,576]{1,0:T(8,128)(2,1)S(1)}, bf16[96,576]{1,0:T(8,128)(2,1)S(1)}, u32[]{:S(2)}, u32[]{:S(2)}) collective-permute-start(bf16[96,576]{1,0:T(8,128)(2,1)S(1)} %get-tuple-element.226), channel_id=1, source_target_pairs={{0,2},{1,3},{2,0},{3,1},{4,6},{5,7},{6,4},{7,5},{8,10},{9,11},{10,... | collective-permute-start | bytes 331784 | tf_op jit(solution)/shard_map/ppermute | solution.py:26
  355.5 21.1 %collective-permute-start.63 = (bf16[96,576]{1,0:T(8,128)(2,1)S(1)}, bf16[96,576]{1,0:T(8,128)(2,1)S(1)}, u32[]{:S(2)}, u32[]{:S(2)}) collective-permute-start(bf16[96,576]{1,0:T(8,128)(2,1)S(1)} %get-tuple-element.225), channel_id=1, source_target_pairs={{0,3},{1,2},{2,1},{3,0},{4,7},{5,6},{6,5},{7,4},{8,11},{9,10},{10,... | collective-permute-start | bytes 331784 | tf_op jit(solution)/shard_map/ppermute | solution.py:26
  (109 other events, 812.3 us)
Sparse Core Ops, SparseCore 0:
  10.9 110.6 all-gather.2
  210.8 83.1 reduce-scatter.2
  332.3 41.4 reduce-scatter.4

commit v4 on v3

v4 whole, which is shorter than its diff:
```python
import functools
import math

import jax
import jax.numpy as jnp
from jax import lax
from jax.experimental import pallas as pl
from jax.experimental.pallas import tpu as pltpu
from jax.sharding import PartitionSpec as P

HEAD_DIM = 64
EPSILON = 1e-05
ROPE_BASE = 10000.0
GROUP = 4
DP = ("quad", "core")
TENSOR = ("high", "low")
AXES = DP + TENSOR
TEAM = ("core", "low")
f32 = jnp.float32
bf16 = jnp.bfloat16
VMEM = pl.BlockSpec(memory_space=pltpu.VMEM)
SMEM = pl.BlockSpec(memory_space=pltpu.SMEM)
ANY = pl.BlockSpec(memory_space=pl.ANY)
HALF = HEAD_DIM // 2


def whole(array):
    return pl.BlockSpec(
        array.shape, lambda *at: (0,) * len(array.shape), pipeline_mode=pl.Buffered(1)
    )


def permute(array, dp_size, target):
    pairs = []
    for d in range(dp_size):
        for z in range(GROUP):
            to_d, to_z = target(d, z)
            if (d, z) != (to_d, to_z):
                pairs.append((d * GROUP + z, to_d * GROUP + to_z))
    return lax.ppermute(array, AXES, pairs)


def swap_dp(array, dp_size, mask):
    return permute(array, dp_size, lambda d, z: (d ^ mask, z))


def swap_z(array, dp_size, mask):
    return permute(array, dp_size, lambda d, z: (d, z ^ mask))


def send_tokens(array, dp_size):
    return permute(array, dp_size, lambda d, z: (d // 2 * 2 + z // 2, d % 2 * 2 + z % 2))


def settle(array, moved):
    stay = lax.axis_index("core") == lax.axis_index("high")
    return jnp.where(stay, array, moved)


def regroup(array, dp_size):
    return settle(array, send_tokens(array, dp_size))


def meet(*arrays):
    return lax.optimization_barrier(arrays)


def exchange(blocks):
    return lax.all_to_all(blocks, TEAM, 0, 0, tiled=True)


def reorder(array, index):
    count = array.shape[0]
    for k in range(count.bit_length() - 1):
        pairs = array.reshape(count >> (k + 1), 2, 1 << k, *array.shape[1:])
        pairs = jnp.concatenate([pairs[:, 1:], pairs[:, :1]], axis=1).reshape(array.shape)
        array = jnp.where((index >> k) % 2 == 1, pairs, array)
    return array


def first_step(array, dp_size):
    return jnp.stack([array, swap_dp(array, dp_size, 2)])


def spread_dp(blocks, dp_size):
    array = blocks[0]
    mask = 4
    while mask < dp_size:
        blocks = jnp.concatenate([blocks, swap_dp(blocks, dp_size, mask)])
        mask *= 2
    blocks = jnp.stack([blocks, swap_dp(blocks, dp_size, 1)], axis=1)
    return blocks.reshape(dp_size, *array.shape)


WHOLE = ((0, 0), (2, 0), (4, 0), (6, 0), (1, 0), (3, 0), (5, 0), (7, 0))
HALVES = WHOLE[:4] + ((6, 2),) + WHOLE[4:] + ((7, 2),)


def send_planes(shard, dp_size):
    return [swap_z(shard, dp_size, t) for t in range(1, GROUP)]


def gather_sides(own, dp_size):
    if dp_size != 8:
        return ()
    return swap_dp(own, dp_size, 2), swap_dp(own, dp_size, 4)


def gather_weights(own, sides, dp_size):
    if dp_size != 8:
        return (lax.all_gather(own, DP, axis=1, tiled=True),)
    x, y = sides
    near = (own, x, y, swap_dp(x[:2], dp_size, 4), swap_dp(y[2:], dp_size, 2))
    return near + tuple(swap_dp(piece, dp_size, 1) for piece in near)


def load_weights(me, pieces, full, sems, flip=None):
    if len(pieces) == 1:
        flips = [t if flip is None else t ^ flip for t in range(GROUP)]
        copies = [
            pltpu.make_async_copy(pieces[0].at[t], full.at[flips[t]], sems.at[t])
            for t in range(GROUP)
        ]
    else:
        copies = []
        for i, (piece, (rel, first)) in enumerate(
            zip(pieces, HALVES if len(pieces) == len(HALVES) else WHOLE)
        ):
            count, rows = piece.shape[:2]
            start = pl.multiple_of((me ^ rel) * rows, rows)
            if flip is None:
                place = full.at[first : first + count, pl.ds(start, rows)]
                copies.append(pltpu.make_async_copy(piece, place, sems.at[i]))
                continue
            for t in range(count):
                place = full.at[(first + t) ^ flip, pl.ds(start, rows)]
                sem = sems.at[GROUP * i + t]
                copies.append(pltpu.make_async_copy(piece.at[t], place, sem))
    for copy in copies:
        copy.start()
    return copies


def store_blocks(me, parity, outs, slot, value):
    if len(outs) == 1:
        outs[0][slot] = value
        return
    rows = outs[0].shape[2]
    for owner in range(2 * outs[0].shape[0]):
        out = outs[(owner + parity) % 2]
        out[(me ^ owner) >> 1, slot] = value[owner * rows : (owner + 1) * rows]


def grad_shapes(dp_size, width, columns):
    if dp_size != 8:
        return [jax.ShapeDtypeStruct((GROUP, width, columns), bf16)]
    return [jax.ShapeDtypeStruct((dp_size // 2, GROUP, width // dp_size, columns), bf16)] * 2


def plus(a, b):
    return (a.astype(f32) + b.astype(f32)).astype(bf16)


def reduce_cores(parts, dp_size):
    return swap_dp(parts[1], dp_size, 1) if dp_size == 8 else None


def reduce_diagonal(parts, far, dp_size):
    return plus(parts[0][3], far[3]) if dp_size == 8 else None


def reduce_first(diagonal, dp_size):
    if dp_size != 8:
        return None
    return swap_dp(diagonal[:2], dp_size, 2), swap_dp(diagonal[2:], dp_size, 4)


def reduce_sides(parts, far, half, dp_size):
    if dp_size != 8:
        return None
    x = parts[0][1].astype(f32) + far[1].astype(f32)
    y = parts[0][2].astype(f32) + far[2].astype(f32)
    x = jnp.concatenate([x[:2], x[2:] + half[1].astype(f32)]).astype(bf16)
    y = jnp.concatenate([y[:2] + half[0].astype(f32), y[2:]]).astype(bf16)
    return x, y


def reduce_second(parts, far, sides, dp_size):
    if dp_size != 8:
        return lax.psum_scatter(parts[0], DP, scatter_dimension=1, tiled=True).astype(f32)
    from_x = swap_dp(sides[0], dp_size, 2)
    from_y = swap_dp(sides[1], dp_size, 4)
    own = parts[0][0].astype(f32) + far[0].astype(f32)
    return own + from_x.astype(f32) + from_y.astype(f32)


def reduce_planes(own):
    terms = lax.all_to_all(own.astype(bf16), TENSOR, 0, 0, tiled=True)
    return jnp.sum(terms.astype(f32), axis=0)


def attend_kernel(packed, out, lse, key_t, value_t, key):
    count, _, block = packed.shape
    for i in range(count):
        columns = slice(i * block, (i + 1) * block)
        key_t[:, columns] = packed[i, HEAD_DIM : 2 * HEAD_DIM]
        value_t[:, columns] = packed[i, 2 * HEAD_DIM :]
    key[...] = key_t[...].T
    for i in range(count):
        query = packed[i, :HEAD_DIM] * bf16(HEAD_DIM**-0.5)
        scores = jnp.dot(key[...], query, preferred_element_type=f32)
        highest = jnp.max(scores, axis=0, keepdims=True)
        exponent = jnp.exp(scores - highest)
        totals = jnp.sum(exponent, axis=0, keepdims=True)
        mixture = jnp.dot(value_t[...], exponent.astype(bf16), preferred_element_type=f32)
        out[i] = (mixture / totals).astype(bf16)
        lse[0, i : i + 1, :] = highest + jnp.log(totals)


def attend(packed):
    count, lines, block = packed.shape
    heads = lines // (3 * HEAD_DIM)
    length = count * block
    return pl.pallas_call(
        attend_kernel,
        out_shape=[
            jax.ShapeDtypeStruct((count, heads * HEAD_DIM, block), bf16),
            jax.ShapeDtypeStruct((heads, count, block), f32),
        ],
        grid=(heads,),
        in_specs=[pl.BlockSpec((count, 3 * HEAD_DIM, block), lambda h: (0, h, 0))],
        out_specs=[
            pl.BlockSpec((count, HEAD_DIM, block), lambda h: (0, h, 0)),
            pl.BlockSpec((1, count, block), lambda h: (h, 0, 0)),
        ],
        scratch_shapes=[
            pltpu.VMEM((HEAD_DIM, length), bf16),
            pltpu.VMEM((HEAD_DIM, length), bf16),
            pltpu.VMEM((length, HEAD_DIM), bf16),
        ],
        compiler_params=pltpu.CompilerParams(vmem_limit_bytes=32 << 20),
        cost_estimate=pl.CostEstimate(
            flops=16 * heads * length * length * HEAD_DIM,
            bytes_accessed=8 * heads * length * HEAD_DIM,
            transcendentals=heads * length * length,
        ),
        name="attend",
    )(packed)


def attend_back_kernel(packed, grads, lse, cosine, sine, out, *scratch):
    key_t, key, value_t, query_grad, key_grad, value_grad = scratch
    count, _, block = packed.shape
    rows = min(256, block)
    half = HEAD_DIM // 2
    for i in range(count):
        columns = slice(i * block, (i + 1) * block)
        key_t[:, columns] = packed[i, HEAD_DIM : 2 * HEAD_DIM]
        value_t[:, columns] = packed[i, 2 * HEAD_DIM :]
        key[columns, :] = packed[i, HEAD_DIM : 2 * HEAD_DIM].T
    for i in range(count):
        log_total = lse[0, i : i + 1, :].T
        for c in range(block // rows):
            own = slice(c * rows, (c + 1) * rows)
            query_t = packed[i, :HEAD_DIM, own] * bf16(HEAD_DIM**-0.5)
            grad_t = grads[i, :, own]
            scores = jnp.dot(query_t.T, key_t[...], preferred_element_type=f32)
            weights = jnp.exp(scores - log_total[own])
            pull = jnp.dot(grad_t.T, value_t[...], preferred_element_type=f32)
            centre = jnp.sum(weights * pull, axis=1, keepdims=True)
            score_grad = (weights * (pull - centre)).astype(bf16)
            value_term = jnp.dot(grad_t, weights.astype(bf16), preferred_element_type=f32)
            key_term = jnp.dot(query_t, score_grad, preferred_element_type=f32)
            if i == 0 and c == 0:
                value_grad[...] = value_term
                key_grad[...] = key_term
            else:
                value_grad[...] += value_term
                key_grad[...] += key_term
            query_grad[:, i * block + c * rows : i * block + (c + 1) * rows] = (
                jnp.dot(score_grad, key[...], preferred_element_type=f32) * HEAD_DIM**-0.5
            ).T
    for i in range(count):
        columns = slice(i * block, (i + 1) * block)
        cos, sin = cosine[:, columns], sine[:, columns]
        for first, source in ((0, query_grad), (HEAD_DIM, key_grad)):
            upper, lower = source[:half, columns], source[half:, columns]
            out[i, first : first + half] = (upper * cos + lower * sin).astype(bf16)
            out[i, first + half : first + HEAD_DIM] = (lower * cos - upper * sin).astype(bf16)
        out[i, 2 * HEAD_DIM :] = value_grad[:, columns].astype(bf16)


def attend_back(head, packed, grads, lse, cosine, sine):
    count, _, block = packed.shape
    length = count * block
    lines = 3 * HEAD_DIM
    return pl.pallas_call(
        attend_back_kernel,
        out_shape=jax.ShapeDtypeStruct((count, lines, block), bf16),
        grid=(1,),
        in_specs=[
            pl.BlockSpec((count, lines, block), lambda i: (0, head, 0)),
            pl.BlockSpec((count, HEAD_DIM, block), lambda i: (0, head, 0)),
            pl.BlockSpec((1, count, block), lambda i: (head, 0, 0)),
            whole(cosine),
            whole(sine),
        ],
        out_specs=pl.BlockSpec((count, lines, block), lambda i: (0, 0, 0)),
        scratch_shapes=[
            pltpu.VMEM((HEAD_DIM, length), bf16),
            pltpu.VMEM((length, HEAD_DIM), bf16),
            pltpu.VMEM((HEAD_DIM, length), bf16),
            pltpu.VMEM((HEAD_DIM, length), f32),
            pltpu.VMEM((HEAD_DIM, length), f32),
            pltpu.VMEM((HEAD_DIM, length), f32),
        ],
        compiler_params=pltpu.CompilerParams(vmem_limit_bytes=60 << 20),
        cost_estimate=pl.CostEstimate(
            flops=40 * length * length * HEAD_DIM,
            bytes_accessed=16 * length * HEAD_DIM,
            transcendentals=length * length,
        ),
        name="attend_back",
    )(packed, grads, lse, cosine, sine)


def normalize(rows):
    center = jnp.mean(rows, axis=1, keepdims=True)
    shifted = rows - center
    inverse = lax.rsqrt(jnp.mean(shifted * shifted, axis=1, keepdims=True) + EPSILON)
    return shifted * inverse, inverse


def norm_back(scaled, normed, inverse):
    return inverse * (
        scaled
        - jnp.mean(scaled, axis=1, keepdims=True)
        - normed * jnp.mean(scaled * normed, axis=1, keepdims=True)
    )


def dot(a, b):
    return jnp.dot(a, b, preferred_element_type=f32)


def dot_nt(a, b):
    return lax.dot_general(a, b, (((1,), (1,)), ((), ())), preferred_element_type=f32)


def total(values):
    return jnp.sum(values, axis=0, keepdims=True)


def pack_kernel(ada, ada_bias, embed, gain_one, gain_two, bias_down, out, rows):
    lines = ada.shape[0]
    rows[...] = jnp.zeros_like(rows)
    for n, ref in enumerate((ada_bias, embed, gain_one, gain_two, bias_down)):
        rows[n : n + 1, : ref.shape[1]] = ref[...].astype(f32)
    out[:lines, : ada.shape[1]] = ada[...]
    out[lines:] = rows[...].astype(bf16)


def pack(ada, ada_bias, embed, gain_one, gain_two, bias_down):
    lines, columns = ada.shape
    columns = max(columns, embed.shape[1])
    rows = [x.reshape(1, -1) for x in (ada_bias, embed, gain_one, gain_two, bias_down)]
    return pl.pallas_call(
        pack_kernel,
        out_shape=jax.ShapeDtypeStruct((lines + 16, columns), bf16),
        in_specs=[VMEM] * 6,
        out_specs=VMEM,
        scratch_shapes=[pltpu.VMEM((16, columns), f32)],
        name="pack",
    )(ada, *rows)


def prepare_kernel(columns, per, where, packs, vectors, embeds, mods, wide):
    me, z = where[0], where[1]
    count = packs.shape[0]
    cond = embeds.shape[1]
    rel = jnp.where(me % 2 == z // 2, 0, 1)
    embed = jnp.broadcast_to(packs[rel, cond : cond + 16][1:2, :cond], (8, cond))
    mods[...] = jnp.zeros_like(mods)
    wide[...] = jnp.zeros_like(wide)
    vectors[...] = jnp.zeros_like(vectors)

    def add(r, total_mods):
        owner = me ^ r
        rows = packs[r, cond : cond + 16].astype(f32)
        part = dot(embed, packs[r, :cond, :columns]) + rows[0:1, :columns]
        mods[:, :columns] = part
        wide[:, :per] = rows[0:8, :per]
        embeds[pl.ds(owner, 1)] = rows[1:2, :cond]
        vectors[0:8] += pltpu.roll(wide[...], owner * per, 1)
        return total_mods + pltpu.roll(mods[...], owner * columns, 1)

    flat = lax.fori_loop(0, count, add, jnp.zeros(mods.shape, f32))
    width = vectors.shape[1]
    for n in range(6):
        vectors[8 + n : 9 + n] = flat[0:1, n * width : (n + 1) * width]


def prepare(where, packs, width, per, cond):
    dp_size = packs.shape[0]
    columns = 6 * width // dp_size
    return pl.pallas_call(
        functools.partial(prepare_kernel, columns, per),
        out_shape=[
            jax.ShapeDtypeStruct((16, width), f32),
            jax.ShapeDtypeStruct((dp_size, cond), f32),
        ],
        in_specs=[SMEM, VMEM],
        out_specs=[VMEM] * 2,
        scratch_shapes=[pltpu.VMEM((8, 6 * width), f32), pltpu.VMEM((8, width), f32)],
        compiler_params=pltpu.CompilerParams(vmem_limit_bytes=16 << 20),
        name="prepare",
    )(where, packs)


GAIN_ONE, GAIN_TWO, BIAS_DOWN, SHIFT_ONE, SCALE_ONE, GATE_ONE, SHIFT_TWO, SCALE_TWO, GATE_TWO = (
    slice(n, n + 1) for n in (2, 3, 4, 8, 9, 10, 11, 12, 13)
)


def project_kernel(count, *refs):
    where, tokens, vectors, cosine, sine = refs[:5]
    pieces, (hidden, packed, full, sems) = refs[5 : 5 + count], refs[5 + count :]
    me, z = where[0], where[1]
    wide = full.shape[2] // 3
    copies = load_weights(me, pieces, full, sems)
    gain, scale, shift = vectors[GAIN_ONE], vectors[SCALE_ONE], vectors[SHIFT_ONE]
    normed, _ = normalize(tokens[...].astype(f32))
    hidden[...] = (normed * gain * (1.0 + scale) + shift).astype(bf16)
    cos, sin = cosine[...], sine[...]
    for copy in copies:
        copy.wait()
    for i in range(GROUP):
        projected = dot(hidden[...], full[z ^ i]).T
        for h in range(wide // HEAD_DIM):
            at = 3 * HEAD_DIM * h
            for c in range(2):
                first = c * wide + h * HEAD_DIM
                upper = projected[first : first + HALF]
                lower = projected[first + HALF : first + HEAD_DIM]
                packed[i, at : at + HALF] = (upper * cos - lower * sin).astype(bf16)
                packed[i, at + HALF : at + HEAD_DIM] = (lower * cos + upper * sin).astype(bf16)
                at += HEAD_DIM
            first = 2 * wide + h * HEAD_DIM
            packed[i, at : at + HEAD_DIM] = projected[first : first + HEAD_DIM].astype(bf16)


def project(where, tokens, vectors, cosine, sine, pieces):
    rows, width = tokens.shape
    columns = pieces[0].shape[2]
    shapes = [
        jax.ShapeDtypeStruct((rows, width), bf16),
        jax.ShapeDtypeStruct((GROUP, columns, rows), bf16),
    ]
    return pl.pallas_call(
        functools.partial(project_kernel, len(pieces)),
        out_shape=shapes,
        grid=(1,),
        in_specs=[SMEM]
        + [whole(x) for x in (tokens, vectors, cosine, sine)]
        + [ANY] * len(pieces),
        out_specs=[whole(x) for x in shapes],
        scratch_shapes=[
            pltpu.VMEM((GROUP, width, columns), bf16),
            pltpu.SemaphoreType.DMA((GROUP * len(pieces),)),
        ],
        compiler_params=pltpu.CompilerParams(vmem_limit_bytes=32 << 20),
        cost_estimate=pl.CostEstimate(
            flops=2 * rows * width * GROUP * columns,
            bytes_accessed=2 * GROUP * (width + rows) * columns,
            transcendentals=0,
        ),
        name="project",
    )(where, tokens, vectors, cosine, sine, *pieces)


GELU_A = math.sqrt(2.0 / math.pi)
GELU_B = 0.044715


def feed_kernel(count, *refs):
    where, tokens, upstream, vectors, mixtures = refs[:5]
    pieces, refs = refs[5 : 5 + count], refs[5 + count :]
    output, residual_grad, out_hidden, out_branch_one, out_branch_two = refs[:5]
    activated, pre_grad, attention, sums, bias_sums = refs[5:10]
    mixture_grads, full, bias_up, slope, keep_one, keep_two, sems = refs[10:]
    wide = mixtures.shape[1]
    hidden = bias_up.shape[1]
    of_out = slice(0, wide)
    of_up = slice(wide, wide + hidden)
    of_down = slice(wide + hidden, wide + 2 * hidden)
    of_bias = slice(wide + 2 * hidden, wide + 2 * hidden + 64)
    copies = load_weights(where[0], pieces, full, sems)
    gain, scale, shift = vectors[GAIN_TWO], vectors[SCALE_TWO], vectors[SHIFT_TWO]
    gate_one, gate_two, bias_down = vectors[GATE_ONE], vectors[GATE_TWO], vectors[BIAS_DOWN]
    for r in range(GROUP):
        attention[r] = mixtures[r].T
    for copy in copies:
        copy.wait()
    for t in range(GROUP):
        bias_up[t : t + 1] = full[t, :, of_bias].T[0:1].astype(f32)
    branch_one = dot_nt(attention[0], full[0, :, of_out])
    for r in range(1, GROUP):
        branch_one = branch_one + dot_nt(attention[r], full[r, :, of_out])
    keep_one[...] = branch_one
    residual = tokens[...].astype(f32) + gate_one * branch_one
    normed, _ = normalize(residual)
    out_hidden[...] = (normed * gain * (1.0 + scale) + shift).astype(bf16)

    keep_two[...] = jnp.broadcast_to(bias_down, keep_two.shape)

    def forward(t, carry):
        pre = dot(out_hidden[...], full[t, :, of_up]) + bias_up[pl.ds(t, 1)]
        inner = jnp.tanh(GELU_A * (pre + GELU_B * pre * pre * pre))
        activated[t] = (0.5 * pre * (1.0 + inner)).astype(bf16)
        slope[t] = 0.5 * (1.0 + inner) + (
            0.5 * GELU_A * pre * (1.0 - inner * inner) * (1.0 + 3.0 * GELU_B * pre * pre)
        )
        keep_two[...] += dot_nt(activated[t], full[t, :, of_down])
        return carry

    lax.fori_loop(0, GROUP, forward, 0)
    branch_two = keep_two[...]
    residual = tokens[...].astype(f32) + gate_one * keep_one[...]
    output[...] = (residual + gate_two * branch_two).astype(bf16)
    grad = upstream[...].astype(f32)
    branch_two_grad = gate_two * grad
    out_branch_two[...] = branch_two_grad.astype(bf16)
    sums[2:3] = total(grad * branch_two)
    sums[4:5] = total(out_branch_two[...].astype(f32))

    keep_two[...] = jnp.zeros_like(keep_two)

    def backward(t, carry):
        act_grad = dot(out_branch_two[...], full[t, :, of_down])
        pre_grad[t] = (act_grad * slope[t]).astype(bf16)
        bias_sums[pl.ds(t, 1)] = total(pre_grad[t].astype(f32))
        keep_two[...] += dot_nt(pre_grad[t], full[t, :, of_up])
        return carry

    lax.fori_loop(0, GROUP, backward, 0)
    hidden_grad = keep_two[...]
    residual = tokens[...].astype(f32) + gate_one * keep_one[...]
    normed, inverse = normalize(residual)
    sums[0:1] = total(hidden_grad)
    sums[1:2] = total(hidden_grad * normed)
    grad = upstream[...].astype(f32) + norm_back(
        hidden_grad * gain * (1.0 + scale), normed, inverse
    )
    residual_grad[...] = grad
    sums[3:4] = total(grad * keep_one[...])
    out_branch_one[...] = (gate_one * grad).astype(bf16)
    for r in range(GROUP):
        back = dot(out_branch_one[...], full[r, :, of_out])
        mixture_grads[r] = back.astype(bf16).T


def feed(where, tokens, upstream, vectors, mixtures, pieces):
    rows, width = tokens.shape
    wide = mixtures.shape[1]
    columns = pieces[0].shape[2]
    hidden = width

    def shape(dtype, *lengths):
        return jax.ShapeDtypeStruct(lengths, dtype)

    shapes = [
        shape(bf16, rows, width),
        shape(f32, rows, width),
        shape(bf16, rows, width),
        shape(bf16, rows, width),
        shape(bf16, rows, width),
        shape(bf16, GROUP, rows, hidden),
        shape(bf16, GROUP, rows, hidden),
        shape(bf16, GROUP, rows, wide),
        shape(f32, 5, width),
        shape(f32, GROUP, hidden),
        shape(bf16, GROUP, wide, rows),
    ]
    return pl.pallas_call(
        functools.partial(feed_kernel, len(pieces)),
        out_shape=shapes,
        grid=(1,),
        in_specs=[SMEM]
        + [whole(x) for x in (tokens, upstream, vectors, mixtures)]
        + [ANY] * len(pieces),
        out_specs=[whole(x) for x in shapes],
        scratch_shapes=[
            pltpu.VMEM((GROUP, width, columns), bf16),
            pltpu.VMEM((GROUP, hidden), f32),
            pltpu.VMEM((GROUP, rows, hidden), f32),
            pltpu.VMEM((rows, width), f32),
            pltpu.VMEM((rows, width), f32),
            pltpu.SemaphoreType.DMA((GROUP * len(pieces),)),
        ],
        compiler_params=pltpu.CompilerParams(vmem_limit_bytes=60 << 20),
        cost_estimate=pl.CostEstimate(
            flops=4 * rows * width * GROUP * columns,
            bytes_accessed=2 * GROUP * (width + rows) * columns,
            transcendentals=GROUP * rows * hidden,
        ),
        name="feed",
    )(where, tokens, upstream, vectors, mixtures, *pieces)


def feed_grads_kernel(hidden, branch_one, branch_two, act, pre, attention, sums, out):
    t = pl.program_id(0)
    up = dot(hidden[...].T, pre[0]).astype(bf16)
    down = dot(branch_two[...].T, act[0]).astype(bf16)
    own = dot(branch_one[...].T, attention[0]).astype(bf16)
    line = lax.broadcasted_iota(jnp.int32, (8, 1), 0)
    lines = jnp.where(line == 0, sums[pl.ds(t, 1)], 0.0)
    for n in (1, 2):
        lines = jnp.where(line == n, sums[3 + n : 4 + n], lines)
    lines = jnp.concatenate([lines, jnp.zeros((120, lines.shape[1]), f32)])
    extra = lines.T[:, :64].astype(bf16)
    value = jnp.concatenate([own, up, down, extra], axis=1)
    if len(out.shape) == 3:
        out[0] = value
    else:
        out[...] = value.reshape(out.shape)


def feed_grads(dp_size, hidden, branch_one, branch_two, act, pre, attention, sums):
    rows, width = hidden.shape
    wide, inner = attention.shape[2], act.shape[2]
    columns = wide + 2 * inner + 64
    if dp_size == 8:
        shape = (dp_size, GROUP, width // dp_size, columns)
        out_spec = pl.BlockSpec((dp_size, 1, width // dp_size, columns), lambda t: (0, t, 0, 0))
    else:
        shape = (GROUP, width, columns)
        out_spec = pl.BlockSpec((1, width, columns), lambda t: (t, 0, 0))
    return pl.pallas_call(
        feed_grads_kernel,
        out_shape=jax.ShapeDtypeStruct(shape, bf16),
        grid=(GROUP,),
        in_specs=[whole(hidden)] * 3
        + [pl.BlockSpec((1, rows, inner), lambda t: (t, 0, 0))] * 2
        + [pl.BlockSpec((1, rows, wide), lambda t: (t, 0, 0)), whole(sums)],
        out_specs=out_spec,
        compiler_params=pltpu.CompilerParams(vmem_limit_bytes=60 << 20),
        cost_estimate=pl.CostEstimate(
            flops=2 * rows * width * GROUP * columns,
            bytes_accessed=2 * GROUP * (width + rows) * columns,
            transcendentals=0,
        ),
        name="feed_grads",
    )(hidden, branch_one, branch_two, act, pre, attention, sums)


def join_heads(received, i):
    return jnp.concatenate(
        [ref[i, c * HEAD_DIM : (c + 1) * HEAD_DIM] for c in range(3) for ref in received]
    )


def project_grads_kernel(heads, where, hidden, *refs):
    received, outs = refs[:heads], refs[heads:]
    me = where[0]
    for parity in range(2):

        @pl.when(me % 2 == parity)
        def _():
            hidden_t = hidden[...].T
            for i in range(GROUP):
                value = dot_nt(hidden_t, join_heads(received, i)).astype(bf16)
                store_blocks(me, parity, outs, i, value)


def project_grads(dp_size, where, hidden, received):
    rows, width = hidden.shape
    heads = len(received)
    columns = 3 * heads * HEAD_DIM
    shapes = grad_shapes(dp_size, width, columns)
    return pl.pallas_call(
        functools.partial(project_grads_kernel, heads),
        out_shape=shapes,
        grid=(1,),
        in_specs=[SMEM] + [whole(x) for x in (hidden, *received)],
        out_specs=[whole(x) for x in shapes],
        compiler_params=pltpu.CompilerParams(vmem_limit_bytes=32 << 20),
        cost_estimate=pl.CostEstimate(
            flops=2 * rows * width * GROUP * columns,
            bytes_accessed=2 * GROUP * (width + rows) * columns,
            transcendentals=0,
        ),
        name="project_grads",
    )(where, hidden, *received)


def project_back_kernel(count, heads, *refs):
    where, tokens, vectors, residual_grad = refs[:4]
    received, refs = refs[4 : 4 + heads], refs[4 + heads :]
    pieces, (input_grad, sums, full, sems) = refs[:count], refs[count:]
    me, z = where[0], where[1]
    copies = load_weights(me, pieces, full, sems)
    gain, scale = vectors[GAIN_ONE], vectors[SCALE_ONE]
    normed, inverse = normalize(tokens[...].astype(f32))
    for copy in copies:
        copy.wait()
    hidden_grad = None
    for i in range(GROUP):
        term = dot_nt(join_heads(received, i).T, full[z ^ i])
        hidden_grad = term if hidden_grad is None else hidden_grad + term
    sums[0:1] = total(hidden_grad)
    sums[1:2] = total(hidden_grad * normed)
    input_grad[...] = (
        residual_grad[...] + norm_back(hidden_grad * gain * (1.0 + scale), normed, inverse)
    ).astype(bf16)


def project_back(where, tokens, vectors, residual_grad, received, pieces):
    rows, width = tokens.shape
    columns = pieces[0].shape[2]
    shapes = [
        jax.ShapeDtypeStruct((rows, width), bf16),
        jax.ShapeDtypeStruct((2, width), f32),
    ]
    return pl.pallas_call(
        functools.partial(project_back_kernel, len(pieces), len(received)),
        out_shape=shapes,
        grid=(1,),
        in_specs=[SMEM]
        + [whole(x) for x in (tokens, vectors, residual_grad, *received)]
        + [ANY] * len(pieces),
        out_specs=[whole(x) for x in shapes],
        scratch_shapes=[
            pltpu.VMEM((GROUP, width, columns), bf16),
            pltpu.SemaphoreType.DMA((GROUP * len(pieces),)),
        ],
        compiler_params=pltpu.CompilerParams(vmem_limit_bytes=32 << 20),
        cost_estimate=pl.CostEstimate(
            flops=2 * rows * width * GROUP * columns,
            bytes_accessed=2 * GROUP * (width + rows) * columns,
            transcendentals=0,
        ),
        name="project_back",
    )(where, tokens, vectors, residual_grad, *received, *pieces)


def einsum(spec, a, b):
    return jnp.einsum(spec, a, b, preferred_element_type=f32)


def per_device(
    dp_size,
    tokens,
    time_embed,
    ada_weight,
    ada_bias,
    norm1_gain,
    qkv_weight,
    out_weight,
    norm2_gain,
    up_weight,
    up_bias,
    down_weight,
    down_bias,
    out_grad,
):
    me = lax.axis_index(DP)
    z = lax.axis_index(TENSOR)
    position = lax.axis_index(TEAM)
    where = jnp.stack([me, z]).astype(jnp.int32)
    rows, width = tokens.shape
    heads = qkv_weight.shape[2] // HEAD_DIM
    wide = heads * HEAD_DIM
    hidden = up_weight.shape[1]
    cond = time_embed.shape[1]
    per = norm1_gain.shape[0]

    first_shard = jnp.concatenate([*qkv_weight], axis=1)
    packs = pack(ada_weight, ada_bias, time_embed, norm1_gain, norm2_gain, down_bias)
    packs, *others = meet(first_step(packs, dp_size), *send_planes(first_shard, dp_size))
    packs = spread_dp(packs, dp_size)
    first_own = jnp.stack([first_shard, *others])
    extra = jnp.pad(up_bias[:, None], ((0, 0), (0, 63)))
    second_shard = jnp.concatenate([out_weight.T, up_weight, down_weight.T, extra], axis=1)
    tokens, first_own = meet(tokens, first_own)
    sent = send_tokens(tokens, dp_size)
    first_pieces = gather_weights(first_own, gather_sides(first_own, dp_size), dp_size)
    moved = settle(tokens, sent)
    second_own = lax.all_gather(second_shard, TENSOR, axis=0, tiled=False)

    columns = ada_weight.shape[1]
    vectors, embeds = prepare(where, packs, width, per, cond)
    ada_full = packs[:, :cond, :columns]
    gain_one, gain_two = vectors[GAIN_ONE], vectors[GAIN_TWO]
    scale_one, scale_two = vectors[SCALE_ONE], vectors[SCALE_TWO]

    frequency = jnp.exp(
        jnp.arange(HALF, dtype=f32) * (-2.0 * math.log(ROPE_BASE) / HEAD_DIM)
    )
    angles = frequency[:, None] * jnp.arange(GROUP * rows, dtype=jnp.int32).astype(f32)[None, :]
    cosine, sine = jnp.cos(angles), jnp.sin(angles)
    cosine_own = lax.dynamic_slice_in_dim(cosine, position * rows, rows, axis=1)
    sine_own = lax.dynamic_slice_in_dim(sine, position * rows, rows, axis=1)

    cosine_own, second_own = meet(cosine_own, second_own)
    second_sides = gather_sides(second_own, dp_size)
    hidden_one, packed = project(where, moved, vectors, cosine_own, sine_own, first_pieces)
    packed = exchange(packed)
    out_grad, packed = meet(out_grad, packed)
    upstream = send_tokens(out_grad, dp_size)
    mixtures, lse = attend(packed)
    lse, *second_sides = meet(lse, *second_sides)
    second_pieces = gather_weights(second_own, second_sides, dp_size)
    mixtures, upstream = meet(mixtures, upstream)
    upstream = settle(out_grad, upstream)
    mixtures = exchange(mixtures)

    outs = feed(where, moved, upstream, vectors, mixtures, second_pieces)
    output, residual_grad, hidden_two, branch_one_grad, branch_two_grad = outs[:5]
    activated, pre_grad, attention, feed_sums, bias_sums, mixture_grads = outs[5:]
    incoming = exchange(mixture_grads)
    sums_two = jnp.concatenate(
        [bias_sums, feed_sums[1:2] * (1.0 + scale_two), feed_sums[4:5]]
    )
    second_grad = feed_grads(
        dp_size,
        hidden_two,
        branch_one_grad,
        branch_two_grad,
        activated,
        pre_grad,
        attention,
        jnp.pad(sums_two, ((0, 2), (0, 0))),
    )
    incoming, second_grad, output = meet(incoming, second_grad, output)
    output = regroup(output, dp_size)
    if dp_size == 8:
        second_sum = lax.psum_scatter(second_grad, DP, scatter_dimension=0, tiled=False)
    else:
        second_sum = lax.psum_scatter(second_grad, DP, scatter_dimension=1, tiled=True)

    received = []
    for h in range(heads):
        received.append(exchange(attend_back(h, packed, incoming, lse, cosine, sine)))
        if h == 0:
            incoming, output = meet(incoming, output)
    first_grad = list(project_grads(dp_size, where, hidden_one, received))
    first_far = reduce_cores(first_grad, dp_size)
    if dp_size == 8:
        first_diagonal = reduce_diagonal(first_grad, first_far, dp_size)
        *received, first_diagonal, second_sum = meet(*received, first_diagonal, second_sum)
        first_half = reduce_first(first_diagonal, dp_size)
    input_grad, project_sums = project_back(
        where, moved, vectors, residual_grad, received, first_pieces
    )
    sent = send_tokens(input_grad, dp_size)
    pull_one, pull_two = project_sums[1:2], feed_sums[1:2]
    mine = jnp.concatenate(
        [
            project_sums[:1],
            pull_one * gain_one,
            feed_sums[3:4],
            feed_sums[:1],
            pull_two * gain_two,
            feed_sums[2:3],
            pull_one * (1.0 + scale_one),
        ]
    )
    second_sum = lax.psum_scatter(second_sum, TENSOR, scatter_dimension=0, tiled=False)
    second_sum = second_sum.astype(f32)

    def widen(mods, swap, mask):
        return jnp.concatenate([mods, swap(mods, dp_size, mask)])

    mods = mine[None]
    mask = 2
    while mask < dp_size:
        mods = widen(mods, swap_dp, mask)
        mask *= 2
    mods = mods + swap_dp(mods, dp_size, 1)
    first_sides = None
    if dp_size == 8:
        first_sides = reduce_sides(first_grad, first_far, first_half, dp_size)
    first_sum = reduce_second(first_grad, first_far, first_sides, dp_size)
    mods, first_sum, second_sum = meet(mods, first_sum, second_sum)
    first_sum = reduce_planes(first_sum)
    mods = mods + swap_z(mods, dp_size, 1)
    mods = mods.at[:, :6].set(mods[:, :6].astype(bf16).astype(f32))
    mods = widen(mods, swap_z, 2)
    tail = jnp.sum(mods[:, 6:], axis=0)
    mods = mods[:, :6]
    input_grad = settle(input_grad, sent)
    out_out = second_sum[:, :wide].T
    up_out = second_sum[:, wide : wide + hidden]
    down_out = second_sum[:, wide + hidden : wide + 2 * hidden].T
    bias_up_out, gain_two_out, bias_down_out = second_sum[:, wide + 2 * hidden :].T[:3]
    qkv_out = jnp.stack(jnp.split(first_sum, 3, axis=1))

    rel = jnp.arange(dp_size)
    quads = dp_size // 2
    seq_at = (me // 2 ^ rel % quads) * 2 + (z // 2 ^ rel // quads)
    mods = mods.reshape(dp_size, 6 * width).astype(bf16)
    own_mods = lax.dynamic_slice_in_dim(mods, me * columns, columns, axis=1)
    pick = (seq_at[:, None] == jnp.arange(dp_size)[None, :]).astype(bf16)
    ada_out = einsum("sc,se->ce", jnp.dot(pick, embeds.astype(bf16)), own_mods)
    ada_bias_out = jnp.sum(own_mods.astype(f32), axis=0)
    mine_at = (seq_at == me).astype(f32)
    own_row = jnp.sum(mods.astype(f32) * mine_at[:, None], axis=0).astype(bf16)
    own_row = reorder(own_row.reshape(dp_size, columns), me)
    time_out = jnp.sum(einsum("oe,oce->oc", own_row, ada_full), axis=0, keepdims=True)

    def own_part(row):
        return lax.dynamic_slice_in_dim(row, me * per, per)

    return (
        output,
        input_grad,
        time_out,
        ada_out,
        ada_bias_out,
        own_part(tail[0]),
        qkv_out,
        out_out,
        gain_two_out,
        up_out,
        bias_up_out,
        down_out,
        bias_down_out,
    )


def solution(mesh):
    dp_size, tensor_size = mesh.shape["dp"], mesh.shape["tensor"]
    parts = jax.sharding.Mesh(
        mesh.devices.reshape(dp_size // 2, 2, tensor_size // 2, 2), AXES
    )
    in_specs = (
        P(AXES, None),
        P(DP, None),
        P(None, DP),
        P(DP),
        P(DP),
        P(None, DP, TENSOR),
        P(TENSOR, DP),
        P(DP),
        P(DP, TENSOR),
        P(TENSOR + DP),
        P(TENSOR, DP),
        P(DP),
        P(AXES, None),
    )
    out_specs = (
        P(AXES, None),
        P(AXES, None),
        P(DP, None),
        P(None, DP),
        P(DP),
        P(DP),
        P(None, DP, TENSOR),
        P(TENSOR, DP),
        P(DP),
        P(DP, TENSOR),
        P(TENSOR + DP),
        P(TENSOR, DP),
        P(DP),
    )
    return jax.shard_map(
        functools.partial(per_device, dp_size),
        mesh=parts,
        in_specs=in_specs,
        out_specs=out_specs,
        check_vma=False,
    )
```

time: 398 us -> 394 us (0.990)
  blocking collectives: 0 us -> 15.5 us
  waiting for transfers between devices: 96.7 us -> 85.5 us
  Pallas kernels: 113 us -> 124 us
  starting transfers between devices: 99.6 us -> 90.1 us
  local copies, waits for them, and re-layouts: 41.6 us -> 36.5 us
    ppermute x64 -> x38, starting transfers between devices: 99 us -> 58 us  [permute(): return lax.ppermute(array, AXES, pairs)]
    ppermute x64 -> x38, waiting for transfers between devices: 96.7 us -> 59 us  [permute(): return lax.ppermute(array, AXES, pairs)]
    all_to_all x0 -> x6, starting transfers between devices: none -> 31.9 us  [the longest x5 23.3 us: exchange(): return lax.all_to_all(blocks, TEAM, 0, 0, tiled=True)]
    all_to_all x0 -> x6, waiting for transfers between devices: none -> 26.4 us  [the longest x5 26.4 us: exchange(): return lax.all_to_all(blocks, TEAM, 0, 0, tiled=True)]
    all_to_all x0 -> x1, blocking collectives: none -> 15.5 us  [exchange(): return lax.all_to_all(blocks, TEAM, 0, 0, tiled=True)]
    unnamed x158 -> x82, local copies, waits for them, and re-layouts: 28 us -> 19 us
    pallas_call x10, Pallas kernels: 104 us -> 112 us  [the longest x3 39.8 us: attend_back(): pl.pallas_call(attend_back_kernel, out_shape=jax.ShapeDtypeStruct((count,...]
    another operation x9 -> x7, other arithmetic: 7.98 us -> 1.73 us  [the longest x2 3.7 us: gather_dp(): blocks = jnp.stack([blocks, swap_dp(blocks, dp_size, 1)], axis=1)]
  transfers between devices with their start and end apart: 67 -> 47, of which waited for: 23 -> 14; matrix products, arithmetic and copies ran while one was open for 9% -> 10% of each run, Pallas kernels for 19% -> 23%
where the time goes in v4:
time: 394 us; the launch traced here: 386 us
  Pallas kernels  124 us (31%)
  starting transfers between devices  90.1 us (23%)
  waiting for transfers between devices  85.5 us (22%)
  local copies, waits for them, and re-layouts  36.5 us (9%)
  other arithmetic  17.5 us (4%)
  blocking collectives  15.5 us (4%)
  between operations  14.9 us (4%)
    ppermute x38, waiting for transfers between devices, permute(): return lax.ppermute(array, AXES, pairs)  59 us
    ppermute x38, starting transfers between devices, permute(): return lax.ppermute(array, AXES, pairs)  58 us
    pallas_call x3, Pallas kernels, attend_back(): pl.pallas_call(attend_back_kernel, out_shape=jax.ShapeDtypeStruct((count,...  39.8 us
    pallas_call x1, Pallas kernels, feed(): pl.pallas_call(functools.partial(feed_kernel, len(pieces)), out_shape=sha...  29.6 us
    all_to_all x5, waiting for transfers between devices, exchange(): return lax.all_to_all(blocks, TEAM, 0, 0, tiled=True)  26.4 us
    all_to_all x5, starting transfers between devices, exchange(): return lax.all_to_all(blocks, TEAM, 0, 0, tiled=True)  23.3 us
    pallas_call x1, Pallas kernels, attend(): pl.pallas_call(attend_kernel, out_shape=[jax.ShapeDtypeStruct((count, hea...  21.7 us
    unnamed x82, local copies, waits for them, and re-layouts  19 us
  transfers between devices with their start and end apart: 47, of which 14 were waited for; matrix products, arithmetic and copies ran while one was open for 10% of the time, Pallas kernels for 23%

profile of v4, /device:TPU:0, one launch (start us, length us, event | category | flops | bytes accessed | tf_op | source)
XLA Modules:
  0.0 385.8 jit_solution(9535216329527815486)
XLA Ops:
  8.3 3.1 collective-permute-start.1
  11.4 2.6 collective-permute-start.2
  30.1 6.2 %collective-permute-done.5 = bf16[2,144,576]{2,1,0:T(8,128)(2,1)S(1)} collective-permute-done((bf16[2,144,576]{2,1,0:T(8,128)(2,1)S(1)}, bf16[2,144,576]{2,1,0:T(8,128)(2,1)S(1)}, u32[]{:S(2)}, u32[]{:S(2)}) %collective-permute-start.5) | collective-permute-done | bytes 331808 | tf_op jit(solution)/shard_map/ppermute | solution.py:40
  39.1 7.8 %collective-permute-done.8.refs_7_.refs_9_ = bf16[4,96,576]{2,1,0:T(8,128)(2,1)} collective-permute-done((bf16[4,96,576]{2,1,0:T(8,128)(2,1)S(1)}, bf16[4,96,576]{2,1,0:T(8,128)(2,1)}, u32[]{:S(2)}, u32[]{:S(2)}) %collective-permute-start.8) | collective-permute-done | bytes 442400 | tf_op jit(solution)/shard_map/ppermute | solution.py:40
  51.0 3.2 collective-permute-done.10.refs_9_.refs_11_
  54.3 18.3 %collective-permute-start.14 = (bf16[2,96,576]{2,1,0:T(8,128)(2,1)S(1)}, bf16[2,96,576]{2,1,0:T(8,128)(2,1)}, u32[]{:S(2)}, u32[]{:S(2)}) collective-permute-start(bf16[2,96,576]{2,1,0:T(8,128)(2,1)S(1)} %collective-permute-done.9.refs_8_.refs_10_), channel_id=1, source_target_pairs={{0,4},{1,5},{2,6},{3,7},{4,0},{5,1},{6,2},{7,3},{8,12},{9,13},{10,... | collective-permute-start | bytes 663560 | tf_op jit(solution)/shard_map/ppermute | solution.py:40
  74.2 2.6 prepare.1
  78.7 5.8 %project.1 = (bf16[512,768]{1,0:T(8,128)(2,1)S(1)}, bf16[4,576,512]{2,1,0:T(8,128)(2,1)S(1)}) custom-call(s32[2]{0:T(128)S(1)} %pad_add_fusion.where.refs_0_, bf16[512,768]{1,0:T(8,128)(2,1)S(1)} %broadcast_select_fusion.3.refs_1_, f32[16,768]{1,0:T(8,128)S(1)} %get-tuple-element.79.refs_2_.refs_3_, f32[32,512]{1,0:T(8,128)S(1)} %copy-done.17, ...), custom_call_target="tpu_custom_call" | custom-call | flops 1811939328 | bytes 5898240 | tf_op jit(solution)/shard_map/project/pallas_call | solution.py:459
  86.8 4.7 %all-to-all-start = ((bf16[4,576,512]{2,1,0:T(8,128)(2,1)}), bf16[4,576,512]{2,1,0:T(8,128)(2,1)}, u32[]{:S(2)}, u32[]{:S(2)}) async-start(bf16[4,576,512]{2,1,0:T(8,128)(2,1)} %copy-done.6), calls=%async_computation | async-start | bytes 4718592 | tf_op jit(solution)/shard_map/all_to_all | solution.py:69
  93.6 26.4 %all-to-all-done.packed = bf16[4,576,512]{2,1,0:T(8,128)(2,1)} async-done(((bf16[4,576,512]{2,1,0:T(8,128)(2,1)}), bf16[4,576,512]{2,1,0:T(8,128)(2,1)}, u32[]{:S(2)}, u32[]{:S(2)}) %all-to-all-start) | async-done | bytes 2359328 | tf_op jit(solution)/shard_map/all_to_all | solution.py:69
  120.9 21.7 %attend.1 = (bf16[4,192,512]{2,1,0:T(8,128)(2,1)}, f32[3,4,512]{2,1,0:T(4,128)S(1)}) custom-call(bf16[4,576,512]{2,1,0:T(8,128)(2,1)} %all-to-all-done.packed), custom_call_target="tpu_custom_call" | custom-call | flops 12884901888 | bytes 3145728 | tf_op jit(solution)/shard_map/attend/pallas_call | solution.py:224
  149.4 3.0 collective-permute-start.22
  152.4 4.5 %all-to-all-start.1 = ((bf16[4,192,512]{2,1,0:T(8,128)(2,1)}), bf16[4,192,512]{2,1,0:T(8,128)(2,1)}, u32[]{:S(2)}, u32[]{:S(2)}) async-start(bf16[4,192,512]{2,1,0:T(8,128)(2,1)} %get-tuple-element.87), calls=%async_computation.1 | async-start | bytes 1572864 | tf_op jit(solution)/shard_map/all_to_all | solution.py:69
  156.9 5.4 %collective-permute-done.19.refs_8_ = bf16[2,96,1792]{2,1,0:T(8,128)(2,1)} collective-permute-done((bf16[2,96,1792]{2,1,0:T(8,128)(2,1)}, bf16[2,96,1792]{2,1,0:T(8,128)(2,1)}, u32[]{:S(2)}, u32[]{:S(2)}) %collective-permute-start.19) | collective-permute-done | bytes 688160 | tf_op jit(solution)/shard_map/ppermute | solution.py:40
  169.7 29.6 %feed.1 = (bf16[512,768]{1,0:T(8,128)(2,1)}, f32[512,768]{1,0:T(8,128)}, bf16[512,768]{1,0:T(8,128)(2,1)}, bf16[512,768]{1,0:T(8,128)(2,1)}, bf16[512,768]{1,0:T...) custom-call(s32[2]{0:T(128)} %copy-done.19, ...), custom_call_target="tpu_custom_call" | custom-call | flops 11274289152 | bytes 18350080 | tf_op jit(solution)/shard_map/feed/pallas_call | solution.py:584
  199.4 3.6 all-to-all-start.2
  205.0 11.6 %feed_grads.1 = bf16[8,4,96,1792]{3,2,1,0:T(8,128)(2,1)} custom-call(bf16[512,768]{1,0:T(8,128)(2,1)} %get-tuple-element.93.hidden, bf16[512,768]{1,0:T(8,128)(2,1)} %get-tuple-element.94.branch_one, bf16[512,768]{1,0:T(8,128)(2,1)} %get-tuple-element.95.branch_two, bf16[4,512,768]{2,1,0:T(8,128)(2,1)} %get-tuple-element.96.act, ...), custom_call_target="tpu_custom_call" | custom-call | flops 5637144576 | bytes 18350080 | tf_op jit(solution)/shard_map/feed_grads/pallas_call | solution.py:638
  220.1 13.3 %attend_back.3 = bf16[4,192,512]{2,1,0:T(8,128)(2,1)} custom-call(bf16[4,576,512]{2,1,0:T(8,128)(2,1)} %all-to-all-done.packed, bf16[4,192,512]{2,1,0:T(8,128)(2,1)} %copy-done.30, f32[3,4,512]{2,1,0:T(4,128)} %copy-done.23, f32[32,2048]{1,0:T(8,128)} %copy-done.33, f32[32,2048]{1,0:T(8,128)} %copy-done.32), custom_call_target="tpu_custom_call" | custom-call | flops 10737418240 | bytes 2097152 | tf_op jit(solution)/shard_map/attend_back/pallas_call | solution.py:297
  233.4 3.7 all-to-all-start.3
  238.1 13.2 %attend_back.5 = bf16[4,192,512]{2,1,0:T(8,128)(2,1)} custom-call(bf16[4,576,512]{2,1,0:T(8,128)(2,1)} %all-to-all-done.packed, bf16[4,192,512]{2,1,0:T(8,128)(2,1)} %copy-done.30, f32[3,4,512]{2,1,0:T(4,128)} %copy-done.23, f32[32,2048]{1,0:T(8,128)} %copy-done.33, f32[32,2048]{1,0:T(8,128)} %copy-done.32), custom_call_target="tpu_custom_call" | custom-call | flops 10737418240 | bytes 2097152 | tf_op jit(solution)/shard_map/attend_back/pallas_call | solution.py:297
  251.3 6.8 %all-to-all-start.5 = ((bf16[4,192,512]{2,1,0:T(8,128)(2,1)}), bf16[4,192,512]{2,1,0:T(8,128)(2,1)S(1)}, u32[]{:S(2)}, u32[]{:S(2)}) async-start(bf16[4,192,512]{2,1,0:T(8,128)(2,1)} %attend_back.5), calls=%async_computation.5 | async-start | bytes 1572864 | tf_op jit(solution)/shard_map/all_to_all | solution.py:69
  258.4 13.2 %attend_back.4 = bf16[4,192,512]{2,1,0:T(8,128)(2,1)} custom-call(bf16[4,576,512]{2,1,0:T(8,128)(2,1)} %all-to-all-done.packed, bf16[4,192,512]{2,1,0:T(8,128)(2,1)} %copy-done.30, f32[3,4,512]{2,1,0:T(4,128)} %copy-done.23, f32[32,2048]{1,0:T(8,128)} %copy-done.33, f32[32,2048]{1,0:T(8,128)} %copy-done.32), custom_call_target="tpu_custom_call" | custom-call | flops 10737418240 | bytes 2097152 | tf_op jit(solution)/shard_map/attend_back/pallas_call | solution.py:297
  271.6 15.5 %all_to_all.35.refs_1_.refs_5_ = bf16[4,192,512]{2,1,0:T(8,128)(2,1)S(1)} all-to-all(bf16[4,192,512]{2,1,0:T(8,128)(2,1)} %attend_back.4), channel_id=1, replica_groups=mesh['quad'=4,'core'=2,'high'=2,'low'=2] {'core','low'}, dimensions={0} | all-to-all | bytes 1572864 | tf_op jit(solution)/shard_map/all_to_all | solution.py:69
  287.2 4.8 %project_grads.1 = (bf16[4,4,96,576]{3,2,1,0:T(8,128)(2,1)S(1)}, bf16[4,4,96,576]{3,2,1,0:T(8,128)(2,1)}) custom-call(s32[2]{0:T(128)S(1)} %copy-done.20, bf16[512,768]{1,0:T(8,128)(2,1)S(1)} %copy-done.22, bf16[4,192,512]{2,1,0:T(8,128)(2,1)S(1)} %all-to-all-done.3.refs_0_.refs_4_, bf16[4,192,512]{2,1,0:T(8,128)(2,1)S(1)} %all_to_all.35.refs_1_.refs_5_, ...), custom_call_target="tpu_custom_call" | custom-call | flops 1811939328 | bytes 5898240 | tf_op jit(solution)/shard_map/project_grads/pallas_call | solution.py:680
  293.3 4.3 %collective-permute-done.27 = bf16[4,4,96,576]{3,2,1,0:T(8,128)(2,1)} collective-permute-done((bf16[4,4,96,576]{3,2,1,0:T(8,128)(2,1)}, bf16[4,4,96,576]{3,2,1,0:T(8,128)(2,1)}, u32[]{:S(2)}, u32[]{:S(2)}) %collective-permute-start.27) | collective-permute-done | bytes 1769504 | tf_op jit(solution)/shard_map/ppermute | solution.py:40
  297.7 3.3 convert_add_fusion.1
  310.5 6.1 %project_back.1 = (bf16[512,768]{1,0:T(8,128)(2,1)S(1)}, f32[2,768]{1,0:T(2,128)S(1)}) custom-call(s32[2]{0:T(128)S(1)} %copy-done.20, bf16[512,768]{1,0:T(8,128)(2,1)S(1)} %copy-done.1, f32[16,768]{1,0:T(8,128)S(1)} %copy-done.16, f32[512,768]{1,0:T(8,128)S(1)} %copy-done.8, bf16[4,192,512]{2,1,0:T(8,128)(2,1)S(1)} %all-to-all-done.3.refs_0_.refs_4_, ...), custom_call_target="tpu_custom_call" | custom-call | flops 1811939328 | bytes 5898240 | tf_op jit(solution)/shard_map/project_back/pallas_call | solution.py:724
  331.0 7.8 %collective-permute-done.33 = bf16[4,96,576]{2,1,0:T(8,128)(2,1)S(1)} collective-permute-done((bf16[4,96,576]{2,1,0:T(8,128)(2,1)S(1)}, bf16[4,96,576]{2,1,0:T(8,128)(2,1)S(1)}, u32[]{:S(2)}, u32[]{:S(2)}) %collective-permute-start.33) | collective-permute-done | bytes 442400 | tf_op jit(solution)/shard_map/ppermute | solution.py:40
  338.7 2.5 collective-permute-done.35
  346.9 8.6 %all-to-all-start.6 = ((bf16[4,96,576]{2,1,0:T(8,128)(2,1)}), bf16[4,96,576]{2,1,0:T(8,128)(2,1)S(1)}, u32[]{:S(2)}, u32[]{:S(2)}) async-start(bf16[4,96,576]{2,1,0:T(8,128)(2,1)} %fusion.8), calls=%async_computation.8 | async-start | bytes 983040 | tf_op jit(solution)/shard_map/all_to_all | solution.py:198
  356.5 3.0 collective-permute-start.37
  360.2 13.6 %collective-permute-done.37 = f32[4,7,768]{2,1,0:T(8,128)S(1)} collective-permute-done((f32[4,7,768]{2,1,0:T(8,128)S(1)}, f32[4,7,768]{2,1,0:T(8,128)S(1)}, u32[]{:S(2)}, u32[]{:S(2)}) %collective-permute-start.37) | collective-permute-done | bytes 86048 | tf_op jit(solution)/shard_map/ppermute | solution.py:40
  (236 shorter events, 90.8 us)
Async XLA Ops:
  7.2 69.7 %all-gather.3.cloned.1.call-start = ((), (), s32[]{:S(2)}) async-start(), calls=%async_computation.11 | async-start | bytes 1720320 | tf_op jit(solution)/shard_map/all_gather | solution.py:788
  8.3 16.4 %collective-permute-start.1 = (bf16[96,576]{1,0:T(8,128)(2,1)S(1)}, bf16[96,576]{1,0:T(8,128)(2,1)S(1)}, u32[]{:S(2)}, u32[]{:S(2)}) collective-permute-start(bf16[96,576]{1,0:T(8,128)(2,1)S(1)} %pad_maximum_fusion.6), channel_id=1, source_target_pairs={{0,1},{1,0},{2,3},{3,2},{4,5},{5,4},{6,7},{7,6},{8,9},{9,8},{10,11... | collective-permute-start | bytes 331784 | tf_op jit(solution)/shard_map/ppermute | solution.py:40
  11.4 13.3 %collective-permute-start.2 = (bf16[96,576]{1,0:T(8,128)(2,1)S(1)}, bf16[96,576]{1,0:T(8,128)(2,1)S(1)}, u32[]{:S(2)}, u32[]{:S(2)}) collective-permute-start(bf16[96,576]{1,0:T(8,128)(2,1)S(1)} %pad_maximum_fusion.6), channel_id=1, source_target_pairs={{0,2},{1,3},{2,0},{3,1},{4,6},{5,7},{6,4},{7,5},{8,10},{9,11},{10,... | collective-permute-start | bytes 331784 | tf_op jit(solution)/shard_map/ppermute | solution.py:40
  28.0 18.9 %collective-permute-start.8 = (bf16[4,96,576]{2,1,0:T(8,128)(2,1)S(1)}, bf16[4,96,576]{2,1,0:T(8,128)(2,1)}, u32[]{:S(2)}, u32[]{:S(2)}) collective-permute-start(bf16[4,96,576]{2,1,0:T(8,128)(2,1)S(1)} %pad_maximum_fusion.1.refs_5_.refs_7_), channel_id=1, source_target_pairs={{0,16},{1,17},{2,18},{3,19},{4,20},{5,21},{6,22},{7,23},{8,24},{9,... | collective-permute-start | bytes 1327112 | tf_op jit(solution)/shard_map/ppermute | solution.py:40
  28.5 25.8 %collective-permute-start.4 = (bf16[512,768]{1,0:T(8,128)(2,1)S(1)}, bf16[512,768]{1,0:T(8,128)(2,1)}, u32[]{:S(2)}, u32[]{:S(2)}) collective-permute-start(bf16[512,768]{1,0:T(8,128)(2,1)S(1)} %copy-done.27), channel_id=1, source_target_pairs={{2,4},{3,5},{4,2},{5,3},{10,12},{11,13},{12,10},{13,11},{18,20},{1... | collective-permute-start | bytes 2359304 | tf_op jit(solution)/shard_map/ppermute | solution.py:40
  36.3 36.3 %collective-permute-start.6 = (bf16[4,144,576]{2,1,0:T(8,128)(2,1)S(1)}, bf16[4,144,576]{2,1,0:T(8,128)(2,1)S(1)}, u32[]{:S(2)}, u32[]{:S(2)}) collective-permute-start(bf16[4,144,576]{2,1,0:T(8,128)(2,1)S(1)} %constant_dynamic-update-slice_fusion), channel_id=1, source_target_pairs={{0,4},{1,5},{2,6},{3,7},{4,0},{5,1},{6,2},{7,3},{8,12},{9,13},{10,... | collective-permute-start | bytes 1990664 | tf_op jit(solution)/shard_map/ppermute | solution.py:40
  50.5 26.4 %collective-permute-start.11 = (bf16[4,96,576]{2,1,0:T(8,128)(2,1)S(1)}, bf16[4,96,576]{2,1,0:T(8,128)(2,1)}, u32[]{:S(2)}, u32[]{:S(2)}) collective-permute-start(bf16[4,96,576]{2,1,0:T(8,128)(2,1)S(1)} %pad_maximum_fusion.1.refs_5_.refs_7_), channel_id=1, source_target_pairs={{0,4},{1,5},{2,6},{3,7},{4,0},{5,1},{6,2},{7,3},{8,12},{9,13},{10,... | collective-permute-start | bytes 1327112 | tf_op jit(solution)/shard_map/ppermute | solution.py:40
  50.5 26.5 %collective-permute-start.12 = (bf16[4,96,576]{2,1,0:T(8,128)(2,1)S(1)}, bf16[4,96,576]{2,1,0:T(8,128)(2,1)}, u32[]{:S(2)}, u32[]{:S(2)}) collective-permute-start(bf16[4,96,576]{2,1,0:T(8,128)(2,1)S(1)} %collective-permute-done.7.refs_6_.refs_8_), channel_id=1, source_target_pairs={{0,4},{1,5},{2,6},{3,7},{4,0},{5,1},{6,2},{7,3},{8,12},{9,13},{10,... | collective-permute-start | bytes 1327112 | tf_op jit(solution)/shard_map/ppermute | solution.py:40
  54.2 22.7 %collective-permute-start.13 = (bf16[4,96,576]{2,1,0:T(8,128)(2,1)}, bf16[4,96,576]{2,1,0:T(8,128)(2,1)}, u32[]{:S(2)}, u32[]{:S(2)}) collective-permute-start(bf16[4,96,576]{2,1,0:T(8,128)(2,1)} %collective-permute-done.8.refs_7_.refs_9_), channel_id=1, source_target_pairs={{0,4},{1,5},{2,6},{3,7},{4,0},{5,1},{6,2},{7,3},{8,12},{9,13},{10,... | collective-permute-start | bytes 1327112 | tf_op jit(solution)/shard_map/ppermute | solution.py:40
  54.3 22.6 %collective-permute-start.14 = (bf16[2,96,576]{2,1,0:T(8,128)(2,1)S(1)}, bf16[2,96,576]{2,1,0:T(8,128)(2,1)}, u32[]{:S(2)}, u32[]{:S(2)}) collective-permute-start(bf16[2,96,576]{2,1,0:T(8,128)(2,1)S(1)} %collective-permute-done.9.refs_8_.refs_10_), channel_id=1, source_target_pairs={{0,4},{1,5},{2,6},{3,7},{4,0},{5,1},{6,2},{7,3},{8,12},{9,13},{10,... | collective-permute-start | bytes 663560 | tf_op jit(solution)/shard_map/ppermute | solution.py:40
  86.8 33.2 %all-to-all-start = ((bf16[4,576,512]{2,1,0:T(8,128)(2,1)}), bf16[4,576,512]{2,1,0:T(8,128)(2,1)}, u32[]{:S(2)}, u32[]{:S(2)}) async-start(bf16[4,576,512]{2,1,0:T(8,128)(2,1)} %copy-done.6), calls=%async_computation | async-start | bytes 4718592 | tf_op jit(solution)/shard_map/all_to_all | solution.py:69
  91.5 51.8 %collective-permute-start.17 = (bf16[4,96,1792]{2,1,0:T(8,128)(2,1)}, bf16[4,96,1792]{2,1,0:T(8,128)(2,1)}, u32[]{:S(2)}, u32[]{:S(2)}) collective-permute-start(bf16[4,96,1792]{2,1,0:T(8,128)(2,1)} %bitcast.109), channel_id=1, source_target_pairs={{0,8},{1,9},{2,10},{3,11},{4,12},{5,13},{6,14},{7,15},{8,0},{9,1},... | collective-permute-start | bytes 4128776 | tf_op jit(solution)/shard_map/ppermute | solution.py:40
  92.1 51.2 %collective-permute-start.18 = (bf16[4,96,1792]{2,1,0:T(8,128)(2,1)}, bf16[4,96,1792]{2,1,0:T(8,128)(2,1)}, u32[]{:S(2)}, u32[]{:S(2)}) collective-permute-start(bf16[4,96,1792]{2,1,0:T(8,128)(2,1)} %bitcast.110), channel_id=1, source_target_pairs={{0,16},{1,17},{2,18},{3,19},{4,20},{5,21},{6,22},{7,23},{8,24},{9,... | collective-permute-start | bytes 4128776 | tf_op jit(solution)/shard_map/ppermute | solution.py:40
  93.6 75.0 %collective-permute-start.21 = (bf16[4,96,1792]{2,1,0:T(8,128)(2,1)}, bf16[4,96,1792]{2,1,0:T(8,128)(2,1)}, u32[]{:S(2)}, u32[]{:S(2)}) collective-permute-start(bf16[4,96,1792]{2,1,0:T(8,128)(2,1)} %bitcast.111), channel_id=1, source_target_pairs={{0,4},{1,5},{2,6},{3,7},{4,0},{5,1},{6,2},{7,3},{8,12},{9,13},{10,... | collective-permute-start | bytes 4128776 | tf_op jit(solution)/shard_map/ppermute | solution.py:40
  120.0 32.4 %collective-permute-start.16 = (bf16[512,768]{1,0:T(8,128)(2,1)S(1)}, bf16[512,768]{1,0:T(8,128)(2,1)S(1)}, u32[]{:S(2)}, u32[]{:S(2)}) collective-permute-start(bf16[512,768]{1,0:T(8,128)(2,1)S(1)} %copy-done.28), channel_id=1, source_target_pairs={{2,4},{3,5},{4,2},{5,3},{10,12},{11,13},{12,10},{13,11},{18,20},{1... | collective-permute-start | bytes 2359304 | tf_op jit(solution)/shard_map/ppermute | solution.py:40
  145.2 17.0 %collective-permute-start.19 = (bf16[2,96,1792]{2,1,0:T(8,128)(2,1)}, bf16[2,96,1792]{2,1,0:T(8,128)(2,1)}, u32[]{:S(2)}, u32[]{:S(2)}) collective-permute-start(bf16[2,96,1792]{2,1,0:T(8,128)(2,1)} %slice.173), channel_id=1, source_target_pairs={{0,16},{1,17},{2,18},{3,19},{4,20},{5,21},{6,22},{7,23},{8,24},{9,... | collective-permute-start | bytes 2064392 | tf_op jit(solution)/shard_map/ppermute | solution.py:40
  148.8 17.1 %collective-permute-start.20 = (bf16[2,96,1792]{2,1,0:T(8,128)(2,1)}, bf16[2,96,1792]{2,1,0:T(8,128)(2,1)}, u32[]{:S(2)}, u32[]{:S(2)}) collective-permute-start(bf16[2,96,1792]{2,1,0:T(8,128)(2,1)} %slice.174), channel_id=1, source_target_pairs={{0,8},{1,9},{2,10},{3,11},{4,12},{5,13},{6,14},{7,15},{8,0},{9,1},... | collective-permute-start | bytes 2064392 | tf_op jit(solution)/shard_map/ppermute | solution.py:40
  149.4 20.3 %collective-permute-start.22 = (bf16[4,96,1792]{2,1,0:T(8,128)(2,1)}, bf16[4,96,1792]{2,1,0:T(8,128)(2,1)}, u32[]{:S(2)}, u32[]{:S(2)}) collective-permute-start(bf16[4,96,1792]{2,1,0:T(8,128)(2,1)} %collective-permute-done.17.refs_6_), channel_id=1, source_target_pairs={{0,4},{1,5},{2,6},{3,7},{4,0},{5,1},{6,2},{7,3},{8,12},{9,13},{10,... | collective-permute-start | bytes 4128776 | tf_op jit(solution)/shard_map/ppermute | solution.py:40
  152.4 17.3 %collective-permute-start.23 = (bf16[4,96,1792]{2,1,0:T(8,128)(2,1)}, bf16[4,96,1792]{2,1,0:T(8,128)(2,1)}, u32[]{:S(2)}, u32[]{:S(2)}) collective-permute-start(bf16[4,96,1792]{2,1,0:T(8,128)(2,1)} %collective-permute-done.18.refs_7_), channel_id=1, source_target_pairs={{0,4},{1,5},{2,6},{3,7},{4,0},{5,1},{6,2},{7,3},{8,12},{9,13},{10,... | collective-permute-start | bytes 4128776 | tf_op jit(solution)/shard_map/ppermute | solution.py:40
  152.4 17.3 %all-to-all-start.1 = ((bf16[4,192,512]{2,1,0:T(8,128)(2,1)}), bf16[4,192,512]{2,1,0:T(8,128)(2,1)}, u32[]{:S(2)}, u32[]{:S(2)}) async-start(bf16[4,192,512]{2,1,0:T(8,128)(2,1)} %get-tuple-element.87), calls=%async_computation.1 | async-start | bytes 1572864 | tf_op jit(solution)/shard_map/all_to_all | solution.py:69
  199.4 17.3 %all-to-all-start.2 = ((bf16[4,192,512]{2,1,0:T(8,128)(2,1)}), bf16[4,192,512]{2,1,0:T(8,128)(2,1)S(1)}, u32[]{:S(2)}, u32[]{:S(2)}) async-start(bf16[4,192,512]{2,1,0:T(8,128)(2,1)} %get-tuple-element.92), calls=%async_computation.2 | async-start | bytes 1572864 | tf_op jit(solution)/shard_map/all_to_all | solution.py:69
  203.0 99.8 %reduce-scatter.3.cloned.1.call-start = ((), (), s32[]{:S(2)}) async-start(), calls=%async_computation.9 | async-start | bytes 12386304 | tf_op jit(solution)/shard_map/reduce_scatter | solution.py:837
  218.1 19.0 %collective-permute-start.26 = (bf16[512,768]{1,0:T(8,128)(2,1)S(1)}, bf16[512,768]{1,0:T(8,128)(2,1)}, u32[]{:S(2)}, u32[]{:S(2)}) collective-permute-start(bf16[512,768]{1,0:T(8,128)(2,1)S(1)} %copy-done.29), channel_id=1, source_target_pairs={{2,4},{3,5},{4,2},{5,3},{10,12},{11,13},{12,10},{13,11},{18,20},{1... | collective-permute-start | bytes 2359304 | tf_op jit(solution)/shard_map/ppermute | solution.py:40
  233.4 17.9 %all-to-all-start.3 = ((bf16[4,192,512]{2,1,0:T(8,128)(2,1)}), bf16[4,192,512]{2,1,0:T(8,128)(2,1)S(1)}, u32[]{:S(2)}, u32[]{:S(2)}) async-start(bf16[4,192,512]{2,1,0:T(8,128)(2,1)} %attend_back.3), calls=%async_computation.3 | async-start | bytes 1572864 | tf_op jit(solution)/shard_map/all_to_all | solution.py:69
  251.3 20.3 %all-to-all-start.5 = ((bf16[4,192,512]{2,1,0:T(8,128)(2,1)}), bf16[4,192,512]{2,1,0:T(8,128)(2,1)S(1)}, u32[]{:S(2)}, u32[]{:S(2)}) async-start(bf16[4,192,512]{2,1,0:T(8,128)(2,1)} %attend_back.5), calls=%async_computation.5 | async-start | bytes 1572864 | tf_op jit(solution)/shard_map/all_to_all | solution.py:69
  258.1 86.3 %reduce-scatter.5.cloned.1.call-start = ((), (), s32[]{:S(2)}) async-start(), calls=%async_computation.10 | async-start | bytes 1720320 | tf_op jit(solution)/shard_map/reduce_scatter | solution.py:868
  304.8 19.6 %collective-permute-start.32 = (bf16[2,96,576]{2,1,0:T(8,128)(2,1)}, bf16[2,96,576]{2,1,0:T(8,128)(2,1)}, u32[]{:S(2)}, u32[]{:S(2)}) collective-permute-start(bf16[2,96,576]{2,1,0:T(8,128)(2,1)} %get-tuple-element.161), channel_id=1, source_target_pairs={{0,16},{1,17},{2,18},{3,19},{4,20},{5,21},{6,22},{7,23},{8,24},{9,... | collective-permute-start | bytes 663560 | tf_op jit(solution)/shard_map/ppermute | solution.py:40
  321.6 21.9 %collective-permute-start.28 = (bf16[512,768]{1,0:T(8,128)(2,1)}, bf16[512,768]{1,0:T(8,128)(2,1)S(1)}, u32[]{:S(2)}, u32[]{:S(2)}) collective-permute-start(bf16[512,768]{1,0:T(8,128)(2,1)} %copy-done.11), channel_id=1, source_target_pairs={{2,4},{3,5},{4,2},{5,3},{10,12},{11,13},{12,10},{13,11},{18,20},{1... | collective-permute-start | bytes 2359304 | tf_op jit(solution)/shard_map/ppermute | solution.py:40
  325.6 13.1 %collective-permute-start.33 = (bf16[4,96,576]{2,1,0:T(8,128)(2,1)S(1)}, bf16[4,96,576]{2,1,0:T(8,128)(2,1)S(1)}, u32[]{:S(2)}, u32[]{:S(2)}) collective-permute-start(bf16[4,96,576]{2,1,0:T(8,128)(2,1)S(1)} %pad_maximum_fusion.2), channel_id=1, source_target_pairs={{0,8},{1,9},{2,10},{3,11},{4,12},{5,13},{6,14},{7,15},{8,0},{9,1},... | collective-permute-start | bytes 1327112 | tf_op jit(solution)/shard_map/ppermute | solution.py:40
  328.1 13.2 %collective-permute-start.35 = (bf16[4,96,576]{2,1,0:T(8,128)(2,1)S(1)}, bf16[4,96,576]{2,1,0:T(8,128)(2,1)S(1)}, u32[]{:S(2)}, u32[]{:S(2)}) collective-permute-start(bf16[4,96,576]{2,1,0:T(8,128)(2,1)S(1)} %pad_maximum_fusion.3), channel_id=1, source_target_pairs={{0,16},{1,17},{2,18},{3,19},{4,20},{5,21},{6,22},{7,23},{8,24},{9,... | collective-permute-start | bytes 1327112 | tf_op jit(solution)/shard_map/ppermute | solution.py:40
  346.9 31.1 %all-to-all-start.6 = ((bf16[4,96,576]{2,1,0:T(8,128)(2,1)}), bf16[4,96,576]{2,1,0:T(8,128)(2,1)S(1)}, u32[]{:S(2)}, u32[]{:S(2)}) async-start(bf16[4,96,576]{2,1,0:T(8,128)(2,1)} %fusion.8), calls=%async_computation.8 | async-start | bytes 983040 | tf_op jit(solution)/shard_map/all_to_all | solution.py:198
  356.5 17.4 %collective-permute-start.37 = (f32[4,7,768]{2,1,0:T(8,128)S(1)}, f32[4,7,768]{2,1,0:T(8,128)S(1)}, u32[]{:S(2)}, u32[]{:S(2)}) collective-permute-start(f32[4,7,768]{2,1,0:T(8,128)S(1)} %scatter.4), channel_id=1, source_target_pairs={{0,2},{1,3},{2,0},{3,1},{4,6},{5,7},{6,4},{7,5},{8,10},{9,11},{10,... | collective-permute-start | bytes 258056 | tf_op jit(solution)/shard_map/ppermute | solution.py:40
  (53 other events, 436.7 us)
Sparse Core Ops, SparseCore 0:
  23.1 48.1 all-gather.2
  216.8 81.8 reduce-scatter.2
  302.9 32.9 reduce-scatter.4

commit v5 on v4

--- a/solution.py
+++ b/solution.py
@@ -490,10 +490,10 @@
     mixture_grads, full, bias_up, slope, keep_one, keep_two, sems = refs[10:]
     wide = mixtures.shape[1]
     hidden = bias_up.shape[1]
-    of_out = slice(0, wide)
-    of_up = slice(wide, wide + hidden)
-    of_down = slice(wide + hidden, wide + 2 * hidden)
-    of_bias = slice(wide + 2 * hidden, wide + 2 * hidden + 64)
+    of_up = slice(0, hidden)
+    of_down = slice(hidden, 2 * hidden)
+    of_out = slice(2 * hidden, 2 * hidden + wide)
+    of_bias = slice(2 * hidden + wide, 2 * hidden + wide + 64)
     copies = load_weights(where[0], pieces, full, sems)
     gain, scale, shift = vectors[GAIN_TWO], vectors[SCALE_TWO], vectors[SHIFT_TWO]
     gate_one, gate_two, bias_down = vectors[GATE_ONE], vectors[GATE_TWO], vectors[BIAS_DOWN]
@@ -618,11 +618,14 @@
         lines = jnp.where(line == n, sums[3 + n : 4 + n], lines)
     lines = jnp.concatenate([lines, jnp.zeros((120, lines.shape[1]), f32)])
     extra = lines.T[:, :64].astype(bf16)
-    value = jnp.concatenate([own, up, down, extra], axis=1)
-    if len(out.shape) == 3:
-        out[0] = value
-    else:
-        out[...] = value.reshape(out.shape)
+    at = 0
+    for value in (up, down, jnp.concatenate([own, extra], axis=1)):
+        columns = slice(at, at + value.shape[1])
+        at += value.shape[1]
+        if len(out.shape) == 3:
+            out[0, :, columns] = value
+        else:
+            out[:, 0, :, columns] = value.reshape(out.shape[0], out.shape[2], -1)
 
 
 def feed_grads(dp_size, hidden, branch_one, branch_two, act, pre, attention, sums):
@@ -780,7 +783,7 @@
     packs = spread_dp(packs, dp_size)
     first_own = jnp.stack([first_shard, *others])
     extra = jnp.pad(up_bias[:, None], ((0, 0), (0, 63)))
-    second_shard = jnp.concatenate([out_weight.T, up_weight, down_weight.T, extra], axis=1)
+    second_shard = jnp.concatenate([up_weight, down_weight.T, out_weight.T, extra], axis=1)
     tokens, first_own = meet(tokens, first_own)
     sent = send_tokens(tokens, dp_size)
     first_pieces = gather_weights(first_own, gather_sides(first_own, dp_size), dp_size)
@@ -882,16 +885,21 @@
         first_sides = reduce_sides(first_grad, first_far, first_half, dp_size)
     first_sum = reduce_second(first_grad, first_far, first_sides, dp_size)
     mods, first_sum, second_sum = meet(mods, first_sum, second_sum)
-    first_sum = reduce_planes(first_sum)
+    first_sum = [
+        lax.dynamic_index_in_dim(first_sum.astype(bf16), z ^ t, 0, keepdims=False)
+        for t in range(GROUP)
+    ]
+    first_sum = first_sum[:1] + [swap_z(first_sum[t], dp_size, t) for t in range(1, GROUP)]
+    first_sum = sum(term.astype(f32) for term in first_sum)
     mods = mods + swap_z(mods, dp_size, 1)
     mods = mods.at[:, :6].set(mods[:, :6].astype(bf16).astype(f32))
     mods = widen(mods, swap_z, 2)
     tail = jnp.sum(mods[:, 6:], axis=0)
     mods = mods[:, :6]
     input_grad = settle(input_grad, sent)
-    out_out = second_sum[:, :wide].T
-    up_out = second_sum[:, wide : wide + hidden]
-    down_out = second_sum[:, wide + hidden : wide + 2 * hidden].T
+    up_out = second_sum[:, :hidden]
+    down_out = second_sum[:, hidden : 2 * hidden].T
+    out_out = second_sum[:, 2 * hidden : 2 * hidden + wide].T
     bias_up_out, gain_two_out, bias_down_out = second_sum[:, wide + 2 * hidden :].T[:3]
     qkv_out = jnp.stack(jnp.split(first_sum, 3, axis=1))
 

time: 394 us -> 389 us (0.987)
    all_to_all x1 -> x0, starting transfers between devices: 8.6 us -> none  [reduce_planes(): terms = lax.all_to_all(own.astype(bf16), TENSOR, 0, 0, tiled=True)]
    ppermute x38 -> x41, starting transfers between devices: 58 us -> 63.8 us  [permute(): return lax.ppermute(array, AXES, pairs)]
    ppermute x38 -> x41, waiting for transfers between devices: 59 us -> 59.1 us  [permute(): return lax.ppermute(array, AXES, pairs)]
  transfers between devices with their start and end apart: 47 -> 49, of which waited for: 14 -> 15; matrix products, arithmetic and copies ran while one was open for 10% -> 9% of each run, Pallas kernels for 23% -> 23%
where the time goes in v5:
time: 389 us; the launch traced here: 381 us
  Pallas kernels  123 us (32%)
  starting transfers between devices  87.3 us (22%)
  waiting for transfers between devices  85.6 us (22%)
  local copies, waits for them, and re-layouts  36.1 us (9%)
  other arithmetic  16.7 us (4%)
  blocking collectives  15.5 us (4%)
  between operations  15 us (4%)
    ppermute x41, starting transfers between devices, permute(): return lax.ppermute(array, AXES, pairs)  63.8 us
    ppermute x41, waiting for transfers between devices, permute(): return lax.ppermute(array, AXES, pairs)  59.1 us
    pallas_call x3, Pallas kernels, attend_back(): pl.pallas_call(attend_back_kernel, out_shape=jax.ShapeDtypeStruct((count,...  39.8 us
    pallas_call x1, Pallas kernels, feed(): pl.pallas_call(functools.partial(feed_kernel, len(pieces)), out_shape=sha...  29.2 us
    all_to_all x5, waiting for transfers between devices, exchange(): return lax.all_to_all(blocks, TEAM, 0, 0, tiled=True)  26.5 us
    all_to_all x5, starting transfers between devices, exchange(): return lax.all_to_all(blocks, TEAM, 0, 0, tiled=True)  23.2 us
    pallas_call x1, Pallas kernels, attend(): pl.pallas_call(attend_kernel, out_shape=[jax.ShapeDtypeStruct((count, hea...  21.7 us
    unnamed x82, local copies, waits for them, and re-layouts  18.9 us
  transfers between devices with their start and end apart: 49, of which 15 were waited for; matrix products, arithmetic and copies ran while one was open for 9% of the time, Pallas kernels for 23%

profile of v5, /device:TPU:0, one launch (start us, length us, event | category | flops | bytes accessed | tf_op | source)
XLA Modules:
  0.0 381.5 jit_solution(6053233736603920887)
XLA Ops:
  8.3 3.1 collective-permute-start.1
  11.4 2.6 collective-permute-start.2
  30.1 6.2 %collective-permute-done.5 = bf16[2,144,576]{2,1,0:T(8,128)(2,1)S(1)} collective-permute-done((bf16[2,144,576]{2,1,0:T(8,128)(2,1)S(1)}, bf16[2,144,576]{2,1,0:T(8,128)(2,1)S(1)}, u32[]{:S(2)}, u32[]{:S(2)}) %collective-permute-start.5) | collective-permute-done | bytes 331808 | tf_op jit(solution)/shard_map/ppermute | solution.py:40
  39.1 7.8 %collective-permute-done.8.refs_7_.refs_9_ = bf16[4,96,576]{2,1,0:T(8,128)(2,1)} collective-permute-done((bf16[4,96,576]{2,1,0:T(8,128)(2,1)S(1)}, bf16[4,96,576]{2,1,0:T(8,128)(2,1)}, u32[]{:S(2)}, u32[]{:S(2)}) %collective-permute-start.8) | collective-permute-done | bytes 442400 | tf_op jit(solution)/shard_map/ppermute | solution.py:40
  51.0 3.2 collective-permute-done.10.refs_9_.refs_11_
  54.3 18.3 %collective-permute-start.14 = (bf16[2,96,576]{2,1,0:T(8,128)(2,1)S(1)}, bf16[2,96,576]{2,1,0:T(8,128)(2,1)}, u32[]{:S(2)}, u32[]{:S(2)}) collective-permute-start(bf16[2,96,576]{2,1,0:T(8,128)(2,1)S(1)} %collective-permute-done.9.refs_8_.refs_10_), channel_id=1, source_target_pairs={{0,4},{1,5},{2,6},{3,7},{4,0},{5,1},{6,2},{7,3},{8,12},{9,13},{10,... | collective-permute-start | bytes 663560 | tf_op jit(solution)/shard_map/ppermute | solution.py:40
  74.2 2.6 prepare.1
  78.7 5.8 %project.1 = (bf16[512,768]{1,0:T(8,128)(2,1)S(1)}, bf16[4,576,512]{2,1,0:T(8,128)(2,1)S(1)}) custom-call(s32[2]{0:T(128)S(1)} %pad_add_fusion.where.refs_0_, bf16[512,768]{1,0:T(8,128)(2,1)S(1)} %broadcast_select_fusion.3.refs_1_, f32[16,768]{1,0:T(8,128)S(1)} %get-tuple-element.79.refs_2_.refs_3_, f32[32,512]{1,0:T(8,128)S(1)} %copy-done.17, ...), custom_call_target="tpu_custom_call" | custom-call | flops 1811939328 | bytes 5898240 | tf_op jit(solution)/shard_map/project/pallas_call | solution.py:459
  86.8 4.6 %all-to-all-start = ((bf16[4,576,512]{2,1,0:T(8,128)(2,1)}), bf16[4,576,512]{2,1,0:T(8,128)(2,1)}, u32[]{:S(2)}, u32[]{:S(2)}) async-start(bf16[4,576,512]{2,1,0:T(8,128)(2,1)} %copy-done.6), calls=%async_computation | async-start | bytes 4718592 | tf_op jit(solution)/shard_map/all_to_all | solution.py:69
  93.5 26.4 %all-to-all-done.packed = bf16[4,576,512]{2,1,0:T(8,128)(2,1)} async-done(((bf16[4,576,512]{2,1,0:T(8,128)(2,1)}), bf16[4,576,512]{2,1,0:T(8,128)(2,1)}, u32[]{:S(2)}, u32[]{:S(2)}) %all-to-all-start) | async-done | bytes 2359328 | tf_op jit(solution)/shard_map/all_to_all | solution.py:69
  120.9 21.7 %attend.1 = (bf16[4,192,512]{2,1,0:T(8,128)(2,1)}, f32[3,4,512]{2,1,0:T(4,128)S(1)}) custom-call(bf16[4,576,512]{2,1,0:T(8,128)(2,1)} %all-to-all-done.packed), custom_call_target="tpu_custom_call" | custom-call | flops 12884901888 | bytes 3145728 | tf_op jit(solution)/shard_map/attend/pallas_call | solution.py:224
  149.3 2.9 collective-permute-start.22
  152.3 4.4 %all-to-all-start.1 = ((bf16[4,192,512]{2,1,0:T(8,128)(2,1)}), bf16[4,192,512]{2,1,0:T(8,128)(2,1)}, u32[]{:S(2)}, u32[]{:S(2)}) async-start(bf16[4,192,512]{2,1,0:T(8,128)(2,1)} %get-tuple-element.87), calls=%async_computation.1 | async-start | bytes 1572864 | tf_op jit(solution)/shard_map/all_to_all | solution.py:69
  156.7 5.7 %collective-permute-done.19.refs_8_ = bf16[2,96,1792]{2,1,0:T(8,128)(2,1)} collective-permute-done((bf16[2,96,1792]{2,1,0:T(8,128)(2,1)}, bf16[2,96,1792]{2,1,0:T(8,128)(2,1)}, u32[]{:S(2)}, u32[]{:S(2)}) %collective-permute-start.19) | collective-permute-done | bytes 688160 | tf_op jit(solution)/shard_map/ppermute | solution.py:40
  169.7 29.2 %feed.1 = (bf16[512,768]{1,0:T(8,128)(2,1)}, f32[512,768]{1,0:T(8,128)}, bf16[512,768]{1,0:T(8,128)(2,1)}, bf16[512,768]{1,0:T(8,128)(2,1)}, bf16[512,768]{1,0:T...) custom-call(s32[2]{0:T(128)} %copy-done.19, ...), custom_call_target="tpu_custom_call" | custom-call | flops 11274289152 | bytes 18350080 | tf_op jit(solution)/shard_map/feed/pallas_call | solution.py:584
  198.9 3.6 all-to-all-start.2
  204.6 11.5 %feed_grads.1 = bf16[8,4,96,1792]{3,2,1,0:T(8,128)(2,1)} custom-call(bf16[512,768]{1,0:T(8,128)(2,1)} %get-tuple-element.93.hidden, bf16[512,768]{1,0:T(8,128)(2,1)} %get-tuple-element.94.branch_one, bf16[512,768]{1,0:T(8,128)(2,1)} %get-tuple-element.95.branch_two, bf16[4,512,768]{2,1,0:T(8,128)(2,1)} %get-tuple-element.96.act, ...), custom_call_target="tpu_custom_call" | custom-call | flops 5637144576 | bytes 18350080 | tf_op jit(solution)/shard_map/feed_grads/pallas_call | solution.py:641
  219.5 13.3 %attend_back.3 = bf16[4,192,512]{2,1,0:T(8,128)(2,1)} custom-call(bf16[4,576,512]{2,1,0:T(8,128)(2,1)} %all-to-all-done.packed, bf16[4,192,512]{2,1,0:T(8,128)(2,1)} %copy-done.30, f32[3,4,512]{2,1,0:T(4,128)} %copy-done.23, f32[32,2048]{1,0:T(8,128)} %copy-done.33, f32[32,2048]{1,0:T(8,128)} %copy-done.32), custom_call_target="tpu_custom_call" | custom-call | flops 10737418240 | bytes 2097152 | tf_op jit(solution)/shard_map/attend_back/pallas_call | solution.py:297
  232.8 3.7 all-to-all-start.3
  237.5 13.2 %attend_back.5 = bf16[4,192,512]{2,1,0:T(8,128)(2,1)} custom-call(bf16[4,576,512]{2,1,0:T(8,128)(2,1)} %all-to-all-done.packed, bf16[4,192,512]{2,1,0:T(8,128)(2,1)} %copy-done.30, f32[3,4,512]{2,1,0:T(4,128)} %copy-done.23, f32[32,2048]{1,0:T(8,128)} %copy-done.33, f32[32,2048]{1,0:T(8,128)} %copy-done.32), custom_call_target="tpu_custom_call" | custom-call | flops 10737418240 | bytes 2097152 | tf_op jit(solution)/shard_map/attend_back/pallas_call | solution.py:297
  250.7 6.8 %all-to-all-start.5 = ((bf16[4,192,512]{2,1,0:T(8,128)(2,1)}), bf16[4,192,512]{2,1,0:T(8,128)(2,1)S(1)}, u32[]{:S(2)}, u32[]{:S(2)}) async-start(bf16[4,192,512]{2,1,0:T(8,128)(2,1)} %attend_back.5), calls=%async_computation.5 | async-start | bytes 1572864 | tf_op jit(solution)/shard_map/all_to_all | solution.py:69
  257.8 13.2 %attend_back.4 = bf16[4,192,512]{2,1,0:T(8,128)(2,1)} custom-call(bf16[4,576,512]{2,1,0:T(8,128)(2,1)} %all-to-all-done.packed, bf16[4,192,512]{2,1,0:T(8,128)(2,1)} %copy-done.30, f32[3,4,512]{2,1,0:T(4,128)} %copy-done.23, f32[32,2048]{1,0:T(8,128)} %copy-done.33, f32[32,2048]{1,0:T(8,128)} %copy-done.32), custom_call_target="tpu_custom_call" | custom-call | flops 10737418240 | bytes 2097152 | tf_op jit(solution)/shard_map/attend_back/pallas_call | solution.py:297
  271.0 15.5 %all_to_all.30.refs_1_.refs_5_ = bf16[4,192,512]{2,1,0:T(8,128)(2,1)S(1)} all-to-all(bf16[4,192,512]{2,1,0:T(8,128)(2,1)} %attend_back.4), channel_id=1, replica_groups=mesh['quad'=4,'core'=2,'high'=2,'low'=2] {'core','low'}, dimensions={0} | all-to-all | bytes 1572864 | tf_op jit(solution)/shard_map/all_to_all | solution.py:69
  286.6 4.9 %project_grads.1 = (bf16[4,4,96,576]{3,2,1,0:T(8,128)(2,1)S(1)}, bf16[4,4,96,576]{3,2,1,0:T(8,128)(2,1)}) custom-call(s32[2]{0:T(128)S(1)} %copy-done.20, bf16[512,768]{1,0:T(8,128)(2,1)S(1)} %copy-done.22, bf16[4,192,512]{2,1,0:T(8,128)(2,1)S(1)} %all-to-all-done.3.refs_0_.refs_4_, bf16[4,192,512]{2,1,0:T(8,128)(2,1)S(1)} %all_to_all.30.refs_1_.refs_5_, ...), custom_call_target="tpu_custom_call" | custom-call | flops 1811939328 | bytes 5898240 | tf_op jit(solution)/shard_map/project_grads/pallas_call | solution.py:683
  292.8 4.3 %collective-permute-done.27 = bf16[4,4,96,576]{3,2,1,0:T(8,128)(2,1)} collective-permute-done((bf16[4,4,96,576]{3,2,1,0:T(8,128)(2,1)}, bf16[4,4,96,576]{3,2,1,0:T(8,128)(2,1)}, u32[]{:S(2)}, u32[]{:S(2)}) %collective-permute-start.27) | collective-permute-done | bytes 1769504 | tf_op jit(solution)/shard_map/ppermute | solution.py:40
  297.1 3.3 convert_add_fusion.1
  309.7 6.1 %project_back.1 = (bf16[512,768]{1,0:T(8,128)(2,1)S(1)}, f32[2,768]{1,0:T(2,128)S(1)}) custom-call(s32[2]{0:T(128)S(1)} %copy-done.20, bf16[512,768]{1,0:T(8,128)(2,1)S(1)} %copy-done.1, f32[16,768]{1,0:T(8,128)S(1)} %copy-done.16, f32[512,768]{1,0:T(8,128)S(1)} %copy-done.8, bf16[4,192,512]{2,1,0:T(8,128)(2,1)S(1)} %all-to-all-done.3.refs_0_.refs_4_, ...), custom_call_target="tpu_custom_call" | custom-call | flops 1811939328 | bytes 5898240 | tf_op jit(solution)/shard_map/project_back/pallas_call | solution.py:727
  330.3 7.6 %collective-permute-done.33 = bf16[4,96,576]{2,1,0:T(8,128)(2,1)S(1)} collective-permute-done((bf16[4,96,576]{2,1,0:T(8,128)(2,1)S(1)}, bf16[4,96,576]{2,1,0:T(8,128)(2,1)S(1)}, u32[]{:S(2)}, u32[]{:S(2)}) %collective-permute-start.33) | collective-permute-done | bytes 442400 | tf_op jit(solution)/shard_map/ppermute | solution.py:40
  337.9 2.6 collective-permute-done.35
  345.3 8.1 %collective-permute-start.39 = (bf16[96,576]{1,0:T(8,128)(2,1)S(1)}, bf16[96,576]{1,0:T(8,128)(2,1)S(1)}, u32[]{:S(2)}, u32[]{:S(2)}) collective-permute-start(bf16[96,576]{1,0:T(8,128)(2,1)S(1)} %get-tuple-element.162), channel_id=1, source_target_pairs={{0,2},{1,3},{2,0},{3,1},{4,6},{5,7},{6,4},{7,5},{8,10},{9,11},{10,... | collective-permute-start | bytes 331784 | tf_op jit(solution)/shard_map/ppermute | solution.py:40
  355.4 7.5 %collective-permute-done.36 = f32[4,7,768]{2,1,0:T(8,128)S(1)} collective-permute-done((f32[4,7,768]{2,1,0:T(8,128)S(1)}, f32[4,7,768]{2,1,0:T(8,128)S(1)}, u32[]{:S(2)}, u32[]{:S(2)}) %collective-permute-start.36) | collective-permute-done | bytes 86048 | tf_op jit(solution)/shard_map/ppermute | solution.py:40
  364.9 5.4 %collective-permute-done.37 = f32[4,7,768]{2,1,0:T(8,128)S(1)} collective-permute-done((f32[4,7,768]{2,1,0:T(8,128)S(1)}, f32[4,7,768]{2,1,0:T(8,128)S(1)}, u32[]{:S(2)}, u32[]{:S(2)}) %collective-permute-start.37) | collective-permute-done | bytes 86048 | tf_op jit(solution)/shard_map/ppermute | solution.py:40
  (241 shorter events, 91.0 us)
Async XLA Ops:
  7.2 69.7 %all-gather.3.cloned.1.call-start = ((), (), s32[]{:S(2)}) async-start(), calls=%async_computation.10 | async-start | bytes 1720320 | tf_op jit(solution)/shard_map/all_gather | solution.py:791
  8.3 16.4 %collective-permute-start.1 = (bf16[96,576]{1,0:T(8,128)(2,1)S(1)}, bf16[96,576]{1,0:T(8,128)(2,1)S(1)}, u32[]{:S(2)}, u32[]{:S(2)}) collective-permute-start(bf16[96,576]{1,0:T(8,128)(2,1)S(1)} %pad_maximum_fusion.6), channel_id=1, source_target_pairs={{0,1},{1,0},{2,3},{3,2},{4,5},{5,4},{6,7},{7,6},{8,9},{9,8},{10,11... | collective-permute-start | bytes 331784 | tf_op jit(solution)/shard_map/ppermute | solution.py:40
  11.4 13.3 %collective-permute-start.2 = (bf16[96,576]{1,0:T(8,128)(2,1)S(1)}, bf16[96,576]{1,0:T(8,128)(2,1)S(1)}, u32[]{:S(2)}, u32[]{:S(2)}) collective-permute-start(bf16[96,576]{1,0:T(8,128)(2,1)S(1)} %pad_maximum_fusion.6), channel_id=1, source_target_pairs={{0,2},{1,3},{2,0},{3,1},{4,6},{5,7},{6,4},{7,5},{8,10},{9,11},{10,... | collective-permute-start | bytes 331784 | tf_op jit(solution)/shard_map/ppermute | solution.py:40
  28.0 18.9 %collective-permute-start.8 = (bf16[4,96,576]{2,1,0:T(8,128)(2,1)S(1)}, bf16[4,96,576]{2,1,0:T(8,128)(2,1)}, u32[]{:S(2)}, u32[]{:S(2)}) collective-permute-start(bf16[4,96,576]{2,1,0:T(8,128)(2,1)S(1)} %pad_maximum_fusion.1.refs_5_.refs_7_), channel_id=1, source_target_pairs={{0,16},{1,17},{2,18},{3,19},{4,20},{5,21},{6,22},{7,23},{8,24},{9,... | collective-permute-start | bytes 1327112 | tf_op jit(solution)/shard_map/ppermute | solution.py:40
  28.5 25.8 %collective-permute-start.4 = (bf16[512,768]{1,0:T(8,128)(2,1)S(1)}, bf16[512,768]{1,0:T(8,128)(2,1)}, u32[]{:S(2)}, u32[]{:S(2)}) collective-permute-start(bf16[512,768]{1,0:T(8,128)(2,1)S(1)} %copy-done.27), channel_id=1, source_target_pairs={{2,4},{3,5},{4,2},{5,3},{10,12},{11,13},{12,10},{13,11},{18,20},{1... | collective-permute-start | bytes 2359304 | tf_op jit(solution)/shard_map/ppermute | solution.py:40
  36.3 36.3 %collective-permute-start.6 = (bf16[4,144,576]{2,1,0:T(8,128)(2,1)S(1)}, bf16[4,144,576]{2,1,0:T(8,128)(2,1)S(1)}, u32[]{:S(2)}, u32[]{:S(2)}) collective-permute-start(bf16[4,144,576]{2,1,0:T(8,128)(2,1)S(1)} %constant_dynamic-update-slice_fusion), channel_id=1, source_target_pairs={{0,4},{1,5},{2,6},{3,7},{4,0},{5,1},{6,2},{7,3},{8,12},{9,13},{10,... | collective-permute-start | bytes 1990664 | tf_op jit(solution)/shard_map/ppermute | solution.py:40
  37.5 13.0 %collective-permute-start.9 = (bf16[2,96,576]{2,1,0:T(8,128)(2,1)S(1)}, bf16[2,96,576]{2,1,0:T(8,128)(2,1)S(1)}, u32[]{:S(2)}, u32[]{:S(2)}) collective-permute-start(bf16[2,96,576]{2,1,0:T(8,128)(2,1)S(1)} %slice.218), channel_id=1, source_target_pairs={{0,16},{1,17},{2,18},{3,19},{4,20},{5,21},{6,22},{7,23},{8,24},{9,... | collective-permute-start | bytes 663560 | tf_op jit(solution)/shard_map/ppermute | solution.py:40
  50.5 26.5 %collective-permute-start.11 = (bf16[4,96,576]{2,1,0:T(8,128)(2,1)S(1)}, bf16[4,96,576]{2,1,0:T(8,128)(2,1)}, u32[]{:S(2)}, u32[]{:S(2)}) collective-permute-start(bf16[4,96,576]{2,1,0:T(8,128)(2,1)S(1)} %pad_maximum_fusion.1.refs_5_.refs_7_), channel_id=1, source_target_pairs={{0,4},{1,5},{2,6},{3,7},{4,0},{5,1},{6,2},{7,3},{8,12},{9,13},{10,... | collective-permute-start | bytes 1327112 | tf_op jit(solution)/shard_map/ppermute | solution.py:40
  50.5 26.5 %collective-permute-start.12 = (bf16[4,96,576]{2,1,0:T(8,128)(2,1)S(1)}, bf16[4,96,576]{2,1,0:T(8,128)(2,1)}, u32[]{:S(2)}, u32[]{:S(2)}) collective-permute-start(bf16[4,96,576]{2,1,0:T(8,128)(2,1)S(1)} %collective-permute-done.7.refs_6_.refs_8_), channel_id=1, source_target_pairs={{0,4},{1,5},{2,6},{3,7},{4,0},{5,1},{6,2},{7,3},{8,12},{9,13},{10,... | collective-permute-start | bytes 1327112 | tf_op jit(solution)/shard_map/ppermute | solution.py:40
  54.2 22.7 %collective-permute-start.13 = (bf16[4,96,576]{2,1,0:T(8,128)(2,1)}, bf16[4,96,576]{2,1,0:T(8,128)(2,1)}, u32[]{:S(2)}, u32[]{:S(2)}) collective-permute-start(bf16[4,96,576]{2,1,0:T(8,128)(2,1)} %collective-permute-done.8.refs_7_.refs_9_), channel_id=1, source_target_pairs={{0,4},{1,5},{2,6},{3,7},{4,0},{5,1},{6,2},{7,3},{8,12},{9,13},{10,... | collective-permute-start | bytes 1327112 | tf_op jit(solution)/shard_map/ppermute | solution.py:40
  54.3 22.6 %collective-permute-start.14 = (bf16[2,96,576]{2,1,0:T(8,128)(2,1)S(1)}, bf16[2,96,576]{2,1,0:T(8,128)(2,1)}, u32[]{:S(2)}, u32[]{:S(2)}) collective-permute-start(bf16[2,96,576]{2,1,0:T(8,128)(2,1)S(1)} %collective-permute-done.9.refs_8_.refs_10_), channel_id=1, source_target_pairs={{0,4},{1,5},{2,6},{3,7},{4,0},{5,1},{6,2},{7,3},{8,12},{9,13},{10,... | collective-permute-start | bytes 663560 | tf_op jit(solution)/shard_map/ppermute | solution.py:40
  86.8 33.2 %all-to-all-start = ((bf16[4,576,512]{2,1,0:T(8,128)(2,1)}), bf16[4,576,512]{2,1,0:T(8,128)(2,1)}, u32[]{:S(2)}, u32[]{:S(2)}) async-start(bf16[4,576,512]{2,1,0:T(8,128)(2,1)} %copy-done.6), calls=%async_computation | async-start | bytes 4718592 | tf_op jit(solution)/shard_map/all_to_all | solution.py:69
  91.4 51.8 %collective-permute-start.17 = (bf16[4,96,1792]{2,1,0:T(8,128)(2,1)}, bf16[4,96,1792]{2,1,0:T(8,128)(2,1)}, u32[]{:S(2)}, u32[]{:S(2)}) collective-permute-start(bf16[4,96,1792]{2,1,0:T(8,128)(2,1)} %bitcast.118), channel_id=1, source_target_pairs={{0,8},{1,9},{2,10},{3,11},{4,12},{5,13},{6,14},{7,15},{8,0},{9,1},... | collective-permute-start | bytes 4128776 | tf_op jit(solution)/shard_map/ppermute | solution.py:40
  92.0 51.2 %collective-permute-start.18 = (bf16[4,96,1792]{2,1,0:T(8,128)(2,1)}, bf16[4,96,1792]{2,1,0:T(8,128)(2,1)}, u32[]{:S(2)}, u32[]{:S(2)}) collective-permute-start(bf16[4,96,1792]{2,1,0:T(8,128)(2,1)} %bitcast.119), channel_id=1, source_target_pairs={{0,16},{1,17},{2,18},{3,19},{4,20},{5,21},{6,22},{7,23},{8,24},{9,... | collective-permute-start | bytes 4128776 | tf_op jit(solution)/shard_map/ppermute | solution.py:40
  93.5 75.0 %collective-permute-start.21 = (bf16[4,96,1792]{2,1,0:T(8,128)(2,1)}, bf16[4,96,1792]{2,1,0:T(8,128)(2,1)}, u32[]{:S(2)}, u32[]{:S(2)}) collective-permute-start(bf16[4,96,1792]{2,1,0:T(8,128)(2,1)} %bitcast.120), channel_id=1, source_target_pairs={{0,4},{1,5},{2,6},{3,7},{4,0},{5,1},{6,2},{7,3},{8,12},{9,13},{10,... | collective-permute-start | bytes 4128776 | tf_op jit(solution)/shard_map/ppermute | solution.py:40
  120.0 32.3 %collective-permute-start.16 = (bf16[512,768]{1,0:T(8,128)(2,1)S(1)}, bf16[512,768]{1,0:T(8,128)(2,1)S(1)}, u32[]{:S(2)}, u32[]{:S(2)}) collective-permute-start(bf16[512,768]{1,0:T(8,128)(2,1)S(1)} %copy-done.28), channel_id=1, source_target_pairs={{2,4},{3,5},{4,2},{5,3},{10,12},{11,13},{12,10},{13,11},{18,20},{1... | collective-permute-start | bytes 2359304 | tf_op jit(solution)/shard_map/ppermute | solution.py:40
  145.2 17.2 %collective-permute-start.19 = (bf16[2,96,1792]{2,1,0:T(8,128)(2,1)}, bf16[2,96,1792]{2,1,0:T(8,128)(2,1)}, u32[]{:S(2)}, u32[]{:S(2)}) collective-permute-start(bf16[2,96,1792]{2,1,0:T(8,128)(2,1)} %slice.173), channel_id=1, source_target_pairs={{0,16},{1,17},{2,18},{3,19},{4,20},{5,21},{6,22},{7,23},{8,24},{9,... | collective-permute-start | bytes 2064392 | tf_op jit(solution)/shard_map/ppermute | solution.py:40
  148.8 17.3 %collective-permute-start.20 = (bf16[2,96,1792]{2,1,0:T(8,128)(2,1)}, bf16[2,96,1792]{2,1,0:T(8,128)(2,1)}, u32[]{:S(2)}, u32[]{:S(2)}) collective-permute-start(bf16[2,96,1792]{2,1,0:T(8,128)(2,1)} %slice.174), channel_id=1, source_target_pairs={{0,8},{1,9},{2,10},{3,11},{4,12},{5,13},{6,14},{7,15},{8,0},{9,1},... | collective-permute-start | bytes 2064392 | tf_op jit(solution)/shard_map/ppermute | solution.py:40
  149.3 20.3 %collective-permute-start.22 = (bf16[4,96,1792]{2,1,0:T(8,128)(2,1)}, bf16[4,96,1792]{2,1,0:T(8,128)(2,1)}, u32[]{:S(2)}, u32[]{:S(2)}) collective-permute-start(bf16[4,96,1792]{2,1,0:T(8,128)(2,1)} %collective-permute-done.17.refs_6_), channel_id=1, source_target_pairs={{0,4},{1,5},{2,6},{3,7},{4,0},{5,1},{6,2},{7,3},{8,12},{9,13},{10,... | collective-permute-start | bytes 4128776 | tf_op jit(solution)/shard_map/ppermute | solution.py:40
  152.3 17.4 %collective-permute-start.23 = (bf16[4,96,1792]{2,1,0:T(8,128)(2,1)}, bf16[4,96,1792]{2,1,0:T(8,128)(2,1)}, u32[]{:S(2)}, u32[]{:S(2)}) collective-permute-start(bf16[4,96,1792]{2,1,0:T(8,128)(2,1)} %collective-permute-done.18.refs_7_), channel_id=1, source_target_pairs={{0,4},{1,5},{2,6},{3,7},{4,0},{5,1},{6,2},{7,3},{8,12},{9,13},{10,... | collective-permute-start | bytes 4128776 | tf_op jit(solution)/shard_map/ppermute | solution.py:40
  152.3 17.4 %all-to-all-start.1 = ((bf16[4,192,512]{2,1,0:T(8,128)(2,1)}), bf16[4,192,512]{2,1,0:T(8,128)(2,1)}, u32[]{:S(2)}, u32[]{:S(2)}) async-start(bf16[4,192,512]{2,1,0:T(8,128)(2,1)} %get-tuple-element.87), calls=%async_computation.1 | async-start | bytes 1572864 | tf_op jit(solution)/shard_map/all_to_all | solution.py:69
  198.9 17.2 %all-to-all-start.2 = ((bf16[4,192,512]{2,1,0:T(8,128)(2,1)}), bf16[4,192,512]{2,1,0:T(8,128)(2,1)S(1)}, u32[]{:S(2)}, u32[]{:S(2)}) async-start(bf16[4,192,512]{2,1,0:T(8,128)(2,1)} %get-tuple-element.92), calls=%async_computation.2 | async-start | bytes 1572864 | tf_op jit(solution)/shard_map/all_to_all | solution.py:69
  202.6 99.6 %reduce-scatter.3.cloned.1.call-start = ((), (), s32[]{:S(2)}) async-start(), calls=%async_computation.8 | async-start | bytes 12386304 | tf_op jit(solution)/shard_map/reduce_scatter | solution.py:840
  217.5 19.0 %collective-permute-start.26 = (bf16[512,768]{1,0:T(8,128)(2,1)S(1)}, bf16[512,768]{1,0:T(8,128)(2,1)}, u32[]{:S(2)}, u32[]{:S(2)}) collective-permute-start(bf16[512,768]{1,0:T(8,128)(2,1)S(1)} %copy-done.29), channel_id=1, source_target_pairs={{2,4},{3,5},{4,2},{5,3},{10,12},{11,13},{12,10},{13,11},{18,20},{1... | collective-permute-start | bytes 2359304 | tf_op jit(solution)/shard_map/ppermute | solution.py:40
  232.8 17.9 %all-to-all-start.3 = ((bf16[4,192,512]{2,1,0:T(8,128)(2,1)}), bf16[4,192,512]{2,1,0:T(8,128)(2,1)S(1)}, u32[]{:S(2)}, u32[]{:S(2)}) async-start(bf16[4,192,512]{2,1,0:T(8,128)(2,1)} %attend_back.3), calls=%async_computation.3 | async-start | bytes 1572864 | tf_op jit(solution)/shard_map/all_to_all | solution.py:69
  250.7 20.3 %all-to-all-start.5 = ((bf16[4,192,512]{2,1,0:T(8,128)(2,1)}), bf16[4,192,512]{2,1,0:T(8,128)(2,1)S(1)}, u32[]{:S(2)}, u32[]{:S(2)}) async-start(bf16[4,192,512]{2,1,0:T(8,128)(2,1)} %attend_back.5), calls=%async_computation.5 | async-start | bytes 1572864 | tf_op jit(solution)/shard_map/all_to_all | solution.py:69
  257.6 85.5 %reduce-scatter.5.cloned.1.call-start = ((), (), s32[]{:S(2)}) async-start(), calls=%async_computation.9 | async-start | bytes 1720320 | tf_op jit(solution)/shard_map/reduce_scatter | solution.py:871
  304.1 19.6 %collective-permute-start.32 = (bf16[2,96,576]{2,1,0:T(8,128)(2,1)}, bf16[2,96,576]{2,1,0:T(8,128)(2,1)}, u32[]{:S(2)}, u32[]{:S(2)}) collective-permute-start(bf16[2,96,576]{2,1,0:T(8,128)(2,1)} %get-tuple-element.164), channel_id=1, source_target_pairs={{0,16},{1,17},{2,18},{3,19},{4,20},{5,21},{6,22},{7,23},{8,24},{9,... | collective-permute-start | bytes 663560 | tf_op jit(solution)/shard_map/ppermute | solution.py:40
  320.8 21.2 %collective-permute-start.28 = (bf16[512,768]{1,0:T(8,128)(2,1)}, bf16[512,768]{1,0:T(8,128)(2,1)S(1)}, u32[]{:S(2)}, u32[]{:S(2)}) collective-permute-start(bf16[512,768]{1,0:T(8,128)(2,1)} %copy-done.11), channel_id=1, source_target_pairs={{2,4},{3,5},{4,2},{5,3},{10,12},{11,13},{12,10},{13,11},{18,20},{1... | collective-permute-start | bytes 2359304 | tf_op jit(solution)/shard_map/ppermute | solution.py:40
  327.4 13.2 %collective-permute-start.35 = (bf16[4,96,576]{2,1,0:T(8,128)(2,1)S(1)}, bf16[4,96,576]{2,1,0:T(8,128)(2,1)S(1)}, u32[]{:S(2)}, u32[]{:S(2)}) collective-permute-start(bf16[4,96,576]{2,1,0:T(8,128)(2,1)S(1)} %pad_maximum_fusion.3), channel_id=1, source_target_pairs={{0,16},{1,17},{2,18},{3,19},{4,20},{5,21},{6,22},{7,23},{8,24},{9,... | collective-permute-start | bytes 1327112 | tf_op jit(solution)/shard_map/ppermute | solution.py:40
  345.0 19.0 %collective-permute-start.38 = (bf16[96,576]{1,0:T(8,128)(2,1)S(1)}, bf16[96,576]{1,0:T(8,128)(2,1)S(1)}, u32[]{:S(2)}, u32[]{:S(2)}) collective-permute-start(bf16[96,576]{1,0:T(8,128)(2,1)S(1)} %get-tuple-element.161), channel_id=1, source_target_pairs={{0,1},{1,0},{2,3},{3,2},{4,5},{5,4},{6,7},{7,6},{8,9},{9,8},{10,11... | collective-permute-start | bytes 331784 | tf_op jit(solution)/shard_map/ppermute | solution.py:40
  345.3 18.7 %collective-permute-start.39 = (bf16[96,576]{1,0:T(8,128)(2,1)S(1)}, bf16[96,576]{1,0:T(8,128)(2,1)S(1)}, u32[]{:S(2)}, u32[]{:S(2)}) collective-permute-start(bf16[96,576]{1,0:T(8,128)(2,1)S(1)} %get-tuple-element.162), channel_id=1, source_target_pairs={{0,2},{1,3},{2,0},{3,1},{4,6},{5,7},{6,4},{7,5},{8,10},{9,11},{10,... | collective-permute-start | bytes 331784 | tf_op jit(solution)/shard_map/ppermute | solution.py:40
  (55 other events, 453.2 us)
Sparse Core Ops, SparseCore 0:
  23.0 48.1 all-gather.2
  216.2 81.7 reduce-scatter.2
  302.3 32.9 reduce-scatter.4

commit v6 on v5

--- a/solution.py
+++ b/solution.py
@@ -784,7 +784,6 @@
     first_own = jnp.stack([first_shard, *others])
     extra = jnp.pad(up_bias[:, None], ((0, 0), (0, 63)))
     second_shard = jnp.concatenate([up_weight, down_weight.T, out_weight.T, extra], axis=1)
-    tokens, first_own = meet(tokens, first_own)
     sent = send_tokens(tokens, dp_size)
     first_pieces = gather_weights(first_own, gather_sides(first_own, dp_size), dp_size)
     moved = settle(tokens, sent)

time: 389 us -> 384 us (0.987)
  waiting for transfers between devices: 85.6 us -> 76.9 us
    ppermute x41, waiting for transfers between devices: 59.1 us -> 50.4 us  [permute(): return lax.ppermute(array, AXES, pairs)]
where the time goes in v6:
time: 384 us; the launch traced here: 377 us
  Pallas kernels  123 us (32%)
  starting transfers between devices  90.7 us (24%)
  waiting for transfers between devices  76.9 us (20%)
  local copies, waits for them, and re-layouts  36.8 us (10%)
  other arithmetic  16.7 us (4%)
  blocking collectives  15.4 us (4%)
  between operations  14.9 us (4%)
    ppermute x41, starting transfers between devices, permute(): return lax.ppermute(array, AXES, pairs)  67.3 us
    ppermute x41, waiting for transfers between devices, permute(): return lax.ppermute(array, AXES, pairs)  50.4 us
    pallas_call x3, Pallas kernels, attend_back(): pl.pallas_call(attend_back_kernel, out_shape=jax.ShapeDtypeStruct((count,...  39.8 us
    pallas_call x1, Pallas kernels, feed(): pl.pallas_call(functools.partial(feed_kernel, len(pieces)), out_shape=sha...  29.2 us
    all_to_all x5, waiting for transfers between devices, exchange(): return lax.all_to_all(blocks, TEAM, 0, 0, tiled=True)  26.5 us
    all_to_all x5, starting transfers between devices, exchange(): return lax.all_to_all(blocks, TEAM, 0, 0, tiled=True)  23.1 us
    pallas_call x1, Pallas kernels, attend(): pl.pallas_call(attend_kernel, out_shape=[jax.ShapeDtypeStruct((count, hea...  21.7 us
    unnamed x82, local copies, waits for them, and re-layouts  18.9 us
  transfers between devices with their start and end apart: 49, of which 15 were waited for; matrix products, arithmetic and copies ran while one was open for 9% of the time, Pallas kernels for 23%

profile of v6, /device:TPU:0, one launch (start us, length us, event | category | flops | bytes accessed | tf_op | source)
XLA Modules:
  0.0 376.7 jit_solution(4771339024330917579)
XLA Ops:
  8.3 3.1 collective-permute-start.2
  28.5 6.5 %collective-permute-done.5 = bf16[2,144,576]{2,1,0:T(8,128)(2,1)S(1)} collective-permute-done((bf16[2,144,576]{2,1,0:T(8,128)(2,1)S(1)}, bf16[2,144,576]{2,1,0:T(8,128)(2,1)S(1)}, u32[]{:S(2)}, u32[]{:S(2)}) %collective-permute-start.5) | collective-permute-done | bytes 331808 | tf_op jit(solution)/shard_map/ppermute | solution.py:40
  35.1 2.6 collective-permute-start.6
  41.0 4.7 %collective-permute-done.8.refs_7_.refs_9_ = bf16[4,96,576]{2,1,0:T(8,128)(2,1)} collective-permute-done((bf16[4,96,576]{2,1,0:T(8,128)(2,1)S(1)}, bf16[4,96,576]{2,1,0:T(8,128)(2,1)}, u32[]{:S(2)}, u32[]{:S(2)}) %collective-permute-start.8) | collective-permute-done | bytes 442400 | tf_op jit(solution)/shard_map/ppermute | solution.py:40
  50.7 16.2 %collective-permute-start.12 = (bf16[4,96,576]{2,1,0:T(8,128)(2,1)S(1)}, bf16[4,96,576]{2,1,0:T(8,128)(2,1)}, u32[]{:S(2)}, u32[]{:S(2)}) collective-permute-start(bf16[4,96,576]{2,1,0:T(8,128)(2,1)S(1)} %collective-permute-done.7.refs_6_.refs_8_), channel_id=1, source_target_pairs={{0,4},{1,5},{2,6},{3,7},{4,0},{5,1},{6,2},{7,3},{8,12},{9,13},{10,... | collective-permute-start | bytes 1327112 | tf_op jit(solution)/shard_map/ppermute | solution.py:40
  69.3 2.6 prepare.1
  73.7 5.8 %project.1 = (bf16[512,768]{1,0:T(8,128)(2,1)S(1)}, bf16[4,576,512]{2,1,0:T(8,128)(2,1)S(1)}) custom-call(s32[2]{0:T(128)S(1)} %pad_add_fusion.where.refs_0_, bf16[512,768]{1,0:T(8,128)(2,1)S(1)} %broadcast_select_fusion.3.refs_1_, f32[16,768]{1,0:T(8,128)S(1)} %get-tuple-element.73.refs_2_.refs_3_, f32[32,512]{1,0:T(8,128)S(1)} %copy-done.17, ...), custom_call_target="tpu_custom_call" | custom-call | flops 1811939328 | bytes 5898240 | tf_op jit(solution)/shard_map/project/pallas_call | solution.py:459
  81.8 4.6 %all-to-all-start = ((bf16[4,576,512]{2,1,0:T(8,128)(2,1)}), bf16[4,576,512]{2,1,0:T(8,128)(2,1)}, u32[]{:S(2)}, u32[]{:S(2)}) async-start(bf16[4,576,512]{2,1,0:T(8,128)(2,1)} %copy-done.6), calls=%async_computation | async-start | bytes 4718592 | tf_op jit(solution)/shard_map/all_to_all | solution.py:69
  88.6 26.4 %all-to-all-done.packed = bf16[4,576,512]{2,1,0:T(8,128)(2,1)} async-done(((bf16[4,576,512]{2,1,0:T(8,128)(2,1)}), bf16[4,576,512]{2,1,0:T(8,128)(2,1)}, u32[]{:S(2)}, u32[]{:S(2)}) %all-to-all-start) | async-done | bytes 2359328 | tf_op jit(solution)/shard_map/all_to_all | solution.py:69
  115.9 21.7 %attend.1 = (bf16[4,192,512]{2,1,0:T(8,128)(2,1)}, f32[3,4,512]{2,1,0:T(4,128)S(1)}) custom-call(bf16[4,576,512]{2,1,0:T(8,128)(2,1)} %all-to-all-done.packed), custom_call_target="tpu_custom_call" | custom-call | flops 12884901888 | bytes 3145728 | tf_op jit(solution)/shard_map/attend/pallas_call | solution.py:224
  144.4 3.1 collective-permute-start.22
  147.4 4.4 %all-to-all-start.1 = ((bf16[4,192,512]{2,1,0:T(8,128)(2,1)}), bf16[4,192,512]{2,1,0:T(8,128)(2,1)}, u32[]{:S(2)}, u32[]{:S(2)}) async-start(bf16[4,192,512]{2,1,0:T(8,128)(2,1)} %get-tuple-element.83), calls=%async_computation.1 | async-start | bytes 1572864 | tf_op jit(solution)/shard_map/all_to_all | solution.py:69
  151.9 4.2 %collective-permute-done.19.refs_8_ = bf16[2,96,1792]{2,1,0:T(8,128)(2,1)} collective-permute-done((bf16[2,96,1792]{2,1,0:T(8,128)(2,1)}, bf16[2,96,1792]{2,1,0:T(8,128)(2,1)}, u32[]{:S(2)}, u32[]{:S(2)}) %collective-permute-start.19) | collective-permute-done | bytes 688160 | tf_op jit(solution)/shard_map/ppermute | solution.py:40
  156.1 2.8 collective-permute-start.24
  164.7 29.2 %feed.1 = (bf16[512,768]{1,0:T(8,128)(2,1)}, f32[512,768]{1,0:T(8,128)}, bf16[512,768]{1,0:T(8,128)(2,1)}, bf16[512,768]{1,0:T(8,128)(2,1)}, bf16[512,768]{1,0:T...) custom-call(s32[2]{0:T(128)} %copy-done.19, ...), custom_call_target="tpu_custom_call" | custom-call | flops 11274289152 | bytes 18350080 | tf_op jit(solution)/shard_map/feed/pallas_call | solution.py:584
  193.9 3.6 all-to-all-start.2
  199.6 11.4 %feed_grads.1 = bf16[8,4,96,1792]{3,2,1,0:T(8,128)(2,1)} custom-call(bf16[512,768]{1,0:T(8,128)(2,1)} %get-tuple-element.89.hidden, bf16[512,768]{1,0:T(8,128)(2,1)} %get-tuple-element.90.branch_one, bf16[512,768]{1,0:T(8,128)(2,1)} %get-tuple-element.91.branch_two, bf16[4,512,768]{2,1,0:T(8,128)(2,1)} %get-tuple-element.92.act, ...), custom_call_target="tpu_custom_call" | custom-call | flops 5637144576 | bytes 18350080 | tf_op jit(solution)/shard_map/feed_grads/pallas_call | solution.py:641
  214.5 13.4 %attend_back.3 = bf16[4,192,512]{2,1,0:T(8,128)(2,1)} custom-call(bf16[4,576,512]{2,1,0:T(8,128)(2,1)} %all-to-all-done.packed, bf16[4,192,512]{2,1,0:T(8,128)(2,1)} %copy-done.30, f32[3,4,512]{2,1,0:T(4,128)} %copy-done.23, f32[32,2048]{1,0:T(8,128)} %copy-done.33, f32[32,2048]{1,0:T(8,128)} %copy-done.32), custom_call_target="tpu_custom_call" | custom-call | flops 10737418240 | bytes 2097152 | tf_op jit(solution)/shard_map/attend_back/pallas_call | solution.py:297
  227.8 4.2 %all-to-all-start.3 = ((bf16[4,192,512]{2,1,0:T(8,128)(2,1)}), bf16[4,192,512]{2,1,0:T(8,128)(2,1)S(1)}, u32[]{:S(2)}, u32[]{:S(2)}) async-start(bf16[4,192,512]{2,1,0:T(8,128)(2,1)} %attend_back.3), calls=%async_computation.3 | async-start | bytes 1572864 | tf_op jit(solution)/shard_map/all_to_all | solution.py:69
  233.1 13.2 %attend_back.5 = bf16[4,192,512]{2,1,0:T(8,128)(2,1)} custom-call(bf16[4,576,512]{2,1,0:T(8,128)(2,1)} %all-to-all-done.packed, bf16[4,192,512]{2,1,0:T(8,128)(2,1)} %copy-done.30, f32[3,4,512]{2,1,0:T(4,128)} %copy-done.23, f32[32,2048]{1,0:T(8,128)} %copy-done.33, f32[32,2048]{1,0:T(8,128)} %copy-done.32), custom_call_target="tpu_custom_call" | custom-call | flops 10737418240 | bytes 2097152 | tf_op jit(solution)/shard_map/attend_back/pallas_call | solution.py:297
  246.3 6.1 %all-to-all-start.5 = ((bf16[4,192,512]{2,1,0:T(8,128)(2,1)}), bf16[4,192,512]{2,1,0:T(8,128)(2,1)S(1)}, u32[]{:S(2)}, u32[]{:S(2)}) async-start(bf16[4,192,512]{2,1,0:T(8,128)(2,1)} %attend_back.5), calls=%async_computation.5 | async-start | bytes 1572864 | tf_op jit(solution)/shard_map/all_to_all | solution.py:69
  252.7 13.2 %attend_back.4 = bf16[4,192,512]{2,1,0:T(8,128)(2,1)} custom-call(bf16[4,576,512]{2,1,0:T(8,128)(2,1)} %all-to-all-done.packed, bf16[4,192,512]{2,1,0:T(8,128)(2,1)} %copy-done.30, f32[3,4,512]{2,1,0:T(4,128)} %copy-done.23, f32[32,2048]{1,0:T(8,128)} %copy-done.33, f32[32,2048]{1,0:T(8,128)} %copy-done.32), custom_call_target="tpu_custom_call" | custom-call | flops 10737418240 | bytes 2097152 | tf_op jit(solution)/shard_map/attend_back/pallas_call | solution.py:297
  265.9 15.4 %all_to_all.30.refs_1_.refs_5_ = bf16[4,192,512]{2,1,0:T(8,128)(2,1)S(1)} all-to-all(bf16[4,192,512]{2,1,0:T(8,128)(2,1)} %attend_back.4), channel_id=1, replica_groups=mesh['quad'=4,'core'=2,'high'=2,'low'=2] {'core','low'}, dimensions={0} | all-to-all | bytes 1572864 | tf_op jit(solution)/shard_map/all_to_all | solution.py:69
  281.3 4.9 %project_grads.1 = (bf16[4,4,96,576]{3,2,1,0:T(8,128)(2,1)S(1)}, bf16[4,4,96,576]{3,2,1,0:T(8,128)(2,1)}) custom-call(s32[2]{0:T(128)S(1)} %copy-done.20, bf16[512,768]{1,0:T(8,128)(2,1)S(1)} %copy-done.22, bf16[4,192,512]{2,1,0:T(8,128)(2,1)S(1)} %all-to-all-done.3.refs_0_.refs_4_, bf16[4,192,512]{2,1,0:T(8,128)(2,1)S(1)} %all_to_all.30.refs_1_.refs_5_, ...), custom_call_target="tpu_custom_call" | custom-call | flops 1811939328 | bytes 5898240 | tf_op jit(solution)/shard_map/project_grads/pallas_call | solution.py:683
  287.5 4.3 %collective-permute-done.27 = bf16[4,4,96,576]{3,2,1,0:T(8,128)(2,1)} collective-permute-done((bf16[4,4,96,576]{3,2,1,0:T(8,128)(2,1)}, bf16[4,4,96,576]{3,2,1,0:T(8,128)(2,1)}, u32[]{:S(2)}, u32[]{:S(2)}) %collective-permute-start.27) | collective-permute-done | bytes 1769504 | tf_op jit(solution)/shard_map/ppermute | solution.py:40
  291.8 3.3 convert_add_fusion.1
  304.9 6.1 %project_back.1 = (bf16[512,768]{1,0:T(8,128)(2,1)S(1)}, f32[2,768]{1,0:T(2,128)S(1)}) custom-call(s32[2]{0:T(128)S(1)} %copy-done.20, bf16[512,768]{1,0:T(8,128)(2,1)S(1)} %copy-done.1, f32[16,768]{1,0:T(8,128)S(1)} %copy-done.16, f32[512,768]{1,0:T(8,128)S(1)} %copy-done.8, bf16[4,192,512]{2,1,0:T(8,128)(2,1)S(1)} %all-to-all-done.3.refs_0_.refs_4_, ...), custom_call_target="tpu_custom_call" | custom-call | flops 1811939328 | bytes 5898240 | tf_op jit(solution)/shard_map/project_back/pallas_call | solution.py:727
  325.1 6.2 %collective-permute-done.33 = bf16[4,96,576]{2,1,0:T(8,128)(2,1)S(1)} collective-permute-done((bf16[4,96,576]{2,1,0:T(8,128)(2,1)S(1)}, bf16[4,96,576]{2,1,0:T(8,128)(2,1)S(1)}, u32[]{:S(2)}, u32[]{:S(2)}) %collective-permute-start.33) | collective-permute-done | bytes 442400 | tf_op jit(solution)/shard_map/ppermute | solution.py:40
  331.3 4.6 %collective-permute-done.35 = bf16[4,96,576]{2,1,0:T(8,128)(2,1)S(1)} collective-permute-done((bf16[4,96,576]{2,1,0:T(8,128)(2,1)S(1)}, bf16[4,96,576]{2,1,0:T(8,128)(2,1)S(1)}, u32[]{:S(2)}, u32[]{:S(2)}) %collective-permute-start.35) | collective-permute-done | bytes 442400 | tf_op jit(solution)/shard_map/ppermute | solution.py:40
  340.7 7.9 %collective-permute-start.39 = (bf16[96,576]{1,0:T(8,128)(2,1)S(1)}, bf16[96,576]{1,0:T(8,128)(2,1)S(1)}, u32[]{:S(2)}, u32[]{:S(2)}) collective-permute-start(bf16[96,576]{1,0:T(8,128)(2,1)S(1)} %get-tuple-element.158), channel_id=1, source_target_pairs={{0,2},{1,3},{2,0},{3,1},{4,6},{5,7},{6,4},{7,5},{8,10},{9,11},{10,... | collective-permute-start | bytes 331784 | tf_op jit(solution)/shard_map/ppermute | solution.py:40
  350.7 7.5 %collective-permute-done.36 = f32[4,7,768]{2,1,0:T(8,128)S(1)} collective-permute-done((f32[4,7,768]{2,1,0:T(8,128)S(1)}, f32[4,7,768]{2,1,0:T(8,128)S(1)}, u32[]{:S(2)}, u32[]{:S(2)}) %collective-permute-start.36) | collective-permute-done | bytes 86048 | tf_op jit(solution)/shard_map/ppermute | solution.py:40
  360.2 5.4 %collective-permute-done.37 = f32[4,7,768]{2,1,0:T(8,128)S(1)} collective-permute-done((f32[4,7,768]{2,1,0:T(8,128)S(1)}, f32[4,7,768]{2,1,0:T(8,128)S(1)}, u32[]{:S(2)}, u32[]{:S(2)}) %collective-permute-start.37) | collective-permute-done | bytes 86048 | tf_op jit(solution)/shard_map/ppermute | solution.py:40
  (241 shorter events, 92.6 us)
Async XLA Ops:
  7.2 64.7 %all-gather.3.cloned.1.call-start = ((), (), s32[]{:S(2)}) async-start(), calls=%async_computation.10 | async-start | bytes 1720320 | tf_op jit(solution)/shard_map/all_gather | solution.py:790
  8.3 16.4 %collective-permute-start.2 = (bf16[96,576]{1,0:T(8,128)(2,1)S(1)}, bf16[96,576]{1,0:T(8,128)(2,1)S(1)}, u32[]{:S(2)}, u32[]{:S(2)}) collective-permute-start(bf16[96,576]{1,0:T(8,128)(2,1)S(1)} %pad_maximum_fusion.6), channel_id=1, source_target_pairs={{0,1},{1,0},{2,3},{3,2},{4,5},{5,4},{6,7},{7,6},{8,9},{9,8},{10,11... | collective-permute-start | bytes 331784 | tf_op jit(solution)/shard_map/ppermute | solution.py:40
  11.4 13.3 %collective-permute-start.3 = (bf16[96,576]{1,0:T(8,128)(2,1)S(1)}, bf16[96,576]{1,0:T(8,128)(2,1)S(1)}, u32[]{:S(2)}, u32[]{:S(2)}) collective-permute-start(bf16[96,576]{1,0:T(8,128)(2,1)S(1)} %pad_maximum_fusion.6), channel_id=1, source_target_pairs={{0,2},{1,3},{2,0},{3,1},{4,6},{5,7},{6,4},{7,5},{8,10},{9,11},{10,... | collective-permute-start | bytes 331784 | tf_op jit(solution)/shard_map/ppermute | solution.py:40
  22.9 27.9 %collective-permute-start = (bf16[512,768]{1,0:T(8,128)(2,1)S(1)}, bf16[512,768]{1,0:T(8,128)(2,1)}, u32[]{:S(2)}, u32[]{:S(2)}) collective-permute-start(bf16[512,768]{1,0:T(8,128)(2,1)S(1)} %copy-done.27), channel_id=1, source_target_pairs={{2,4},{3,5},{4,2},{5,3},{10,12},{11,13},{12,10},{13,11},{18,20},{1... | collective-permute-start | bytes 2359304 | tf_op jit(solution)/shard_map/ppermute | solution.py:40
  26.4 13.3 %collective-permute-start.7 = (bf16[4,96,576]{2,1,0:T(8,128)(2,1)S(1)}, bf16[4,96,576]{2,1,0:T(8,128)(2,1)S(1)}, u32[]{:S(2)}, u32[]{:S(2)}) collective-permute-start(bf16[4,96,576]{2,1,0:T(8,128)(2,1)S(1)} %pad_maximum_fusion.1.refs_5_.refs_7_), channel_id=1, source_target_pairs={{0,8},{1,9},{2,10},{3,11},{4,12},{5,13},{6,14},{7,15},{8,0},{9,1},... | collective-permute-start | bytes 1327112 | tf_op jit(solution)/shard_map/ppermute | solution.py:40
  28.0 17.7 %collective-permute-start.8 = (bf16[4,96,576]{2,1,0:T(8,128)(2,1)S(1)}, bf16[4,96,576]{2,1,0:T(8,128)(2,1)}, u32[]{:S(2)}, u32[]{:S(2)}) collective-permute-start(bf16[4,96,576]{2,1,0:T(8,128)(2,1)S(1)} %pad_maximum_fusion.1.refs_5_.refs_7_), channel_id=1, source_target_pairs={{0,16},{1,17},{2,18},{3,19},{4,20},{5,21},{6,22},{7,23},{8,24},{9,... | collective-permute-start | bytes 1327112 | tf_op jit(solution)/shard_map/ppermute | solution.py:40
  35.1 32.5 %collective-permute-start.6 = (bf16[4,144,576]{2,1,0:T(8,128)(2,1)S(1)}, bf16[4,144,576]{2,1,0:T(8,128)(2,1)S(1)}, u32[]{:S(2)}, u32[]{:S(2)}) collective-permute-start(bf16[4,144,576]{2,1,0:T(8,128)(2,1)S(1)} %constant_dynamic-update-slice_fusion), channel_id=1, source_target_pairs={{0,4},{1,5},{2,6},{3,7},{4,0},{5,1},{6,2},{7,3},{8,12},{9,13},{10,... | collective-permute-start | bytes 1990664 | tf_op jit(solution)/shard_map/ppermute | solution.py:40
  39.8 27.2 %collective-permute-start.9 = (bf16[2,96,576]{2,1,0:T(8,128)(2,1)S(1)}, bf16[2,96,576]{2,1,0:T(8,128)(2,1)S(1)}, u32[]{:S(2)}, u32[]{:S(2)}) collective-permute-start(bf16[2,96,576]{2,1,0:T(8,128)(2,1)S(1)} %slice.218), channel_id=1, source_target_pairs={{0,16},{1,17},{2,18},{3,19},{4,20},{5,21},{6,22},{7,23},{8,24},{9,... | collective-permute-start | bytes 663560 | tf_op jit(solution)/shard_map/ppermute | solution.py:40
  47.4 19.7 %collective-permute-start.10 = (bf16[2,96,576]{2,1,0:T(8,128)(2,1)}, bf16[2,96,576]{2,1,0:T(8,128)(2,1)}, u32[]{:S(2)}, u32[]{:S(2)}) collective-permute-start(bf16[2,96,576]{2,1,0:T(8,128)(2,1)} %slice.219), channel_id=1, source_target_pairs={{0,8},{1,9},{2,10},{3,11},{4,12},{5,13},{6,14},{7,15},{8,0},{9,1},... | collective-permute-start | bytes 663560 | tf_op jit(solution)/shard_map/ppermute | solution.py:40
  50.5 21.4 %collective-permute-start.11 = (bf16[4,96,576]{2,1,0:T(8,128)(2,1)S(1)}, bf16[4,96,576]{2,1,0:T(8,128)(2,1)}, u32[]{:S(2)}, u32[]{:S(2)}) collective-permute-start(bf16[4,96,576]{2,1,0:T(8,128)(2,1)S(1)} %pad_maximum_fusion.1.refs_5_.refs_7_), channel_id=1, source_target_pairs={{0,4},{1,5},{2,6},{3,7},{4,0},{5,1},{6,2},{7,3},{8,12},{9,13},{10,... | collective-permute-start | bytes 1327112 | tf_op jit(solution)/shard_map/ppermute | solution.py:40
  50.7 21.3 %collective-permute-start.12 = (bf16[4,96,576]{2,1,0:T(8,128)(2,1)S(1)}, bf16[4,96,576]{2,1,0:T(8,128)(2,1)}, u32[]{:S(2)}, u32[]{:S(2)}) collective-permute-start(bf16[4,96,576]{2,1,0:T(8,128)(2,1)S(1)} %collective-permute-done.7.refs_6_.refs_8_), channel_id=1, source_target_pairs={{0,4},{1,5},{2,6},{3,7},{4,0},{5,1},{6,2},{7,3},{8,12},{9,13},{10,... | collective-permute-start | bytes 1327112 | tf_op jit(solution)/shard_map/ppermute | solution.py:40
  81.8 33.2 %all-to-all-start = ((bf16[4,576,512]{2,1,0:T(8,128)(2,1)}), bf16[4,576,512]{2,1,0:T(8,128)(2,1)}, u32[]{:S(2)}, u32[]{:S(2)}) async-start(bf16[4,576,512]{2,1,0:T(8,128)(2,1)} %copy-done.6), calls=%async_computation | async-start | bytes 4718592 | tf_op jit(solution)/shard_map/all_to_all | solution.py:69
  86.4 51.8 %collective-permute-start.17 = (bf16[4,96,1792]{2,1,0:T(8,128)(2,1)}, bf16[4,96,1792]{2,1,0:T(8,128)(2,1)}, u32[]{:S(2)}, u32[]{:S(2)}) collective-permute-start(bf16[4,96,1792]{2,1,0:T(8,128)(2,1)} %bitcast.118), channel_id=1, source_target_pairs={{0,8},{1,9},{2,10},{3,11},{4,12},{5,13},{6,14},{7,15},{8,0},{9,1},... | collective-permute-start | bytes 4128776 | tf_op jit(solution)/shard_map/ppermute | solution.py:40
  87.0 51.2 %collective-permute-start.18 = (bf16[4,96,1792]{2,1,0:T(8,128)(2,1)}, bf16[4,96,1792]{2,1,0:T(8,128)(2,1)}, u32[]{:S(2)}, u32[]{:S(2)}) collective-permute-start(bf16[4,96,1792]{2,1,0:T(8,128)(2,1)} %bitcast.119), channel_id=1, source_target_pairs={{0,16},{1,17},{2,18},{3,19},{4,20},{5,21},{6,22},{7,23},{8,24},{9,... | collective-permute-start | bytes 4128776 | tf_op jit(solution)/shard_map/ppermute | solution.py:40
  88.6 74.9 %collective-permute-start.21 = (bf16[4,96,1792]{2,1,0:T(8,128)(2,1)}, bf16[4,96,1792]{2,1,0:T(8,128)(2,1)}, u32[]{:S(2)}, u32[]{:S(2)}) collective-permute-start(bf16[4,96,1792]{2,1,0:T(8,128)(2,1)} %bitcast.120), channel_id=1, source_target_pairs={{0,4},{1,5},{2,6},{3,7},{4,0},{5,1},{6,2},{7,3},{8,12},{9,13},{10,... | collective-permute-start | bytes 4128776 | tf_op jit(solution)/shard_map/ppermute | solution.py:40
  115.0 32.4 %collective-permute-start.16 = (bf16[512,768]{1,0:T(8,128)(2,1)S(1)}, bf16[512,768]{1,0:T(8,128)(2,1)S(1)}, u32[]{:S(2)}, u32[]{:S(2)}) collective-permute-start(bf16[512,768]{1,0:T(8,128)(2,1)S(1)} %copy-done.28), channel_id=1, source_target_pairs={{2,4},{3,5},{4,2},{5,3},{10,12},{11,13},{12,10},{13,11},{18,20},{1... | collective-permute-start | bytes 2359304 | tf_op jit(solution)/shard_map/ppermute | solution.py:40
  140.2 15.9 %collective-permute-start.19 = (bf16[2,96,1792]{2,1,0:T(8,128)(2,1)}, bf16[2,96,1792]{2,1,0:T(8,128)(2,1)}, u32[]{:S(2)}, u32[]{:S(2)}) collective-permute-start(bf16[2,96,1792]{2,1,0:T(8,128)(2,1)} %slice.173), channel_id=1, source_target_pairs={{0,16},{1,17},{2,18},{3,19},{4,20},{5,21},{6,22},{7,23},{8,24},{9,... | collective-permute-start | bytes 2064392 | tf_op jit(solution)/shard_map/ppermute | solution.py:40
  143.8 16.1 %collective-permute-start.20 = (bf16[2,96,1792]{2,1,0:T(8,128)(2,1)}, bf16[2,96,1792]{2,1,0:T(8,128)(2,1)}, u32[]{:S(2)}, u32[]{:S(2)}) collective-permute-start(bf16[2,96,1792]{2,1,0:T(8,128)(2,1)} %slice.174), channel_id=1, source_target_pairs={{0,8},{1,9},{2,10},{3,11},{4,12},{5,13},{6,14},{7,15},{8,0},{9,1},... | collective-permute-start | bytes 2064392 | tf_op jit(solution)/shard_map/ppermute | solution.py:40
  144.4 20.3 %collective-permute-start.22 = (bf16[4,96,1792]{2,1,0:T(8,128)(2,1)}, bf16[4,96,1792]{2,1,0:T(8,128)(2,1)}, u32[]{:S(2)}, u32[]{:S(2)}) collective-permute-start(bf16[4,96,1792]{2,1,0:T(8,128)(2,1)} %collective-permute-done.17.refs_6_), channel_id=1, source_target_pairs={{0,4},{1,5},{2,6},{3,7},{4,0},{5,1},{6,2},{7,3},{8,12},{9,13},{10,... | collective-permute-start | bytes 4128776 | tf_op jit(solution)/shard_map/ppermute | solution.py:40
  147.4 17.2 %collective-permute-start.23 = (bf16[4,96,1792]{2,1,0:T(8,128)(2,1)}, bf16[4,96,1792]{2,1,0:T(8,128)(2,1)}, u32[]{:S(2)}, u32[]{:S(2)}) collective-permute-start(bf16[4,96,1792]{2,1,0:T(8,128)(2,1)} %collective-permute-done.18.refs_7_), channel_id=1, source_target_pairs={{0,4},{1,5},{2,6},{3,7},{4,0},{5,1},{6,2},{7,3},{8,12},{9,13},{10,... | collective-permute-start | bytes 4128776 | tf_op jit(solution)/shard_map/ppermute | solution.py:40
  147.4 17.2 %all-to-all-start.1 = ((bf16[4,192,512]{2,1,0:T(8,128)(2,1)}), bf16[4,192,512]{2,1,0:T(8,128)(2,1)}, u32[]{:S(2)}, u32[]{:S(2)}) async-start(bf16[4,192,512]{2,1,0:T(8,128)(2,1)} %get-tuple-element.83), calls=%async_computation.1 | async-start | bytes 1572864 | tf_op jit(solution)/shard_map/all_to_all | solution.py:69
  193.9 17.1 %all-to-all-start.2 = ((bf16[4,192,512]{2,1,0:T(8,128)(2,1)}), bf16[4,192,512]{2,1,0:T(8,128)(2,1)S(1)}, u32[]{:S(2)}, u32[]{:S(2)}) async-start(bf16[4,192,512]{2,1,0:T(8,128)(2,1)} %get-tuple-element.88), calls=%async_computation.2 | async-start | bytes 1572864 | tf_op jit(solution)/shard_map/all_to_all | solution.py:69
  197.5 99.3 %reduce-scatter.3.cloned.1.call-start = ((), (), s32[]{:S(2)}) async-start(), calls=%async_computation.8 | async-start | bytes 12386304 | tf_op jit(solution)/shard_map/reduce_scatter | solution.py:839
  212.5 19.6 %collective-permute-start.26 = (bf16[512,768]{1,0:T(8,128)(2,1)S(1)}, bf16[512,768]{1,0:T(8,128)(2,1)}, u32[]{:S(2)}, u32[]{:S(2)}) collective-permute-start(bf16[512,768]{1,0:T(8,128)(2,1)S(1)} %copy-done.29), channel_id=1, source_target_pairs={{2,4},{3,5},{4,2},{5,3},{10,12},{11,13},{12,10},{13,11},{18,20},{1... | collective-permute-start | bytes 2359304 | tf_op jit(solution)/shard_map/ppermute | solution.py:40
  227.8 18.5 %all-to-all-start.3 = ((bf16[4,192,512]{2,1,0:T(8,128)(2,1)}), bf16[4,192,512]{2,1,0:T(8,128)(2,1)S(1)}, u32[]{:S(2)}, u32[]{:S(2)}) async-start(bf16[4,192,512]{2,1,0:T(8,128)(2,1)} %attend_back.3), calls=%async_computation.3 | async-start | bytes 1572864 | tf_op jit(solution)/shard_map/all_to_all | solution.py:69
  246.3 19.6 %all-to-all-start.5 = ((bf16[4,192,512]{2,1,0:T(8,128)(2,1)}), bf16[4,192,512]{2,1,0:T(8,128)(2,1)S(1)}, u32[]{:S(2)}, u32[]{:S(2)}) async-start(bf16[4,192,512]{2,1,0:T(8,128)(2,1)} %attend_back.5), calls=%async_computation.5 | async-start | bytes 1572864 | tf_op jit(solution)/shard_map/all_to_all | solution.py:69
  252.4 86.0 %reduce-scatter.5.cloned.1.call-start = ((), (), s32[]{:S(2)}) async-start(), calls=%async_computation.9 | async-start | bytes 1720320 | tf_op jit(solution)/shard_map/reduce_scatter | solution.py:870
  298.9 19.3 %collective-permute-start.32 = (bf16[2,96,576]{2,1,0:T(8,128)(2,1)}, bf16[2,96,576]{2,1,0:T(8,128)(2,1)}, u32[]{:S(2)}, u32[]{:S(2)}) collective-permute-start(bf16[2,96,576]{2,1,0:T(8,128)(2,1)} %get-tuple-element.160), channel_id=1, source_target_pairs={{0,16},{1,17},{2,18},{3,19},{4,20},{5,21},{6,22},{7,23},{8,24},{9,... | collective-permute-start | bytes 663560 | tf_op jit(solution)/shard_map/ppermute | solution.py:40
  316.0 21.4 %collective-permute-start.28 = (bf16[512,768]{1,0:T(8,128)(2,1)}, bf16[512,768]{1,0:T(8,128)(2,1)S(1)}, u32[]{:S(2)}, u32[]{:S(2)}) collective-permute-start(bf16[512,768]{1,0:T(8,128)(2,1)} %copy-done.11), channel_id=1, source_target_pairs={{2,4},{3,5},{4,2},{5,3},{10,12},{11,13},{12,10},{13,11},{18,20},{1... | collective-permute-start | bytes 2359304 | tf_op jit(solution)/shard_map/ppermute | solution.py:40
  322.4 13.5 %collective-permute-start.35 = (bf16[4,96,576]{2,1,0:T(8,128)(2,1)S(1)}, bf16[4,96,576]{2,1,0:T(8,128)(2,1)S(1)}, u32[]{:S(2)}, u32[]{:S(2)}) collective-permute-start(bf16[4,96,576]{2,1,0:T(8,128)(2,1)S(1)} %pad_maximum_fusion.3), channel_id=1, source_target_pairs={{0,16},{1,17},{2,18},{3,19},{4,20},{5,21},{6,22},{7,23},{8,24},{9,... | collective-permute-start | bytes 1327112 | tf_op jit(solution)/shard_map/ppermute | solution.py:40
  340.4 18.8 %collective-permute-start.38 = (bf16[96,576]{1,0:T(8,128)(2,1)S(1)}, bf16[96,576]{1,0:T(8,128)(2,1)S(1)}, u32[]{:S(2)}, u32[]{:S(2)}) collective-permute-start(bf16[96,576]{1,0:T(8,128)(2,1)S(1)} %get-tuple-element.157), channel_id=1, source_target_pairs={{0,1},{1,0},{2,3},{3,2},{4,5},{5,4},{6,7},{7,6},{8,9},{9,8},{10,11... | collective-permute-start | bytes 331784 | tf_op jit(solution)/shard_map/ppermute | solution.py:40
  340.7 18.6 %collective-permute-start.39 = (bf16[96,576]{1,0:T(8,128)(2,1)S(1)}, bf16[96,576]{1,0:T(8,128)(2,1)S(1)}, u32[]{:S(2)}, u32[]{:S(2)}) collective-permute-start(bf16[96,576]{1,0:T(8,128)(2,1)S(1)} %get-tuple-element.158), channel_id=1, source_target_pairs={{0,2},{1,3},{2,0},{3,1},{4,6},{5,7},{6,4},{7,5},{8,10},{9,11},{10,... | collective-permute-start | bytes 331784 | tf_op jit(solution)/shard_map/ppermute | solution.py:40
  (55 other events, 430.9 us)
Sparse Core Ops, SparseCore 0:
  23.0 43.5 all-gather.2
  211.2 82.0 reduce-scatter.2
  297.0 33.5 reduce-scatter.4
